TPU v7x, 32 devices: a whole 2x2x4 slice. The times are simulated.
32 devices in a mesh: dp: 4 (over y, core), mp: 8 (over z, x).
Axes of the slice: x: 2, y: 2, z: 4, core: 2. Of those that a mesh axis runs over, the one named last changes fastest.
Arguments:
- features: bfloat16 [1024, 4, 576], P('mp', 'dp'), may hold values from -6 to 6
- position: bfloat16 [1024, 576], P('mp'), may hold values from -3 to 3
- image_sizes: int32 [4], P('dp'), may hold values from 16 to 24, as said below
- gain_early: float32 [1024], P('mp'), may hold values from 0.5 to 1.5
- bias_early: float32 [1024], P('mp'), may hold values from -2 to 2
- conv_early: bfloat16 [1024, 9, 1024], P(None, None, 'mp'), may hold values from -0.0625 to 0.0625
- conv_bias_early: float32 [1024], P('mp'), may hold values from -4 to 4
- squeeze_down_early: float32 [1024, 256], P('mp'), may hold values from -0.1875 to 0.1875
- squeeze_down_bias_early: float32 [256], replicated, may hold values from -3 to 3
- squeeze_up_early: float32 [256, 1024], P(None, 'mp'), may hold values from -0.375 to 0.375
- squeeze_up_bias_early: float32 [1024], P('mp'), may hold values from -3 to 3
- gain_late: float32 [1024], P('mp'), may hold values from 0.5 to 1.5
- bias_late: float32 [1024], P('mp'), may hold values from -2 to 2
- conv_late: bfloat16 [1024, 9, 1024], P(None, None, 'mp'), may hold values from -0.0625 to 0.0625
- conv_bias_late: float32 [1024], P('mp'), may hold values from -4 to 4
- squeeze_down_late: float32 [1024, 256], P('mp'), may hold values from -0.1875 to 0.1875
- squeeze_down_bias_late: float32 [256], replicated, may hold values from -3 to 3
- squeeze_up_late: float32 [256, 1024], P(None, 'mp'), may hold values from -0.375 to 0.375
- squeeze_up_bias_late: float32 [1024], P('mp'), may hold values from -3 to 3
- readout_in: bfloat16 [1024, 4096], P(None, 'mp'), may hold values from -0.1875 to 0.1875
- readout_in_bias: float32 [4096], P('mp'), may hold values from -3 to 3
- readout_out: bfloat16 [4096, 4096], P(None, 'mp'), may hold values from -0.09375 to 0.09375
- readout_out_bias: float32 [4096], P('mp'), may hold values from -3 to 3
- out_grad: bfloat16 [576, 4096], P('dp', 'mp'), may hold values from -6 to 6
Outputs:
- tokens_out: bfloat16 [576, 4096], P('dp', 'mp')
- features_grad: float32 [1024, 4, 576], P('mp', 'dp')
- position_grad: float32 [1024, 576], P('mp')
- grad_gain_early: float32 [1024], P('mp')
- grad_bias_early: float32 [1024], P('mp')
- grad_conv_early: float32 [1024, 9, 1024], P(None, None, 'mp')
- grad_conv_bias_early: float32 [1024], P('mp')
- grad_down_early: float32 [1024, 256], P('mp')
- grad_down_bias_early: float32 [256], replicated
- grad_up_early: float32 [256, 1024], P(None, 'mp')
- grad_up_bias_early: float32 [1024], P('mp')
- grad_gain_late: float32 [1024], P('mp')
- grad_bias_late: float32 [1024], P('mp')
- grad_conv_late: float32 [1024, 9, 1024], P(None, None, 'mp')
- grad_conv_bias_late: float32 [1024], P('mp')
- grad_down_late: float32 [1024, 256], P('mp')
- grad_down_bias_late: float32 [256], replicated
- grad_up_late: float32 [256, 1024], P(None, 'mp')
- grad_up_bias_late: float32 [1024], P('mp')
- grad_readout_in: float32 [1024, 4096], P(None, 'mp')
- grad_readout_in_bias: float32 [4096], P('mp')
- grad_readout_out: float32 [4096, 4096], P(None, 'mp')
- grad_readout_out_bias: float32 [4096], P('mp')
Inputs may be any that keep to these rules, and one draw needn't show every extreme that they name: `image_sizes`: each entry is 16 or 24, and both occur.
All inputs are finite; a program needn't handle non-finite values.
Results may differ from a plain program's by a relative error of at most 0.0064.
Values may be sent and summed in bfloat16 or wider, within the bound.
No kernel may reach another device: no remote copies, remote signals or barrier semaphores. Data moves between devices by JAX's collectives and lax.ppermute only.
A program may use at most 128 MiB of HBM per device.

v0:
```python
from functools import partial

import jax
import jax.numpy as jnp
from jax import lax
from jax.sharding import PartitionSpec as P

SIDE = 24
SMALL = 16
GRID = 12


epsilon = 1e-06
highest_precision = lax.Precision.HIGHEST


def shifted(values, down_by, right_by):
    side_len = values.shape[-1]
    padding_extents = [(0, 0)] * (values.ndim - 2) + [(1, 1), (1, 1)]
    padded = jnp.pad(values, padding_extents)
    return padded[..., 1 + down_by : 1 + down_by + side_len, 1 + right_by : 1 + right_by + side_len]


def pool_matrix(extent, side_len, grid_len):
    row_index = jnp.arange(grid_len)[:, None]
    col_index = jnp.arange(side_len)[None, :]
    first_col = row_index * extent // grid_len
    end_col = -(-(row_index + 1) * extent // grid_len)
    in_bin = (col_index >= first_col) & (col_index < end_col)
    return jnp.where(in_bin, 1.0, 0.0).astype(jnp.float32) / (end_col - first_col).astype(
        jnp.float32
    )


def contract_in(local_rows, fold, initial):
    return (
        fold(initial, lax.all_gather(local_rows, "mp", axis=0, tiled=True), jnp.int32(0)),
        local_rows,
    )


def weight_rows(kept, rows_fn):
    return rows_fn(lax.all_gather(kept, "mp", axis=0, tiled=True), jnp.int32(0))


def conv_fold(running, block_rows, first_row, kernel):
    for tap_index in range(9):
        partial_out = lax.dot_general(
            kernel[:, tap_index, :],
            block_rows,
            (((0,), (0,)), ((), ())),
            preferred_element_type=jnp.float32,
        )
        running = running + shifted(partial_out, tap_index // 3 - 1, tap_index % 3 - 1)
    return running


def kernel_rows(block_rows, first_row, grad_conv):
    tap_grads = []
    for tap_index in range(9):
        moved_rows = shifted(block_rows, tap_index // 3 - 1, tap_index % 3 - 1)
        tap_grads.append(
            lax.dot_general(
                moved_rows,
                grad_conv,
                (((1, 2, 3), (1, 2, 3)), ((), ())),
                preferred_element_type=jnp.float32,
            )
        )
    return jnp.stack(tap_grads, axis=1)


def conv_back_term(row_count, kernel, grad_conv):
    running = jnp.zeros((row_count,) + grad_conv.shape[1:], jnp.float32)
    for tap_index in range(9):
        partial_in = lax.dot_general(
            kernel[:, tap_index, :],
            grad_conv,
            (((1,), (0,)), ((), ())),
            preferred_element_type=jnp.float32,
        )
        running = running + shifted(partial_in, 1 - tap_index // 3, 1 - tap_index % 3)
    return running


def readout_fold(running, block_rows, first_row, weight):
    return lax.dot_general(
        weight, block_rows, (((0,), (0,)), ((), ())), preferred_element_type=jnp.float32
    )


def output_fold(running, block_rows, first_row, weight):
    return lax.dot_general(
        block_rows, weight, (((0,), (0,)), ((), ())), preferred_element_type=jnp.float32
    )


def product_rows(block_rows, first_row, other):
    return jnp.dot(block_rows, other, preferred_element_type=jnp.float32)


def transpose_rows(block_rows, first_row, other):
    return lax.dot_general(
        block_rows, other, (((1,), (1,)), ((), ())), preferred_element_type=jnp.float32
    )


def hidden_term(weight, grad_rows):
    return lax.dot_general(
        weight, grad_rows, (((1,), (1,)), ((), ())), preferred_element_type=jnp.float32
    )


def token_term(weight, grad_rows):
    return jnp.dot(weight, grad_rows, preferred_element_type=jnp.float32)


def block_forward(inputs, valid_mask, counts, weights):
    norm_gain, norm_bias, kernel, conv_bias, se_down, se_down_bias, se_up, se_up_bias = weights
    channels = inputs.shape[0] * lax.axis_size("mp")
    moments = lax.psum((jnp.sum(inputs, axis=0), jnp.sum(inputs * inputs, axis=0)), "mp")
    center = moments[0] / channels
    inv_scale = lax.rsqrt(moments[1] / channels - center * center + epsilon)
    normed = (inputs - center) * inv_scale
    pre_act = normed * norm_gain[:, None, None, None] + norm_bias[:, None, None, None]
    hidden = (jax.nn.silu(pre_act) * valid_mask).astype(jnp.bfloat16)
    zeros_out = jnp.zeros((kernel.shape[2],) + inputs.shape[1:], jnp.float32)
    conv_sum, kept = contract_in(hidden, partial(conv_fold, kernel=kernel), zeros_out)
    conv_out = (conv_sum + conv_bias[:, None, None, None]) * valid_mask
    squeezed = jnp.sum(conv_out, axis=(2, 3)) / counts[None, :]
    reduced_pre = (
        lax.psum(jnp.dot(squeezed.T, se_down, precision=highest_precision), "mp")
        + se_down_bias[None, :]
    )
    reduced = jax.nn.silu(reduced_pre)
    excite = jax.nn.sigmoid(
        jnp.dot(reduced, se_up, precision=highest_precision) + se_up_bias[None, :]
    )
    output = inputs + conv_out * excite.T[:, :, None, None]
    stored = (normed, inv_scale, pre_act, kept, conv_out, squeezed, reduced_pre, reduced, excite)
    return (output, stored)


def block_backward(grad_out, valid_mask, counts, weights, stored):
    norm_gain, norm_bias, kernel, conv_bias, se_down, se_down_bias, se_up, se_up_bias = weights
    normed, inv_scale, pre_act, kept, conv_out, squeezed, reduced_pre, reduced, excite = stored
    channels = grad_out.shape[0] * lax.axis_size("mp")
    grad_excite = jnp.sum(grad_out * conv_out, axis=(2, 3)).T
    grad_logit = grad_excite * excite * (1.0 - excite)
    grad_up_bias = jnp.sum(grad_logit, axis=0)
    grad_up = jnp.dot(reduced.T, grad_logit, precision=highest_precision)
    grad_reduced = lax.psum(jnp.dot(grad_logit, se_up.T, precision=highest_precision), "mp")
    grad_reduced_pre = jax.vjp(jax.nn.silu, reduced_pre)[1](grad_reduced)[0]
    grad_down_bias = jnp.sum(grad_reduced_pre, axis=0)
    grad_down = jnp.dot(squeezed, grad_reduced_pre, precision=highest_precision)
    grad_squeezed = jnp.dot(se_down, grad_reduced_pre.T, precision=highest_precision)
    grad_conv = (
        (
            grad_out * excite.T[:, :, None, None]
            + (grad_squeezed / counts[None, :])[:, :, None, None]
        )
        * valid_mask
    ).astype(jnp.bfloat16)
    grad_conv_bias = jnp.sum(grad_conv.astype(jnp.float32), axis=(1, 2, 3))
    grad_kernel = weight_rows(kept, partial(kernel_rows, grad_conv=grad_conv))
    row_count = grad_out.shape[0]
    grad_hidden = lax.psum_scatter(
        conv_back_term(row_count * lax.axis_size("mp"), kernel=kernel, grad_conv=grad_conv),
        "mp",
        scatter_dimension=0,
        tiled=True,
    )
    grad_pre = jax.vjp(jax.nn.silu, pre_act)[1](grad_hidden * valid_mask)[0]
    grad_gain = jnp.sum(grad_pre * normed, axis=(1, 2, 3))
    grad_bias = jnp.sum(grad_pre, axis=(1, 2, 3))
    grad_normed = grad_pre * norm_gain[:, None, None, None]
    grad_moments = lax.psum(
        (jnp.sum(grad_normed, axis=0), jnp.sum(grad_normed * normed, axis=0)), "mp"
    )
    grad_inputs = grad_out + inv_scale * (
        grad_normed - grad_moments[0] / channels - normed * (grad_moments[1] / channels)
    )
    return (
        grad_inputs,
        (
            grad_gain,
            grad_bias,
            grad_kernel,
            grad_conv_bias,
            grad_down,
            grad_down_bias,
            grad_up,
            grad_up_bias,
        ),
    )


def per_device(
    features,
    position,
    image_sizes,
    gain_early,
    bias_early,
    conv_early,
    conv_bias_early,
    squeeze_down_early,
    squeeze_down_bias_early,
    squeeze_up_early,
    squeeze_up_bias_early,
    gain_late,
    bias_late,
    conv_late,
    conv_bias_late,
    squeeze_down_late,
    squeeze_down_bias_late,
    squeeze_up_late,
    squeeze_up_bias_late,
    readout_in,
    readout_in_bias,
    readout_out,
    readout_out_bias,
    out_grad,
):
    local_images = image_sizes.shape[0]
    channels_here = features.shape[0]
    extent = jnp.arange(SIDE)
    in_rows = extent[None, :] < image_sizes[:, None]
    valid_mask = jnp.where(in_rows[:, :, None] & in_rows[:, None, :], 1.0, 0.0).astype(jnp.float32)
    counts = (image_sizes * image_sizes).astype(jnp.float32)
    grid_in = features.astype(jnp.float32).reshape(channels_here, local_images, SIDE, SIDE)
    pos_grid = position.astype(jnp.float32).reshape(channels_here, 1, SIDE, SIDE)
    start_grid = (grid_in + pos_grid) * valid_mask
    early = (
        gain_early,
        bias_early,
        conv_early,
        conv_bias_early,
        squeeze_down_early,
        squeeze_down_bias_early,
        squeeze_up_early,
        squeeze_up_bias_early,
    )
    late = (
        gain_late,
        bias_late,
        conv_late,
        conv_bias_late,
        squeeze_down_late,
        squeeze_down_bias_late,
        squeeze_up_late,
        squeeze_up_bias_late,
    )
    early_block_output, stored_early = block_forward(start_grid, valid_mask, counts, early)
    lookup_tables = jnp.where(
        (image_sizes == SIDE)[:, None, None],
        pool_matrix(SIDE, SIDE, GRID)[None],
        pool_matrix(SMALL, SIDE, GRID)[None],
    )
    pooled_tokens = jnp.einsum(
        "qjx,kqxf->kqjf", lookup_tables, early_block_output, precision=highest_precision
    )
    pooled_tokens = jnp.einsum(
        "ibc,diac->diab", lookup_tables, pooled_tokens, precision=highest_precision
    )
    full_mask = jnp.ones((local_images, GRID, GRID), jnp.float32)
    grid_counts = jnp.full((local_images,), GRID * GRID, jnp.float32)
    after_late, stored_late = block_forward(pooled_tokens, full_mask, grid_counts, late)
    tokens = after_late.reshape(channels_here, -1).astype(jnp.bfloat16)
    token_rows = tokens.shape[1]
    hidden_here = readout_in.shape[1]
    pre_gelu, kept_tokens = contract_in(
        tokens,
        partial(readout_fold, weight=readout_in),
        jnp.zeros((hidden_here, token_rows), jnp.float32),
    )
    pre_gelu = pre_gelu + readout_in_bias[:, None]
    hidden_act = jax.nn.gelu(pre_gelu, approximate=False).astype(jnp.bfloat16)
    out_sum, kept_hidden = contract_in(
        hidden_act,
        partial(output_fold, weight=readout_out),
        jnp.zeros((token_rows, readout_out.shape[1]), jnp.float32),
    )
    tokens_out = (out_sum + readout_out_bias[None, :]).astype(jnp.bfloat16)
    grad_out_bias = jnp.sum(out_grad.astype(jnp.float32), axis=0)
    grad_out_weight = weight_rows(kept_hidden, partial(product_rows, other=out_grad))
    grad_hidden_act = lax.psum_scatter(
        hidden_term(weight=readout_out, grad_rows=out_grad), "mp", scatter_dimension=0, tiled=True
    )
    gelu_exact = partial(jax.nn.gelu, approximate=False)
    grad_pre_gelu = jax.vjp(gelu_exact, pre_gelu)[1](grad_hidden_act)[0].astype(jnp.bfloat16)
    grad_in_bias = jnp.sum(grad_pre_gelu.astype(jnp.float32), axis=1)
    grad_in_weight = weight_rows(kept_tokens, partial(transpose_rows, other=grad_pre_gelu))
    grad_tokens = lax.psum_scatter(
        token_term(weight=readout_in, grad_rows=grad_pre_gelu),
        "mp",
        scatter_dimension=0,
        tiled=True,
    )
    grad_after_late = grad_tokens.reshape(channels_here, local_images, GRID, GRID)
    pooled_tokens_gradient, late_grads = block_backward(
        grad_after_late, full_mask, grid_counts, late, stored_late
    )
    early_block_output_gradient = jnp.einsum(
        "hnj,chnv->chjv", lookup_tables, pooled_tokens_gradient, precision=highest_precision
    )
    early_block_output_gradient = jnp.einsum(
        "ibc,dirb->dirc", lookup_tables, early_block_output_gradient, precision=highest_precision
    )
    grad_start, early_grads = block_backward(
        early_block_output_gradient, valid_mask, counts, early, stored_early
    )
    feature_grid_grad = grad_start * valid_mask
    features_grad = feature_grid_grad.reshape(channels_here, local_images, SIDE * SIDE)
    position_part = jnp.sum(feature_grid_grad, axis=1).reshape(channels_here, SIDE * SIDE)
    summed = lax.psum(
        (
            position_part,
            early_grads[0],
            early_grads[1],
            early_grads[2],
            early_grads[3],
            early_grads[4],
            early_grads[5],
            early_grads[6],
            early_grads[7],
            late_grads[0],
            late_grads[1],
            late_grads[2],
            late_grads[3],
            late_grads[4],
            late_grads[5],
            late_grads[6],
            late_grads[7],
            grad_in_weight,
            grad_in_bias,
            grad_out_weight,
            grad_out_bias,
        ),
        "dp",
    )
    return (
        tokens_out,
        features_grad,
        summed[0],
        summed[1],
        summed[2],
        summed[3],
        summed[4],
        summed[5],
        summed[6],
        summed[7],
        summed[8],
        summed[9],
        summed[10],
        summed[11],
        summed[12],
        summed[13],
        summed[14],
        summed[15],
        summed[16],
        summed[17],
        summed[18],
        summed[19],
        summed[20],
    )


def solution(mesh):
    return jax.shard_map(
        per_device,
        mesh=mesh,
        in_specs=(
            P("mp", "dp", None),
            P("mp", None),
            P("dp"),
            P("mp"),
            P("mp"),
            P(None, None, "mp"),
            P("mp"),
            P("mp", None),
            P(),
            P(None, "mp"),
            P("mp"),
            P("mp"),
            P("mp"),
            P(None, None, "mp"),
            P("mp"),
            P("mp", None),
            P(),
            P(None, "mp"),
            P("mp"),
            P(None, "mp"),
            P("mp"),
            P(None, "mp"),
            P("mp"),
            P("dp", "mp"),
        ),
        out_specs=(
            P("dp", "mp"),
            P("mp", "dp", None),
            P("mp", None),
            P("mp"),
            P("mp"),
            P(None, None, "mp"),
            P("mp"),
            P("mp", None),
            P(),
            P(None, "mp"),
            P("mp"),
            P("mp"),
            P("mp"),
            P(None, None, "mp"),
            P("mp"),
            P("mp", None),
            P(),
            P(None, "mp"),
            P("mp"),
            P(None, "mp"),
            P("mp"),
            P(None, "mp"),
            P("mp"),
        ),
        check_vma=False,
    )
```

profile of v0, /device:TPU:0, one launch (start us, length us, event | category | flops | bytes accessed | tf_op | source)
XLA Modules:
  0.0 932.9 jit_solution(9525566716653618364)
XLA Ops:
  9.9 38.9 %all-reduce.37 = (f32[1,24,24]{2,1,0:T(8,128)S(1)}, f32[1,24,24]{2,1,0:T(8,128)S(1)}) all-reduce(f32[1,24,24]{2,1,0:T(8,128)S(1)} %reduce_sum.219, f32[1,24,24]{2,1,0:T(8,128)S(1)} %reduce_sum.217), channel_id=1, replica_groups=mesh['dp'=4,'mp'=8] {'mp'}, use_global_device_ids=true, to_apply=%region_3.4 | all-reduce | flops 1152 | bytes 9216 | tf_op jit(solution)/shard_map/psum | solution.py:121
  50.8 5.1 fusion.337
  56.1 32.4 %all-gather.4.cloned.1.call-done = bf16[1024,1,24,24]{0,3,2,1:T(8,128)(2,1)} async-done(((bf16[128,1,24,24]{0,3,2,1:T(8,128)(2,1)}), bf16[1024,1,24,24]{0,3,2,1:T(8,128)(2,1)}) %all-gather.4.cloned.1.call-update) | async-done | bytes 1179664 | tf_op jit(solution)/shard_map/all_gather | solution.py:37
  97.6 19.4 %psum.233 = f32[1,256]{1,0:T(1,128)S(1)} all-reduce(f32[1,256]{1,0:T(1,128)S(1)} %fusion.300), channel_id=1, replica_groups=mesh['dp'=4,'mp'=8] {'mp'}, use_global_device_ids=true, to_apply=%region_5.6 | all-reduce | flops 256 | bytes 2048 | tf_op jit(solution)/shard_map/psum | solution.py:132
  119.1 33.0 %all-reduce.36 = (f32[1,12,12]{2,1,0:T(8,128)S(1)}, f32[1,12,12]{2,1,0:T(8,128)S(1)}) all-reduce(f32[1,12,12]{2,1,0:T(8,128)S(1)} %bitcast.842, f32[1,12,12]{2,1,0:T(8,128)S(1)} %bitcast.841), channel_id=1, replica_groups=mesh['dp'=4,'mp'=8] {'mp'}, use_global_device_ids=true, to_apply=%region_9.10 | all-reduce | flops 288 | bytes 2304 | tf_op jit(solution)/shard_map/psum | solution.py:121
  152.4 28.4 %all-gather = bf16[1024,12,12]{0,2,1:T(8,128)(2,1)S(1)} all-gather(bf16[128,12,12]{0,2,1:T(8,128)(2,1)S(1)} %multiply_convert_fusion.2), channel_id=2, replica_groups=mesh['dp'=4,'mp'=8] {'mp'}, dimensions={0}, use_global_device_ids=true | all-gather | bytes 331776 | tf_op jit(solution)/shard_map/all_gather | solution.py:37
  186.7 17.3 %psum.236 = f32[1,256]{1,0:T(1,128)S(1)} all-reduce(f32[1,256]{1,0:T(1,128)S(1)} %fusion.298), channel_id=1, replica_groups=mesh['dp'=4,'mp'=8] {'mp'}, use_global_device_ids=true, to_apply=%region_11.12 | all-reduce | flops 256 | bytes 2048 | tf_op jit(solution)/shard_map/psum | solution.py:132
  205.4 27.6 %all_gather.18 = bf16[1024,144]{0,1:T(8,128)(2,1)} all-gather(bf16[128,144]{0,1:T(8,128)(2,1)S(1)} %convert_element_type.191), channel_id=1, replica_groups=mesh['dp'=4,'mp'=8] {'mp'}, dimensions={0}, use_global_device_ids=true | all-gather | bytes 331776 | tf_op jit(solution)/shard_map/all_gather | solution.py:37
  232.9 3.4 convert_reduce_fusion.1
  237.7 58.1 %reduce-scatter.7.cloned.1.call-done = f32[128,144]{0,1:T(8,128)} async-done(((f32[1024,144]{0,1:T(8,128)}), f32[128,144]{0,1:T(8,128)}) %reduce-scatter.7.cloned.1.call-update) | async-done | bytes 73744 | tf_op jit(solution)/shard_map/reduce_scatter | solution.py:293
  298.5 19.5 %psum.237 = f32[1,256]{1,0:T(1,128)S(1)} all-reduce(f32[1,256]{1,0:T(1,128)S(1)} %fusion.296), channel_id=1, replica_groups=mesh['dp'=4,'mp'=8] {'mp'}, use_global_device_ids=true, to_apply=%region_15.16 | all-reduce | flops 256 | bytes 2048 | tf_op jit(solution)/shard_map/psum | solution.py:152
  329.5 2.8 fusion.338
  337.8 51.2 %reduce-scatter.9.cloned.1.call-done = f32[128,1,12,12]{0,3,2,1:T(8,128)} async-done(((f32[1024,1,12,12]{0,3,2,1:T(8,128)}), f32[128,1,12,12]{0,3,2,1:T(8,128)}) %reduce-scatter.9.cloned.1.call-update) | async-done | bytes 73744 | tf_op jit(solution)/shard_map/reduce_scatter | solution.py:167
  390.2 35.6 %all-reduce.35 = (f32[1,12,12]{2,1,0:T(8,128)S(1)}, f32[1,12,12]{2,1,0:T(8,128)S(1)}) all-reduce(f32[1,12,12]{2,1,0:T(8,128)S(1)} %bitcast.833, f32[1,12,12]{2,1,0:T(8,128)S(1)} %bitcast.834), channel_id=1, replica_groups=mesh['dp'=4,'mp'=8] {'mp'}, use_global_device_ids=true, to_apply=%region_20.21 | all-reduce | flops 288 | bytes 2304 | tf_op jit(solution)/shard_map/psum | solution.py:177
  427.2 17.2 %psum.240 = f32[1,256]{1,0:T(1,128)S(1)} all-reduce(f32[1,256]{1,0:T(1,128)S(1)} %fusion.294), channel_id=1, replica_groups=mesh['dp'=4,'mp'=8] {'mp'}, use_global_device_ids=true, to_apply=%region_22.23 | all-reduce | flops 256 | bytes 2048 | tf_op jit(solution)/shard_map/psum | solution.py:152
  450.1 2.9 fusion.7
  459.8 6.0 fusion.339
  479.5 42.5 %reduce-scatter.11.cloned.1.call-done = f32[128,1,24,24]{0,3,2,1:T(8,128)} async-done(((f32[1024,1,24,24]{0,3,2,1:T(8,128)}), f32[128,1,24,24]{0,3,2,1:T(8,128)}) %reduce-scatter.11.cloned.1.call-update) | async-done | bytes 294928 | tf_op jit(solution)/shard_map/reduce_scatter | solution.py:167
  523.5 34.9 %all-reduce.34 = (f32[1,24,24]{2,1,0:T(8,128)S(1)}, f32[1,24,24]{2,1,0:T(8,128)S(1)}) all-reduce(f32[1,24,24]{2,1,0:T(8,128)S(1)} %bitcast.831, f32[1,24,24]{2,1,0:T(8,128)S(1)} %bitcast.832), channel_id=1, replica_groups=mesh['dp'=4,'mp'=8] {'mp'}, use_global_device_ids=true, to_apply=%region_27.28 | all-reduce | flops 1152 | bytes 9216 | tf_op jit(solution)/shard_map/psum | solution.py:177
  560.8 4.2 fusion.114
  565.1 12.3 %all-reduce.38 = (f32[128]{0:T(128)}, f32[128]{0:T(128)}, f32[128]{0:T(128)}, f32[256]{0:T(256)}, f32[128]{0:T(128)}, /*index=5*/f32[128]{0:T(128)}, f32[128]{0:...) all-reduce(f32[128]{0:T(128)S(1)} %get-tuple-element.23, ...), channel_id=1, replica_groups=mesh['dp'=4,'mp'=8] {'dp'}, use_global_device_ids=true, to_apply=%region_30.31 | all-reduce | flops 2560 | bytes 20480 | tf_op jit(solution)/shard_map/psum | solution.py:315
  577.4 332.0 %all-reduce.42.cloned.1.call-done = (f32[128,576]{0,1:T(8,128)}, f32[1024,9,128]{2,0,1:T(8,128)}, f32[128,256]{1,0:T(8,128)}, f32[256,128]{1,0:T(8,128)}, f32[10...) async-done(((f32[128,576]{0,1:T(8,128)}, f32[1024,9,128]{2,0,1:T(8,128)}, f32[128,256]{1,0:T(8,128)}, ...) | async-done | bytes 20742160 | tf_op jit(solution)/shard_map/psum | solution.py:315
  911.1 5.2 copy.94
  922.7 3.4 copy.101
  (281 shorter events, 83.9 us)
Async XLA Ops:
  7.2 225.7 %copy-start = (bf16[1024,512]{1,0:T(8,128)(2,1)S(1)}, bf16[1024,512]{1,0:T(8,128)(2,1)}, u32[]{:S(2)}) copy-start(bf16[1024,512]{1,0:T(8,128)(2,1)} %param.43) | copy-start | bytes 3145732
  7.2 81.3 %all-gather.4.cloned.1.call-start = ((), (), s32[]{:S(2)}) async-start(), calls=%async_computation.4 | async-start | bytes 1327104 | tf_op jit(solution)/shard_map/all_gather | solution.py:37
  8.1 88.1 %copy-start.17 = (f32[24,24]{1,0:T(8,128)}, f32[24,24]{1,0:T(8,128)S(1)}, u32[]{:S(2)}) copy-start(f32[24,24]{1,0:T(8,128)S(1)} %and_select_fusion) | copy-start | bytes 6916
  50.8 182.2 %reduce-scatter.5.cloned.1.call-start = ((), (), s32[]{:S(2)}) async-start(), calls=%async_computation.6 | async-start | bytes 2654208 | tf_op jit(solution)/shard_map/reduce_scatter | solution.py:286
  56.0 239.9 %reduce-scatter.7.cloned.1.call-start = ((), (), s32[]{:S(2)}) async-start(), calls=%async_computation.7 | async-start | bytes 663552 | tf_op jit(solution)/shard_map/reduce_scatter | solution.py:293
  56.0 62.6 %copy-start.49 = (f32[12]{0:T(128)}, f32[12]{0:T(128)S(1)}, u32[]{:S(2)}) copy-start(f32[12]{0:T(128)S(1)} %get-tuple-element.95) | copy-start | bytes 148
  56.0 62.6 %copy-start.51 = (s32[12]{0:T(128)}, s32[12]{0:T(128)S(1)}, u32[]{:S(2)}) copy-start(s32[12]{0:T(128)S(1)} %get-tuple-element.96) | copy-start | bytes 148
  56.1 62.6 %copy-start.53 = (s32[12]{0:T(128)}, s32[12]{0:T(128)S(1)}, u32[]{:S(2)}) copy-start(s32[12]{0:T(128)S(1)} %get-tuple-element.93) | copy-start | bytes 148
  237.7 151.3 %reduce-scatter.9.cloned.1.call-start = ((), (), s32[]{:S(2)}) async-start(), calls=%async_computation.8 | async-start | bytes 884736 | tf_op jit(solution)/shard_map/reduce_scatter | solution.py:167
  327.6 132.2 %all-gather.6.cloned.1.call-start = ((), (), s32[]{:S(2)}) async-start(), calls=%async_computation.5 | async-start | bytes 1327104 | tf_op jit(solution)/shard_map/all_gather | solution.py:37
  332.3 189.8 %reduce-scatter.11.cloned.1.call-start = ((), (), s32[]{:S(2)}) async-start(), calls=%async_computation.9 | async-start | bytes 2654208 | tf_op jit(solution)/shard_map/reduce_scatter | solution.py:167
  335.8 90.2 %copy-start.50 = (f32[12]{0:T(128)S(1)}, f32[12]{0:T(128)}, u32[]{:S(2)}) copy-start(f32[12]{0:T(128)} %copy-done.49) | copy-start | bytes 148
  335.8 90.2 %copy-start.52 = (s32[12]{0:T(128)S(1)}, s32[12]{0:T(128)}, u32[]{:S(2)}) copy-start(s32[12]{0:T(128)} %copy-done.51) | copy-start | bytes 148
  335.8 90.2 %copy-start.54 = (s32[12]{0:T(128)S(1)}, s32[12]{0:T(128)}, u32[]{:S(2)}) copy-start(s32[12]{0:T(128)} %copy-done.53) | copy-start | bytes 148
  335.8 90.2 %copy-start.56 = (s32[12]{0:T(128)S(1)}, s32[12]{0:T(128)}, u32[]{:S(2)}) copy-start(s32[12]{0:T(128)} %copy-done.55) | copy-start | bytes 148
  335.8 90.2 %copy-start.58 = (f32[12]{0:T(128)S(1)}, f32[12]{0:T(128)}, u32[]{:S(2)}) copy-start(f32[12]{0:T(128)} %copy-done.57) | copy-start | bytes 148
  335.8 90.2 %copy-start.60 = (s32[12]{0:T(128)S(1)}, s32[12]{0:T(128)}, u32[]{:S(2)}) copy-start(s32[12]{0:T(128)} %copy-done.59) | copy-start | bytes 148
  335.8 91.2 %copy-start.40 = (f32[128]{0:T(128)S(1)}, f32[128]{0:T(128)}, u32[]{:S(2)}) copy-start(f32[128]{0:T(128)} %copy-done.39) | copy-start | bytes 1540
  335.8 91.2 %copy-start.14 = (f32[256,128]{1,0:T(8,128)S(1)}, f32[256,128]{1,0:T(8,128)}, u32[]{:S(2)}) copy-start(f32[256,128]{1,0:T(8,128)} %param.33) | copy-start | bytes 393220
  335.8 108.5 %copy-start.41 = (f32[1,256]{1,0:T(1,128)S(1)}, f32[1,256]{1,0:T(1,128)}, u32[]{:S(2)}) copy-start(f32[1,256]{1,0:T(1,128)} %get-tuple-element.77) | copy-start | bytes 3076
  335.8 108.5 %copy-start.42 = (f32[1,256]{1,0:T(1,128)S(1)}, f32[1,256]{1,0:T(1,128)}, u32[]{:S(2)}) copy-start(f32[1,256]{1,0:T(1,128)} %get-tuple-element.78) | copy-start | bytes 3076
  335.9 108.5 %copy-start.16 = (f32[128,256]{1,0:T(8,128)S(1)}, f32[128,256]{1,0:T(8,128)}, u32[]{:S(2)}) copy-start(f32[128,256]{1,0:T(8,128)} %param.31) | copy-start | bytes 393220
  335.9 108.7 %copy-start.18 = (f32[24,24]{1,0:T(8,128)S(1)}, f32[24,24]{1,0:T(8,128)}, u32[]{:S(2)}) copy-start(f32[24,24]{1,0:T(8,128)} %copy-done.17) | copy-start | bytes 6916
  453.1 456.3 %all-reduce.42.cloned.1.call-start = ((), (), s32[]{:S(2)}) async-start(), calls=%async_computation.10 | async-start | bytes 41484288 | tf_op jit(solution)/shard_map/psum | solution.py:315
  (55 other events, 1060.2 us)
Sparse Core Ops, SparseCore 0:
  50.9 37.6 all-gather.3
  92.6 69.6 reduce-scatter.4
  237.8 58.0 reduce-scatter.6
  327.8 61.1 reduce-scatter.8
  391.4 39.4 all-gather.5
  453.2 68.7 reduce-scatter.10
  559.7 349.6 all-reduce.41
where the time goes:
time: 934 us; the launch traced here: 933 us
  waiting for transfers between devices  516 us (55%)
  blocking collectives  284 us (30%)
  matrix products  78.5 us (8%)
  local copies, waits for them, and re-layouts  21.6 us (2%)
  other arithmetic  16.2 us (2%)
  between operations  15.9 us (2%)
    psum x1, waiting for transfers between devices, per_device(): lax.psum((position_part, early_grads[0], early_grads[1], early_grads[2],...  332 us
    reduce_scatter x2, waiting for transfers between devices, block_backward(): lax.psum_scatter(conv_back_term(row_count * lax.axis_size('mp'), kernel=k...  93.7 us
    psum x2, blocking collectives, block_forward(): lax.psum((jnp.sum(inputs, axis=0), jnp.sum(inputs * inputs, axis=0)), 'mp')  71.9 us
    psum x2, blocking collectives, block_backward(): lax.psum((jnp.sum(grad_normed, axis=0), jnp.sum(grad_normed * normed, axi...  70.5 us
    reduce_scatter x1, waiting for transfers between devices, per_device(): lax.psum_scatter(token_term(weight=readout_in, grad_rows=grad_pre_gelu),...  58.1 us
    all_gather x2, blocking collectives, contract_in(): lax.all_gather(local_rows, 'mp', axis=0, tiled=True)  55.9 us
    psum x2, blocking collectives, block_forward(): lax.psum(jnp.dot(squeezed.T, se_down, precision=highest_precision), 'mp')  36.7 us
    psum x2, blocking collectives, block_backward(): lax.psum(jnp.dot(grad_logit, se_up.T, precision=highest_precision), 'mp')  36.7 us
  transfers between devices with their start and end apart: 7, of which 5 were waited for; matrix products, arithmetic and copies ran while one was open for 8% of the time, Pallas kernels for 0%

commit v1 on v0

v1 whole, which is shorter than its diff:
```python
from functools import partial

import jax
import jax.numpy as jnp
from jax import lax
from jax.experimental import pallas as pl
from jax.experimental.pallas import tpu as pltpu
from jax.sharding import PartitionSpec as P

SIDE = 24
SMALL = 16
GRID = 12
EPS = 1e-06
F32 = jnp.float32
BF16 = jnp.bfloat16
HI = lax.Precision.HIGHEST


def pool_matrix(extent, side_len, grid_len):
    row_index = jnp.arange(grid_len)[:, None]
    col_index = jnp.arange(side_len)[None, :]
    first_col = row_index * extent // grid_len
    end_col = -(-(row_index + 1) * extent // grid_len)
    in_bin = (col_index >= first_col) & (col_index < end_col)
    return jnp.where(in_bin, 1.0, 0.0).astype(F32) / (end_col - first_col).astype(F32)


def shape(dims, dtype=F32):
    return jax.ShapeDtypeStruct(dims, dtype)


def cost(flops, nbytes):
    return pl.CostEstimate(flops=int(flops), bytes_accessed=int(nbytes), transcendentals=0)


def call(kernel, outs, *args, flops=1e6, smem=(), name=None):
    specs = [
        pl.BlockSpec(memory_space=pltpu.SMEM if k in smem else pltpu.VMEM)
        for k in range(len(args))
    ]
    nbytes = sum(a.size * a.dtype.itemsize for a in args) + sum(
        o.size * jnp.dtype(o.dtype).itemsize for o in outs
    )
    return pl.pallas_call(
        kernel,
        out_shape=list(outs),
        in_specs=specs,
        out_specs=[pl.BlockSpec(memory_space=pltpu.VMEM) for _ in outs],
        cost_estimate=cost(flops, nbytes),
        name=name,
    )(*args)


def mm(a, b, ca, cb, precision=None):
    return lax.dot_general(
        a, b, (((ca,), (cb,)), ((), ())), preferred_element_type=F32, precision=precision
    )


def sigmoid(v):
    return 1.0 / (1.0 + jnp.exp(-v))


def silu_grad(v):
    s = sigmoid(v)
    return s * (1.0 + v * (1.0 - s))


def grid_rc(side, lanes):
    i = lax.broadcasted_iota(jnp.int32, (side * side, lanes), 0).astype(F32)
    r = jnp.floor((i + 0.5) * (1.0 / side))
    return r, i - r * side


def tap_ok(r, c, side, dy, dx):
    ok = None
    for v, d in ((r, dy), (c, dx)):
        if d == 0:
            continue
        one = (v >= 0.5) if d < 0 else (v <= side - 1.5)
        ok = one if ok is None else ok & one
    return ok


def tap_sum(y, side, width):
    n = side * side
    r, c = grid_rc(side, width)
    total = None
    for t in range(9):
        dy, dx = t // 3 - 1, t % 3 - 1
        part = y[:, t * width : (t + 1) * width]
        off = dy * side + dx
        if off:
            part = pltpu.roll(part, (-off) % n, 0)
        ok = tap_ok(r, c, side, dy, dx)
        if ok is not None:
            part = jnp.where(ok, part, 0.0)
        total = part if total is None else total + part
    return total


def tap_spread(g, side, width):
    n = side * side
    r, c = grid_rc(side, width)
    parts = []
    for t in range(9):
        dy, dx = t // 3 - 1, t % 3 - 1
        off = dy * side + dx
        part = pltpu.roll(g, off % n, 0) if off else g
        ok = tap_ok(r, c, side, -dy, -dx)
        if ok is not None:
            part = jnp.where(ok, part, 0.0)
        parts.append(part.astype(BF16))
    return jnp.concatenate(parts, axis=1)


def wide(ref):
    return jnp.concatenate([ref[j] for j in range(ref.shape[0])], axis=1)


def split_mm(p, v, ca, cb):
    top = v.astype(BF16)
    low = (v - top.astype(F32)).astype(BF16)
    return mm(p, top, ca, cb) + mm(p, low, ca, cb)


def size_mask(size, width):
    r, c = grid_rc(SIDE, width)
    s = size.astype(F32) - 0.5
    return jnp.where((r < s) & (c < s), 1.0, 0.0).astype(F32)


def put_all(ref, value):
    for j in range(ref.shape[0]):
        ref[j] = value


def rows_of(pair_ref, total):
    acc = pair_ref[0]
    for j in range(1, total):
        acc = acc + pair_ref[j]
    return acc


def row_sums(u, v):
    ones = jnp.ones((8, u.shape[1]), F32)
    su = mm(ones, u, 1, 1, HI)
    sv = mm(ones, v, 1, 1, HI)
    row = lax.broadcasted_iota(jnp.int32, su.shape, 0)
    return jnp.where(row < 4, su, sv)


def spread_rows(acc, which, width):
    row = lax.broadcasted_iota(jnp.int32, (8, width), 0)
    pick = jnp.where(row == which, 1.0, 0.0).astype(F32)
    return mm(acc, pick, 0, 0, HI)


def prep_kernel(size_ref, f_ref, p_ref, x_ref, s_ref):
    width = f_ref.shape[1]
    x = (f_ref[...].astype(F32) + p_ref[...].astype(F32)) * size_mask(size_ref[0], width)
    x_ref[...] = x
    put_all(s_ref, row_sums(x, x * x))


def hidden_kernel(channels, size_ref, x_ref, s_ref, gain_ref, bias_ref, out_ref, mom_ref):
    width = x_ref.shape[1]
    acc = rows_of(s_ref, s_ref.shape[0]) * (1.0 / channels)
    center = spread_rows(acc, 0, width)
    square = spread_rows(acc, 4, width)
    inv = lax.rsqrt(square - center * center + EPS)
    mom_ref[0] = center
    mom_ref[1] = inv
    pre = (x_ref[...] - center) * inv * gain_ref[...] + bias_ref[...]
    hid = (pre * sigmoid(pre) * size_mask(size_ref[0], width)).astype(BF16)
    put_all(out_ref, hid)


def conv_kernel(
    size_ref, h_ref, w_ref, cb_ref, x_ref, pp_ref, down_ref, conv_ref, a_ref, b_ref, sq_ref, rp_ref
):
    out = w_ref.shape[2]
    h = wide(h_ref)
    y = mm(h, wide(w_ref), 1, 0)
    size = size_ref[0].astype(F32)
    conv = (tap_sum(y, SIDE, out) + cb_ref[...]) * size_mask(size_ref[0], out)
    conv_ref[...] = conv
    a_ref[...] = split_mm(pp_ref[...], x_ref[...], 1, 0)
    b_ref[...] = split_mm(pp_ref[...], conv, 1, 0)
    sq = jnp.sum(conv, axis=0, keepdims=True) * (1.0 / (size * size + jnp.zeros((1, out), F32)))
    sq_ref[...] = sq
    put_all(rp_ref, mm(jnp.broadcast_to(sq, (8, out)), down_ref[...], 1, 0, HI))


def excite_of(rp_ref, db_ref, up_ref, ub_ref):
    rpre = rows_of(rp_ref, rp_ref.shape[0]) + db_ref[...]
    red = rpre * sigmoid(rpre)
    e = sigmoid(mm(red, up_ref[...], 1, 0, HI) + ub_ref[...])
    return rpre[0:1], e[0:1]


def pooled_kernel(rp_ref, db_ref, up_ref, ub_ref, a_ref, b_ref, out_ref, rpre_ref, e_ref):
    rpre, e = excite_of(rp_ref, db_ref, up_ref, ub_ref)
    rpre_ref[...] = rpre
    e_ref[...] = e
    put_all(out_ref, (a_ref[...] + b_ref[...] * e).astype(out_ref.dtype))


def late_norm(pool_ref, gain_ref, bias_ref):
    x = wide(pool_ref).astype(F32)
    channels = x.shape[1]
    center = jnp.sum(x, axis=1, keepdims=True) * (1.0 / channels)
    d = x - center
    inv = lax.rsqrt(jnp.sum(d * d, axis=1, keepdims=True) * (1.0 / channels) + EPS)
    normed = d * inv
    return normed, inv, normed * gain_ref[...] + bias_ref[...]


def late_kernel(
    pool_ref, gain_ref, bias_ref, w_ref, cb_ref, down_ref, h_ref, conv_ref, sq_ref, rp_ref
):
    out = w_ref.shape[2]
    _, _, pre = late_norm(pool_ref, gain_ref, bias_ref)
    h = (pre * sigmoid(pre)).astype(BF16)
    h_ref[...] = h
    y = mm(h, wide(w_ref), 1, 0)
    conv = tap_sum(y, GRID, out) + cb_ref[...]
    conv_ref[...] = conv
    sq = jnp.sum(conv, axis=0, keepdims=True) * (1.0 / (GRID * GRID))
    sq_ref[...] = sq
    put_all(rp_ref, mm(jnp.broadcast_to(sq, (8, out)), down_ref[...], 1, 0, HI))


def late_slope_kernel(pool_ref, gain_ref, bias_ref, n_ref, i_ref, d_ref):
    normed, inv, pre = late_norm(pool_ref, gain_ref, bias_ref)
    n_ref[...] = normed
    i_ref[...] = jnp.broadcast_to(inv, i_ref.shape)
    d_ref[...] = silu_grad(pre)


def token_kernel(rp_ref, db_ref, up_ref, ub_ref, pool_ref, conv_ref, out_ref, rpre_ref, e_ref):
    rpre, e = excite_of(rp_ref, db_ref, up_ref, ub_ref)
    rpre_ref[...] = rpre
    e_ref[...] = e
    put_all(out_ref, (pool_ref[...] + conv_ref[...] * e).astype(BF16))


def readout_kernel(t_ref, w_ref, b_ref, gh_ref, act_ref, gp_ref, gt_ref):
    pre = mm(wide(t_ref), w_ref[...], 1, 0) + b_ref[...]
    phi = 0.5 * (1.0 + lax.erf(pre * 0.7071067811865476))
    act_ref[...] = (pre * phi).astype(BF16)
    dens = 0.3989422804014327 * jnp.exp(-0.5 * pre * pre)
    gh = gh_ref[0].astype(F32)
    for j in range(1, gh_ref.shape[0]):
        gh = gh + gh_ref[j].astype(F32)
    gp = (gh * (phi + pre * dens)).astype(BF16)
    gp_ref[...] = gp
    gt = mm(gp, w_ref[...], 1, 1)
    step = gt_ref.shape[2]
    for j in range(gt_ref.shape[0]):
        gt_ref[j] = gt[:, j * step : (j + 1) * step].astype(BF16)


def act_grad_kernel(g_ref, w_ref, out_ref):
    out_ref[0] = mm(g_ref[...], w_ref[...], 1, 1).astype(BF16)


def logits_kernel(act_ref, w_ref, b_ref, out_ref, acc_ref):
    j = pl.program_id(0)
    part = mm(act_ref[0], w_ref[...], 1, 0)

    @pl.when(j == 0)
    def _():
        acc_ref[...] = part

    @pl.when(j > 0)
    def _():
        acc_ref[...] += part

    @pl.when(j == pl.num_programs(0) - 1)
    def _():
        out_ref[...] = (acc_ref[...] + b_ref[...]).astype(BF16)


def excite_back(g, conv, e_ref, up_ref, gl_ref):
    e = e_ref[...]
    gl = jnp.sum(g * conv, axis=0, keepdims=True) * e * (1.0 - e)
    gl_ref[...] = gl
    return mm(jnp.broadcast_to(gl, (8, gl.shape[1])), up_ref[...], 1, 1, HI)


def late_back_a(gt_ref, conv_ref, e_ref, up_ref, g_ref, gl_ref, gr_ref):
    g = gt_ref[0].astype(F32)
    for j in range(1, gt_ref.shape[0]):
        g = g + gt_ref[j].astype(F32)
    g_ref[...] = g
    put_all(gr_ref, excite_back(g, conv_ref[...], e_ref, up_ref, gl_ref))


def squeeze_back(gr, rpre_ref, down_ref, grp_ref):
    rp = rpre_ref[...]
    grp = gr * silu_grad(rp)
    grp_ref[...] = grp[0:1]
    return mm(grp, down_ref[...], 1, 1, HI)[0:1]


def late_back_b(
    gr_ref, rpre_ref, down_ref, e_ref, g_ref, w_ref, n_ref, i_ref, d_ref, gain_ref,
    gc_ref, grp_ref, part_ref, gg_ref,
):
    out = w_ref.shape[2]
    gs = squeeze_back(rows_of(gr_ref, gr_ref.shape[0]), rpre_ref, down_ref, grp_ref)
    gc = (g_ref[...] * e_ref[...] + gs * (1.0 / (GRID * GRID))).astype(BF16)
    gc_ref[...] = gc
    spread = tap_spread(gc.astype(F32), GRID, out)
    gh = mm(spread, wide(w_ref), 1, 1)
    normed = n_ref[...]
    gpre = gh * d_ref[...]
    channels = gpre.shape[1]
    gg_ref[0:1] = jnp.sum(gpre * normed, axis=0, keepdims=True)
    gg_ref[1:2] = jnp.sum(gpre, axis=0, keepdims=True)
    gn = gpre * gain_ref[...]
    m1 = jnp.sum(gn, axis=1, keepdims=True) * (1.0 / channels)
    m2 = jnp.sum(gn * normed, axis=1, keepdims=True) * (1.0 / channels)
    part = (gn - m1 - normed * m2) * i_ref[:, 0:1]
    step = part_ref.shape[2]
    for j in range(part_ref.shape[0]):
        part_ref[j] = part[:, j * step : (j + 1) * step].astype(BF16)


def early_back_a(part_ref, g_ref, b_ref, e_ref, up_ref, pp_ref, gae_ref, gl_ref, gr_ref):
    g = part_ref[0].astype(F32)
    for j in range(1, part_ref.shape[0]):
        g = g + part_ref[j].astype(F32)
    g = g + g_ref[...]
    put_all(gr_ref, excite_back(g, b_ref[...], e_ref, up_ref, gl_ref))
    gae_ref[...] = split_mm(pp_ref[...], g, 0, 0)


def early_back_b(
    size_ref, gr_ref, rpre_ref, down_ref, e_ref, gae_ref, w_ref, gc_ref, grp_ref, part_ref
):
    out = w_ref.shape[2]
    size = size_ref[0].astype(F32)
    gs = squeeze_back(rows_of(gr_ref, gr_ref.shape[0]), rpre_ref, down_ref, grp_ref)
    gs = gs * (1.0 / (size * size + jnp.zeros((1, out), F32)))
    gc = ((gae_ref[...] * e_ref[...] + gs) * size_mask(size_ref[0], out)).astype(BF16)
    gc_ref[...] = gc
    spread = tap_spread(gc.astype(F32), SIDE, out)
    gh = mm(spread, wide(w_ref), 1, 1)
    step = part_ref.shape[2]
    for j in range(part_ref.shape[0]):
        part_ref[j] = gh[:, j * step : (j + 1) * step].astype(BF16)


def early_back_c(
    size_ref, part_ref, x_ref, mom_ref, gain_ref, bias_ref, gn_ref, gg_ref, s_ref
):
    width = x_ref.shape[1]
    gh = part_ref[0].astype(F32)
    for j in range(1, part_ref.shape[0]):
        gh = gh + part_ref[j].astype(F32)
    normed = (x_ref[...] - mom_ref[0]) * mom_ref[1]
    pre = normed * gain_ref[...] + bias_ref[...]
    gpre = gh * size_mask(size_ref[0], width) * silu_grad(pre)
    gg_ref[0:1] = jnp.sum(gpre * normed, axis=0, keepdims=True)
    gg_ref[1:2] = jnp.sum(gpre, axis=0, keepdims=True)
    gn = gpre * gain_ref[...]
    gn_ref[...] = gn
    put_all(s_ref, row_sums(gn, gn * normed))


def early_back_d(channels, size_ref, s_ref, gn_ref, x_ref, mom_ref, gae_ref, fg_ref, low_ref):
    width = x_ref.shape[1]
    acc = rows_of(s_ref, s_ref.shape[0]) * (1.0 / channels)
    m1 = spread_rows(acc, 0, width)
    m2 = spread_rows(acc, 4, width)
    inv = mom_ref[1]
    normed = (x_ref[...] - mom_ref[0]) * inv
    out = (gae_ref[...] + inv * (gn_ref[...] - m1 - normed * m2)) * size_mask(size_ref[0], width)
    fg_ref[...] = out
    low_ref[...] = out.astype(BF16)


def conv_weight_kernel(side, images, slot_ref, h_ref, g_ref, out_ref, gb_ref, spread_ref):
    out = g_ref.shape[2]
    n = side * side

    @pl.when(pl.program_id(0) == 0)
    def _():
        total = None
        for s in range(images):
            g = g_ref[slot_ref[s]].astype(F32)
            one = jnp.sum(g, axis=0, keepdims=True)
            total = one if total is None else total + one
            spread_ref[s * n : (s + 1) * n, :] = tap_spread(g, side, out)
        gb_ref[...] = total

    if len(h_ref.shape) == 4:
        h = jnp.concatenate(
            [
                jnp.concatenate([h_ref[slot_ref[s], j] for j in range(h_ref.shape[1])], axis=1)
                for s in range(images)
            ],
            axis=0,
        )
    else:
        h = jnp.concatenate([h_ref[slot_ref[s]] for s in range(images)], axis=0)
    res = mm(h, spread_ref[...], 0, 0)
    for t in range(9):
        out_ref[t] = res[:, t * out : (t + 1) * out]


def conv_weights(side, slot, h, g, channels, steps):
    images, n, out = g.shape
    rows = channels // steps
    if h.ndim == 4:
        h_spec = pl.BlockSpec(
            (images, h.shape[1] // steps, n, h.shape[3]), lambda k, s: (0, k, 0, 0)
        )
    else:
        h_spec = pl.BlockSpec((images, n, rows), lambda k, s: (0, 0, k))
    return pl.pallas_call(
        partial(conv_weight_kernel, side, images),
        out_shape=[shape((9, channels, out)), shape((1, out))],
        grid_spec=pltpu.PrefetchScalarGridSpec(
            num_scalar_prefetch=1,
            grid=(steps,),
            in_specs=[h_spec, pl.BlockSpec((images, n, out), lambda k, s: (0, 0, 0))],
            out_specs=[
                pl.BlockSpec((9, rows, out), lambda k, s: (0, k, 0)),
                pl.BlockSpec((1, out), lambda k, s: (0, 0)),
            ],
            scratch_shapes=[pltpu.VMEM((images * n, 9 * out), BF16)],
        ),
        cost_estimate=cost(2 * images * n * 9 * out * channels, h.size * 2 + 36 * channels * out),
        name="conv_weights_%d" % side,
    )(slot, h, g)


def dense_weight_kernel(images, slot_ref, a_ref, g_ref, out_ref, gb_ref):
    a = jnp.concatenate([a_ref[slot_ref[s], 0] for s in range(images)], axis=0)
    g = jnp.concatenate([g_ref[slot_ref[s]] for s in range(images)], axis=0)
    out_ref[...] = mm(a, g, 0, 0)

    @pl.when(pl.program_id(0) == 0)
    def _():
        gb_ref[...] = jnp.sum(g.astype(F32), axis=0, keepdims=True)


def dense_weights(slot, a, g):
    images, blocks, rows, width = a.shape
    cols = g.shape[2]
    return pl.pallas_call(
        partial(dense_weight_kernel, images),
        out_shape=[shape((blocks * width, cols)), shape((1, cols))],
        grid_spec=pltpu.PrefetchScalarGridSpec(
            num_scalar_prefetch=1,
            grid=(blocks,),
            in_specs=[
                pl.BlockSpec((images, 1, rows, width), lambda k, s: (0, k, 0, 0)),
                pl.BlockSpec((images, rows, cols), lambda k, s: (0, 0, 0)),
            ],
            out_specs=[
                pl.BlockSpec((width, cols), lambda k, s: (k, 0)),
                pl.BlockSpec((1, cols), lambda k, s: (0, 0)),
            ],
        ),
        cost_estimate=cost(2 * images * rows * blocks * width * cols, a.size * 2 + blocks * width * cols * 4),
        name="dense_weights_%d" % width,
    )(slot, a, g)


def swap(v):
    return lax.all_to_all(v, "mp", 0, 0)


def dp_permute(v, fn):
    n = lax.axis_size("dp")
    return lax.ppermute(v, "dp", [(i, fn(i) % n) for i in range(n)])


def dp_gather(v, relay=True):
    n = lax.axis_size("dp")
    slots = [v, dp_permute(v, lambda i: i ^ 1)]
    for k in range(1, n // 2):
        far = dp_permute(v, lambda i: i + 2 * k)
        slots.append(far)
        if relay:
            slots.append(dp_permute(far, lambda i: i ^ 1))
        else:
            slots.append(dp_permute(v, lambda i: ((i + 2 * k) % n) ^ 1))
    return jnp.stack(slots)


def dp_slots():
    n = lax.axis_size("dp")
    me = lax.axis_index("dp")
    s = jnp.arange(n)
    hops = (me // 2 - s // 2) % (n // 2)
    return (2 * hops + ((s ^ me) & 1)).astype(jnp.int32)


def in_order(stacked, slot):
    return [lax.dynamic_index_in_dim(stacked, slot[s], 0, False) for s in range(stacked.shape[0])]


def row(v):
    return v.reshape(1, -1)


def per_device(
    features,
    position,
    image_sizes,
    gain_early,
    bias_early,
    conv_early,
    conv_bias_early,
    down_early,
    down_bias_early,
    up_early,
    up_bias_early,
    gain_late,
    bias_late,
    conv_late,
    conv_bias_late,
    down_late,
    down_bias_late,
    up_late,
    up_bias_late,
    readout_in,
    readout_in_bias,
    readout_out,
    readout_out_bias,
    out_grad,
):
    mp = lax.axis_size("mp")
    dp = lax.axis_size("dp")
    width = features.shape[0]
    channels = width * mp
    n = SIDE * SIDE
    n2 = GRID * GRID
    se = down_early.shape[1]
    cols = readout_in.shape[1]
    out_cols = readout_out.shape[1]
    slot = dp_slots()

    feats = jnp.transpose(features.reshape(width, n))
    posn = jnp.transpose(position)
    w_early = jnp.transpose(conv_early, (1, 0, 2))
    w_late = jnp.transpose(conv_late, (1, 0, 2))
    pool = jnp.where(
        image_sizes[0] == SIDE, pool_matrix(SIDE, SIDE, GRID), pool_matrix(SMALL, SIDE, GRID)
    )
    pp = (pool[:, None, :, None] * pool[None, :, None, :]).reshape(n2, n).astype(BF16)

    x, sums = call(
        prep_kernel, (shape((n, width)), shape((mp, 8, n))), image_sizes, feats, posn,
        smem=(0,), name="prep",
    )
    late_vec = jnp.broadcast_to(
        jnp.stack([gain_late, bias_late] * 4)[None], (mp, 8, width)
    )
    sums, late_all = swap(jnp.concatenate([sums, late_vec], axis=2)), None
    late_all = sums[:, :2, n:]
    sums = sums[:, :, :n]
    gain_all = late_all[:, 0].reshape(1, channels)
    bias_all = late_all[:, 1].reshape(1, channels)

    hid, mom = call(
        partial(hidden_kernel, channels), (shape((mp, n, width), BF16), shape((2, n, width))),
        image_sizes, x, sums, row(gain_early), row(bias_early), smem=(0,), name="hidden",
    )
    hid = swap(hid)

    gact = pl.pallas_call(
        act_grad_kernel,
        out_shape=shape((mp, n2, cols), BF16),
        grid=(mp,),
        in_specs=[
            pl.BlockSpec((n2, out_cols), lambda j: (0, 0)),
            pl.BlockSpec((cols, out_cols), lambda j: (j, 0)),
        ],
        out_specs=pl.BlockSpec((1, n2, cols), lambda j: (j, 0, 0)),
        cost_estimate=cost(2 * n2 * out_cols * cols * mp, cols * mp * out_cols * 2),
        name="act_grad",
    )(out_grad, readout_out)
    gact = swap(gact)

    conv1, pool_a, pool_b, sq1, rp1 = call(
        conv_kernel,
        (shape((n, width)), shape((n2, width)), shape((n2, width)), shape((1, width)), shape((mp, 8, se))),
        image_sizes, hid, w_early, row(conv_bias_early), x, pp, down_early,
        smem=(0,), flops=2 * n * channels * 9 * width, name="conv",
    )
    rp1 = swap(rp1)
    pooled_own, rpre1, e1 = call(
        pooled_kernel, (shape((mp, n2, width)), shape((1, se)), shape((1, width))),
        rp1, row(down_bias_early), up_early, row(up_bias_early), pool_a, pool_b, name="pooled",
    )
    pooled = swap(pooled_own)

    hid2, conv2, sq2, rp2 = call(
        late_kernel,
        (shape((n2, channels), BF16), shape((n2, width)), shape((1, width)), shape((mp, 8, se))),
        pooled, gain_all, bias_all, w_late, row(conv_bias_late), down_late,
        flops=2 * n2 * channels * 9 * width, name="late",
    )
    rp2 = swap(rp2)
    normed2, inv2, slope2 = call(
        late_slope_kernel,
        (shape((n2, channels)), shape((n2, 128)), shape((n2, channels))),
        pooled, gain_all, bias_all, name="late_slope",
    )
    tok, rpre2, e2 = call(
        token_kernel, (shape((mp, n2, width), BF16), shape((1, se)), shape((1, width))),
        rp2, row(down_bias_late), up_late, row(up_bias_late), pooled_own[0], conv2, name="tokens",
    )
    tok = swap(tok)

    act, gpre, gtok = call(
        readout_kernel,
        (shape((n2, cols), BF16), shape((n2, cols), BF16), shape((mp, n2, width), BF16)),
        tok, readout_in, row(readout_in_bias), gact,
        flops=4 * n2 * channels * cols, name="readout",
    )
    gtok = swap(gtok)
    g2, gl2, gr2 = call(
        late_back_a, (shape((n2, width)), shape((1, width)), shape((mp, 8, se))),
        gtok, conv2, e2, up_late, name="late_back_a",
    )
    gr2 = swap(gr2)
    gconv2, grp2, part2, gg2 = call(
        late_back_b,
        (shape((n2, width), BF16), shape((1, se)), shape((mp, n2, width), BF16), shape((2, channels))),
        gr2, rpre2, down_late, e2, g2, w_late, normed2, inv2, slope2, gain_all,
        flops=2 * n2 * channels * 9 * width, name="late_back_b",
    )
    part2 = swap(part2)
    gae, gl1, gr1 = call(
        early_back_a, (shape((n, width)), shape((1, width)), shape((mp, 8, se))),
        part2, g2, pool_b, e1, up_early, pp, name="early_back_a",
    )
    gg2_blocks = jnp.transpose(gg2.reshape(2, mp, width), (1, 0, 2))
    gg2_blocks = jnp.concatenate([gg2_blocks, jnp.zeros((mp, 6, width), F32)], axis=1)
    mixed = swap(jnp.concatenate([gr1, gg2_blocks], axis=2))
    gr1 = mixed[:, :, :se]
    gg2_own = jnp.sum(mixed[:, 0:2, se:], axis=0)
    gconv1, grp1, part1 = call(
        early_back_b,
        (shape((n, width), BF16), shape((1, se)), shape((mp, n, width), BF16)),
        image_sizes, gr1, rpre1, down_early, e1, gae, w_early,
        smem=(0,), flops=2 * n * channels * 9 * width, name="early_back_b",
    )
    part1 = swap(part1)
    gn1, gg1, gsum = call(
        early_back_c, (shape((n, width)), shape((2, width)), shape((mp, 8, n))),
        image_sizes, part1, x, mom, row(gain_early), row(bias_early), smem=(0,), name="early_back_c",
    )
    gsum = swap(gsum)
    fgrad, fgrad_low = call(
        partial(early_back_d, channels), (shape((n, width)), shape((n, width), BF16)),
        image_sizes, gsum, gn1, x, mom, gae, smem=(0,), name="early_back_d",
    )

    act_all = swap(jnp.broadcast_to(act[None], (mp, n2, cols)))
    tokens_out = pl.pallas_call(
        logits_kernel,
        out_shape=shape((n2, out_cols), BF16),
        grid=(mp,),
        in_specs=[
            pl.BlockSpec((1, n2, cols), lambda j: (j, 0, 0)),
            pl.BlockSpec((cols, out_cols), lambda j: (j, 0)),
            pl.BlockSpec((1, out_cols), lambda j: (0, 0)),
        ],
        out_specs=pl.BlockSpec((n2, out_cols), lambda j: (0, 0)),
        scratch_shapes=[pltpu.VMEM((n2, out_cols), F32)],
        cost_estimate=cost(2 * n2 * out_cols * cols * mp, cols * mp * out_cols * 2),
        name="logits",
    )(act_all, readout_out, row(readout_out_bias))

    grad_out_w, grad_out_b = dense_weights(slot, dp_gather(act_all), dp_gather(out_grad))
    grad_in_w, grad_in_b = dense_weights(slot, dp_gather(tok), dp_gather(gpre))
    grad_w2, grad_cb2 = conv_weights(GRID, slot, dp_gather(hid2), dp_gather(gconv2), channels, 2)
    grad_w1, grad_cb1 = conv_weights(SIDE, slot, dp_gather(hid), dp_gather(gconv1), channels, 2)

    red1 = jax.nn.silu(rpre1[0])
    red2 = jax.nn.silu(rpre2[0])
    vec = jnp.concatenate(
        [red1, red2, grp1[0], grp2[0], gl1[0], gl2[0], sq1[0], sq2[0], gg2_own[0], gg2_own[1]]
    )
    vecs = jnp.stack(in_order(dp_gather(vec, relay=False), slot))
    cuts = [se] * 4 + [width] * 6
    parts = []
    at = 0
    for size in cuts:
        parts.append(vecs[:, at : at + size])
        at += size
    outer = partial(mm, ca=0, cb=0, precision=HI)
    grad_up1 = outer(parts[0], parts[4])
    grad_up2 = outer(parts[1], parts[5])
    grad_down1 = outer(parts[6], parts[2])
    grad_down2 = outer(parts[7], parts[3])
    flat = jnp.sum(vecs[:, 2 * se :], axis=0)
    grad_db1, grad_db2 = flat[:se], flat[se : 2 * se]
    base = 2 * se
    grad_ub1, grad_ub2 = flat[base : base + width], flat[base + width : base + 2 * width]
    base = base + 4 * width
    grad_gain2, grad_bias2 = flat[base : base + width], flat[base + width : base + 2 * width]

    lows = in_order(dp_gather(fgrad_low, relay=False), slot)
    pos_grad = lows[0].astype(F32)
    for one in lows[1:]:
        pos_grad = pos_grad + one.astype(F32)
    ggs = in_order(dp_gather(gg1, relay=False), slot)
    gg1_all = ggs[0]
    for one in ggs[1:]:
        gg1_all = gg1_all + one

    return (
        tokens_out,
        jnp.transpose(fgrad).reshape(width, 1, n),
        jnp.transpose(pos_grad),
        gg1_all[0],
        gg1_all[1],
        jnp.transpose(grad_w1, (1, 0, 2)),
        grad_cb1[0],
        grad_down1,
        grad_db1,
        grad_up1,
        grad_ub1,
        grad_gain2,
        grad_bias2,
        jnp.transpose(grad_w2, (1, 0, 2)),
        grad_cb2[0],
        grad_down2,
        grad_db2,
        grad_up2,
        grad_ub2,
        grad_in_w,
        grad_in_b[0],
        grad_out_w,
        grad_out_b[0],
    )


def solution(mesh):
    by_mp = P("mp")
    block = (by_mp, by_mp, P(None, None, "mp"), by_mp, P("mp", None), P(), P(None, "mp"), by_mp)
    return jax.shard_map(
        per_device,
        mesh=mesh,
        in_specs=(P("mp", "dp", None), P("mp", None), P("dp"))
        + block
        + block
        + (P(None, "mp"), by_mp, P(None, "mp"), by_mp, P("dp", "mp")),
        out_specs=(P("dp", "mp"), P("mp", "dp", None), P("mp", None))
        + block
        + block
        + (P(None, "mp"), by_mp, P(None, "mp"), by_mp),
        check_vma=False,
    )
```

time: 934 us -> 363 us (0.39)
  waiting for transfers between devices: 516 us -> 114 us
  blocking collectives: 284 us -> 25.9 us
  Pallas kernels: 0 us -> 93.1 us
  starting transfers between devices: 0.51 us -> 72.7 us
  matrix products: 78.5 us -> 6.83 us
    psum x1 -> x0, waiting for transfers between devices: 332 us -> none  [per_device(): lax.psum((position_part, early_grads[0], early_grads[1], early_grads[2],...]
    psum x9 -> x0, blocking collectives: 228 us -> none  [the longest x2 71.9 us: block_forward(): lax.psum((jnp.sum(inputs, axis=0), jnp.sum(inputs * inputs, axis=0)), 'mp')]
    reduce_scatter x4 -> x0, waiting for transfers between devices: 152 us -> none  [the longest x2 93.7 us: block_backward(): lax.psum_scatter(conv_back_term(row_count * lax.axis_size('mp'), kernel=k...]
    pallas_call x0 -> x20, Pallas kernels: none -> 93.1 us  [the longest x14 43.7 us: call(): pl.pallas_call(kernel, out_shape=list(outs), in_specs=specs, out_specs=[p...]
    all_to_all x0 -> x12, waiting for transfers between devices: none -> 84.5 us  [swap(): return lax.all_to_all(v, 'mp', 0, 0)]
    dot_general x72 -> x4, matrix products: 78.5 us -> 6.83 us  [mm(): lax.dot_general(a, b, (((ca,), (cb,)), ((), ())), preferred_element_type=...]
    all_gather x2 -> x0, blocking collectives: 55.9 us -> none  [contract_in(): lax.all_gather(local_rows, 'mp', axis=0, tiled=True)]
    all_to_all x0 -> x12, starting transfers between devices: none -> 54.1 us  [swap(): return lax.all_to_all(v, 'mp', 0, 0)]
  transfers between devices with their start and end apart: 7 -> 45, of which waited for: 5 -> 14; matrix products, arithmetic and copies ran while one was open for 8% -> 8% of each run, Pallas kernels for 0% -> 18%
where the time goes in v1:
time: 363 us; the launch traced here: 360 us
  waiting for transfers between devices  114 us (31%)
  Pallas kernels  93.1 us (26%)
  starting transfers between devices  72.7 us (20%)
  blocking collectives  25.9 us (7%)
  other arithmetic  21.2 us (6%)
  local copies, waits for them, and re-layouts  16.7 us (5%)
  between operations  9.6 us (3%)
  matrix products  6.83 us (2%)
    all_to_all x12, waiting for transfers between devices, swap(): return lax.all_to_all(v, 'mp', 0, 0)  84.5 us
    all_to_all x12, starting transfers between devices, swap(): return lax.all_to_all(v, 'mp', 0, 0)  54.1 us
    pallas_call x14, Pallas kernels, call(): pl.pallas_call(kernel, out_shape=list(outs), in_specs=specs, out_specs=[p...  43.7 us
    ppermute x33, waiting for transfers between devices, dp_permute(): return lax.ppermute(v, 'dp', [(i, fn(i) % n) for i in range(n)])  29.6 us
    all_to_all x2, blocking collectives, swap(): return lax.all_to_all(v, 'mp', 0, 0)  25.9 us
    ppermute x33, starting transfers between devices, dp_permute(): return lax.ppermute(v, 'dp', [(i, fn(i) % n) for i in range(n)])  18.7 us
    pallas_call x2, Pallas kernels, dense_weights(): pl.pallas_call(partial(dense_weight_kernel, images), out_shape=[shape((bl...  18.1 us
    pallas_call x2, Pallas kernels, conv_weights(): pl.pallas_call(partial(conv_weight_kernel, side, images), out_shape=[shap...  17.7 us
  transfers between devices with their start and end apart: 45, of which 14 were waited for; matrix products, arithmetic and copies ran while one was open for 8% of the time, Pallas kernels for 18%

profile of v1, /device:TPU:0, one launch (start us, length us, event | category | flops | bytes accessed | tf_op | source)
XLA Modules:
  0.0 360.1 jit_solution(12926324191978850480)
XLA Ops:
  5.6 15.0 %all_to_all.70 = f32[8,8,704]{2,1,0:T(8,128)S(1)} all-to-all(f32[8,8,704]{2,1,0:T(8,128)S(1)} %pad_maximum_fusion.8), channel_id=1, replica_groups=mesh['dp'=4,'mp'=8] {'mp'}, dimensions={0} | all-to-all | bytes 360448 | tf_op jit(solution)/shard_map/all_to_all | solution.py:475
  29.6 26.5 %all-to-all-done.1.h_ref = bf16[8,576,128]{2,1,0:T(8,128)(2,1)S(1)} async-done(((bf16[8,576,128]{2,1,0:T(8,128)(2,1)}), bf16[8,576,128]{2,1,0:T(8,128)(2,1)S(1)}, u32[]{:S(2)}, u32[]{:S(2)}) %all-to-all-start.1) | async-done | bytes 1179680 | tf_op jit(solution)/shard_map/all_to_all | solution.py:475
  57.1 5.2 %conv.1 = (f32[576,128]{1,0:T(8,128)}, f32[144,128]{1,0:T(8,128)}, f32[144,128]{1,0:T(8,128)}, f32[1,128]{1,0:T(1,128)}, f32[8,8,256]{2,1,0:T(8,128)}) custom-call(s32[1]{0:T(128)S(6)} %copy.57.size_ref, bf16[8,576,128]{2,1,0:T(8,128)(2,1)} %copy-done.3, bf16[9,1024,128]{2,1,0:T(8,128)(2,1)} %bitcast.163, f32[1,128]{1,0:T(1,128)} %bitcast.166, ...), custom_call_target="tpu_custom_call" | custom-call | flops 1358954496 | bytes 4639748 | tf_op jit(solution)/shard_map/conv/pallas_call | solution.py:44
  62.2 10.9 %all_to_all.71.rp_ref = f32[8,8,256]{2,1,0:T(8,128)} all-to-all(f32[8,8,256]{2,1,0:T(8,128)} %get-tuple-element.76), channel_id=1, replica_groups=mesh['dp'=4,'mp'=8] {'mp'}, dimensions={0} | all-to-all | bytes 131072 | tf_op jit(solution)/shard_map/all_to_all | solution.py:475
  79.5 13.7 %all-to-all-done.3.pool_ref = f32[8,144,128]{2,1,0:T(8,128)S(1)} async-done(((f32[8,144,128]{2,1,0:T(8,128)}), f32[8,144,128]{2,1,0:T(8,128)S(1)}, u32[]{:S(2)}, u32[]{:S(2)}) %all-to-all-start.3) | async-done | bytes 589856 | tf_op jit(solution)/shard_map/all_to_all | solution.py:475
  101.1 7.0 %act_grad.1 = bf16[8,144,512]{2,1,0:T(8,128)(2,1)} custom-call(bf16[144,512]{1,0:T(8,128)(2,1)} %g_ref.1, bf16[4096,512]{1,0:T(8,128)(2,1)} %w_ref.5), custom_call_target="tpu_custom_call" | custom-call | flops 603979776 | bytes 4194304 | tf_op jit(solution)/shard_map/act_grad/pallas_call | solution.py:577
  108.8 6.0 %all-to-all-start.6 = ((bf16[8,144,512]{2,1,0:T(8,128)(2,1)}), bf16[8,144,512]{2,1,0:T(8,128)(2,1)S(1)}, u32[]{:S(2)}, u32[]{:S(2)}) async-start(bf16[8,144,512]{2,1,0:T(8,128)(2,1)} %act_grad.1), calls=%async_computation.6 | async-start | bytes 2359296 | tf_op jit(solution)/shard_map/all_to_all | solution.py:475
  119.9 22.3 %all-to-all-done.6.gh_ref = bf16[8,144,512]{2,1,0:T(8,128)(2,1)S(1)} async-done(((bf16[8,144,512]{2,1,0:T(8,128)(2,1)}), bf16[8,144,512]{2,1,0:T(8,128)(2,1)S(1)}, u32[]{:S(2)}, u32[]{:S(2)}) %all-to-all-start.6) | async-done | bytes 1179680 | tf_op jit(solution)/shard_map/all_to_all | solution.py:475
  148.3 4.2 %collective-permute-done.31 = bf16[144,512]{1,0:T(8,128)(2,1)S(1)} collective-permute-done((bf16[144,512]{1,0:T(8,128)(2,1)S(1)}, bf16[144,512]{1,0:T(8,128)(2,1)S(1)}, u32[]{:S(2)}, u32[]{:S(2)}) %collective-permute-start.31) | collective-permute-done | bytes 147488 | tf_op jit(solution)/shard_map/ppermute | solution.py:480
  167.4 6.1 %all-to-all-start.8 = ((bf16[8,144,128]{2,1,0:T(8,128)(2,1)}), bf16[8,144,128]{2,1,0:T(8,128)(2,1)S(1)}, u32[]{:S(2)}, u32[]{:S(2)}) async-start(bf16[8,144,128]{2,1,0:T(8,128)(2,1)} %get-tuple-element.84), calls=%async_computation.8 | async-start | bytes 589824 | tf_op jit(solution)/shard_map/all_to_all | solution.py:475
  186.3 3.9 %all-to-all-start.9 = ((f32[8,8,256]{2,1,0:T(8,128)}), f32[8,8,256]{2,1,0:T(8,128)S(1)}, u32[]{:S(2)}, u32[]{:S(2)}) async-start(f32[8,8,256]{2,1,0:T(8,128)} %get-tuple-element.86), calls=%async_computation.9 | async-start | bytes 131072 | tf_op jit(solution)/shard_map/all_to_all | solution.py:475
  191.7 5.4 %all-to-all-done.9.gr_ref = f32[8,8,256]{2,1,0:T(8,128)S(1)} async-done(((f32[8,8,256]{2,1,0:T(8,128)}), f32[8,8,256]{2,1,0:T(8,128)S(1)}, u32[]{:S(2)}, u32[]{:S(2)}) %all-to-all-start.9) | async-done | bytes 65568 | tf_op jit(solution)/shard_map/all_to_all | solution.py:475
  197.7 4.2 %late_back_b.1 = (bf16[144,128]{1,0:T(8,128)(2,1)}, f32[1,256]{1,0:T(1,128)}, bf16[8,144,128]{2,1,0:T(8,128)(2,1)}, f32[2,1024]{1,0:T(2,128)}) custom-call(f32[8,8,256]{2,1,0:T(8,128)} %copy-done.16, f32[1,256]{1,0:T(1,128)} %get-tuple-element.87.rpre_ref, f32[128,256]{1,0:T(8,128)} %down_ref.6, f32[1,128]{1,0:T(1,128)} %get-tuple-element.85.e_ref, ...), custom_call_target="tpu_custom_call" | custom-call | flops 339738624 | bytes 4229632 | tf_op jit(solution)/shard_map/late_back_b/pallas_call | solution.py:44
  218.9 4.8 %all-to-all-start.11 = ((f32[8,8,384]{2,1,0:T(8,128)}), f32[8,8,384]{2,1,0:T(8,128)S(1)}, u32[]{:S(2)}, u32[]{:S(2)}) async-start(f32[8,8,384]{2,1,0:T(8,128)} %select_maximum_fusion), calls=%async_computation.11 | async-start | bytes 196608 | tf_op jit(solution)/shard_map/all_to_all | solution.py:475
  223.7 7.6 %dense_weights_128.1 = (f32[1024,512]{1,0:T(8,128)}, f32[1,512]{1,0:T(1,128)}) custom-call(s32[4]{0:T(128)} %copy-done.21, bf16[4,8,144,128]{3,2,1,0:T(8,128)(2,1)} %pad_maximum_fusion.3.a_ref, bf16[4,144,512]{2,1,0:T(8,128)(2,1)} %pad_maximum_fusion.6.g_ref), custom_call_target="tpu_custom_call" | custom-call | flops 603979776 | bytes 3276800 | tf_op jit(solution)/shard_map/dense_weights_128/pallas_call | solution.py:454
  233.2 6.0 %all-to-all-start.7 = ((bf16[8,144,512]{2,1,0:T(8,128)(2,1)}), bf16[8,144,512]{2,1,0:T(8,128)(2,1)S(1)}, u32[]{:S(2)}, u32[]{:S(2)}) async-start(bf16[8,144,512]{2,1,0:T(8,128)(2,1)} %broadcast_in_dim.17), calls=%async_computation.7 | async-start | bytes 2359296 | tf_op jit(solution)/shard_map/all_to_all | solution.py:475
  239.8 5.1 %early_back_b.1 = (bf16[576,128]{1,0:T(8,128)(2,1)}, f32[1,256]{1,0:T(1,128)}, bf16[8,576,128]{2,1,0:T(8,128)(2,1)}) custom-call(s32[1]{0:T(128)S(6)} %copy.57.size_ref, f32[8,8,256]{2,1,0:T(8,128)} %slice.132.gr_ref, f32[1,256]{1,0:T(1,128)} %get-tuple-element.96.rpre_ref, f32[128,256]{1,0:T(8,128)} %down_ref.7, f32[1,128]{1,0:T(1,128)} %get-tuple-element.93.e_ref, ...), custom_call_target="tpu_custom_call" | custom-call | flops 1358954496 | bytes 4180484 | tf_op jit(solution)/shard_map/early_back_b/pallas_call | solution.py:44
  247.7 6.0 %conv_weights_12.1 = (f32[9,1024,128]{2,1,0:T(8,128)}, f32[1,128]{1,0:T(1,128)}) custom-call(s32[4]{0:T(128)} %copy-done.21, bf16[4,144,1024]{2,1,0:T(8,128)(2,1)} %pad_maximum_fusion.2.h_ref, bf16[4,144,128]{2,1,0:T(8,128)(2,1)} %pad_maximum_fusion.9.g_ref), custom_call_target="tpu_custom_call" | custom-call | flops 1358954496 | bytes 5898240 | tf_op jit(solution)/shard_map/conv_weights_12/pallas_call | solution.py:423
  255.5 12.4 %all-to-all-done.7.act_ref = bf16[8,144,512]{2,1,0:T(8,128)(2,1)S(1)} async-done(((bf16[8,144,512]{2,1,0:T(8,128)(2,1)}), bf16[8,144,512]{2,1,0:T(8,128)(2,1)S(1)}, u32[]{:S(2)}, u32[]{:S(2)}) %all-to-all-start.7) | async-done | bytes 1179680 | tf_op jit(solution)/shard_map/all_to_all | solution.py:475
  283.7 15.5 %collective-permute-done.28 = bf16[8,144,512]{2,1,0:T(8,128)(2,1)S(1)} collective-permute-done((bf16[8,144,512]{2,1,0:T(8,128)(2,1)S(1)}, bf16[8,144,512]{2,1,0:T(8,128)(2,1)S(1)}, u32[]{:S(2)}, u32[]{:S(2)}) %collective-permute-start.28) | collective-permute-done | bytes 1179680 | tf_op jit(solution)/shard_map/ppermute | solution.py:480
  299.3 11.7 %conv_weights_24.1 = (f32[9,1024,128]{2,1,0:T(8,128)}, f32[1,128]{1,0:T(1,128)}) custom-call(s32[4]{0:T(128)} %copy-done.21, bf16[4,8,576,128]{3,2,1,0:T(8,128)(2,1)} %pad_maximum_fusion.h_ref, bf16[4,576,128]{2,1,0:T(8,128)(2,1)} %pad_maximum_fusion.5.g_ref), custom_call_target="tpu_custom_call" | custom-call | flops 5435817984 | bytes 9437184 | tf_op jit(solution)/shard_map/conv_weights_24/pallas_call | solution.py:423
  317.3 5.7 %all-to-all-start.13 = ((f32[8,8,576]{2,1,0:T(8,128)}), f32[8,8,576]{2,1,0:T(8,128)S(1)}, u32[]{:S(2)}, u32[]{:S(2)}) async-start(f32[8,8,576]{2,1,0:T(8,128)} %get-tuple-element.100), calls=%async_computation.13 | async-start | bytes 327680 | tf_op jit(solution)/shard_map/all_to_all | solution.py:475
  323.0 6.6 %logits.1 = bf16[144,512]{1,0:T(8,128)(2,1)} custom-call(bf16[8,144,512]{2,1,0:T(8,128)(2,1)} %copy-done, bf16[4096,512]{1,0:T(8,128)(2,1)} %w_ref.5, f32[1,512]{1,0:T(1,128)} %bitcast.145), custom_call_target="tpu_custom_call" | custom-call | flops 603979776 | bytes 4194304 | tf_op jit(solution)/shard_map/logits/pallas_call | solution.py:668
  349.7 10.5 %dense_weights_512.1 = (f32[4096,512]{1,0:T(8,128)}, f32[1,512]{1,0:T(1,128)}) custom-call(s32[4]{0:T(128)} %copy-done.21, bf16[4,8,144,512]{3,2,1,0:T(8,128)(2,1)} %pad_maximum_fusion.1.a_ref, bf16[4,144,512]{2,1,0:T(8,128)(2,1)} %pad_maximum_fusion.7.g_ref), custom_call_target="tpu_custom_call" | custom-call | flops 2415919104 | bytes 13107200 | tf_op jit(solution)/shard_map/dense_weights_512/pallas_call | solution.py:454
  (206 shorter events, 128.2 us)
Async XLA Ops:
  24.4 31.7 %all-to-all-start.1 = ((bf16[8,576,128]{2,1,0:T(8,128)(2,1)}), bf16[8,576,128]{2,1,0:T(8,128)(2,1)S(1)}, u32[]{:S(2)}, u32[]{:S(2)}) async-start(bf16[8,576,128]{2,1,0:T(8,128)(2,1)} %get-tuple-element.75), calls=%async_computation.1 | async-start | bytes 2359296 | tf_op jit(solution)/shard_map/all_to_all | solution.py:475
  75.2 17.9 %all-to-all-start.3 = ((f32[8,144,128]{2,1,0:T(8,128)}), f32[8,144,128]{2,1,0:T(8,128)S(1)}, u32[]{:S(2)}, u32[]{:S(2)}) async-start(f32[8,144,128]{2,1,0:T(8,128)} %get-tuple-element.79), calls=%async_computation.3 | async-start | bytes 1179648 | tf_op jit(solution)/shard_map/all_to_all | solution.py:475
  108.8 33.4 %all-to-all-start.6 = ((bf16[8,144,512]{2,1,0:T(8,128)(2,1)}), bf16[8,144,512]{2,1,0:T(8,128)(2,1)S(1)}, u32[]{:S(2)}, u32[]{:S(2)}) async-start(bf16[8,144,512]{2,1,0:T(8,128)(2,1)} %act_grad.1), calls=%async_computation.6 | async-start | bytes 2359296 | tf_op jit(solution)/shard_map/all_to_all | solution.py:475
  114.8 33.0 %collective-permute-start.7 = (bf16[8,576,128]{2,1,0:T(8,128)(2,1)S(1)}, bf16[8,576,128]{2,1,0:T(8,128)(2,1)}, u32[]{:S(2)}, u32[]{:S(2)}) collective-permute-start(bf16[8,576,128]{2,1,0:T(8,128)(2,1)S(1)} %copy-done.4), channel_id=1, source_target_pairs={{0,16},{8,24},{16,0},{24,8},{1,17},{9,25},{17,1},{25,9},{2,18},{10... | collective-permute-start | bytes 3538952 | tf_op jit(solution)/shard_map/ppermute | solution.py:480
  142.2 21.2 %all-to-all-start.5 = ((bf16[8,144,128]{2,1,0:T(8,128)(2,1)}), bf16[8,144,128]{2,1,0:T(8,128)(2,1)S(1)}, u32[]{:S(2)}, u32[]{:S(2)}) async-start(bf16[8,144,128]{2,1,0:T(8,128)(2,1)} %get-tuple-element.82), calls=%async_computation.5 | async-start | bytes 589824 | tf_op jit(solution)/shard_map/all_to_all | solution.py:475
  147.3 14.2 %collective-permute-start.16 = (bf16[144,1024]{1,0:T(8,128)(2,1)S(1)}, bf16[144,1024]{1,0:T(8,128)(2,1)S(1)}, u32[]{:S(2)}, u32[]{:S(2)}) collective-permute-start(bf16[144,1024]{1,0:T(8,128)(2,1)S(1)} %copy-done.15), channel_id=1, source_target_pairs={{0,16},{8,24},{16,0},{24,8},{1,17},{9,25},{17,1},{25,9},{2,18},{10... | collective-permute-start | bytes 884744 | tf_op jit(solution)/shard_map/ppermute | solution.py:480
  147.8 57.7 %collective-permute-start.6 = (bf16[8,576,128]{2,1,0:T(8,128)(2,1)S(1)}, bf16[8,576,128]{2,1,0:T(8,128)(2,1)}, u32[]{:S(2)}, u32[]{:S(2)}) collective-permute-start(bf16[8,576,128]{2,1,0:T(8,128)(2,1)S(1)} %copy-done.4), channel_id=1, source_target_pairs={{0,8},{8,0},{16,24},{24,16},{1,9},{9,1},{17,25},{25,17},{2,10},{10... | collective-permute-start | bytes 3538952 | tf_op jit(solution)/shard_map/ppermute | solution.py:480
  147.8 57.7 %collective-permute-start.8 = (bf16[8,576,128]{2,1,0:T(8,128)(2,1)}, bf16[8,576,128]{2,1,0:T(8,128)(2,1)}, u32[]{:S(2)}, u32[]{:S(2)}) collective-permute-start(bf16[8,576,128]{2,1,0:T(8,128)(2,1)} %collective-permute-done.7), channel_id=1, source_target_pairs={{0,8},{8,0},{16,24},{24,16},{1,9},{9,1},{17,25},{25,17},{2,10},{10... | collective-permute-start | bytes 3538952 | tf_op jit(solution)/shard_map/ppermute | solution.py:480
  160.9 16.6 %collective-permute-start.15 = (bf16[144,1024]{1,0:T(8,128)(2,1)S(1)}, bf16[144,1024]{1,0:T(8,128)(2,1)}, u32[]{:S(2)}, u32[]{:S(2)}) collective-permute-start(bf16[144,1024]{1,0:T(8,128)(2,1)S(1)} %copy-done.15), channel_id=1, source_target_pairs={{0,8},{8,0},{16,24},{24,16},{1,9},{9,1},{17,25},{25,17},{2,10},{10... | collective-permute-start | bytes 884744 | tf_op jit(solution)/shard_map/ppermute | solution.py:480
  161.5 16.1 %collective-permute-start.17 = (bf16[144,1024]{1,0:T(8,128)(2,1)S(1)}, bf16[144,1024]{1,0:T(8,128)(2,1)}, u32[]{:S(2)}, u32[]{:S(2)}) collective-permute-start(bf16[144,1024]{1,0:T(8,128)(2,1)S(1)} %collective-permute-done.16), channel_id=1, source_target_pairs={{0,8},{8,0},{16,24},{24,16},{1,9},{9,1},{17,25},{25,17},{2,10},{10... | collective-permute-start | bytes 884744 | tf_op jit(solution)/shard_map/ppermute | solution.py:480
  167.4 16.2 %all-to-all-start.8 = ((bf16[8,144,128]{2,1,0:T(8,128)(2,1)}), bf16[8,144,128]{2,1,0:T(8,128)(2,1)S(1)}, u32[]{:S(2)}, u32[]{:S(2)}) async-start(bf16[8,144,128]{2,1,0:T(8,128)(2,1)} %get-tuple-element.84), calls=%async_computation.8 | async-start | bytes 589824 | tf_op jit(solution)/shard_map/all_to_all | solution.py:475
  177.5 13.9 %collective-permute-start.22 = (bf16[8,144,128]{2,1,0:T(8,128)(2,1)S(1)}, bf16[8,144,128]{2,1,0:T(8,128)(2,1)S(1)}, u32[]{:S(2)}, u32[]{:S(2)}) collective-permute-start(bf16[8,144,128]{2,1,0:T(8,128)(2,1)S(1)} %copy-done.8), channel_id=1, source_target_pairs={{0,16},{8,24},{16,0},{24,8},{1,17},{9,25},{17,1},{25,9},{2,18},{10... | collective-permute-start | bytes 884744 | tf_op jit(solution)/shard_map/ppermute | solution.py:480
  190.2 20.8 %collective-permute-start.21 = (bf16[8,144,128]{2,1,0:T(8,128)(2,1)S(1)}, bf16[8,144,128]{2,1,0:T(8,128)(2,1)S(1)}, u32[]{:S(2)}, u32[]{:S(2)}) collective-permute-start(bf16[8,144,128]{2,1,0:T(8,128)(2,1)S(1)} %copy-done.8), channel_id=1, source_target_pairs={{0,8},{8,0},{16,24},{24,16},{1,9},{9,1},{17,25},{25,17},{2,10},{10... | collective-permute-start | bytes 884744 | tf_op jit(solution)/shard_map/ppermute | solution.py:480
  191.4 19.6 %collective-permute-start.23 = (bf16[8,144,128]{2,1,0:T(8,128)(2,1)S(1)}, bf16[8,144,128]{2,1,0:T(8,128)(2,1)S(1)}, u32[]{:S(2)}, u32[]{:S(2)}) collective-permute-start(bf16[8,144,128]{2,1,0:T(8,128)(2,1)S(1)} %collective-permute-done.22), channel_id=1, source_target_pairs={{0,8},{8,0},{16,24},{24,16},{1,9},{9,1},{17,25},{25,17},{2,10},{10... | collective-permute-start | bytes 884744 | tf_op jit(solution)/shard_map/ppermute | solution.py:480
  212.2 19.2 %collective-permute-start.18 = (bf16[144,128]{1,0:T(8,128)(2,1)S(1)}, bf16[144,128]{1,0:T(8,128)(2,1)S(1)}, u32[]{:S(2)}, u32[]{:S(2)}) collective-permute-start(bf16[144,128]{1,0:T(8,128)(2,1)S(1)} %copy-done.20), channel_id=1, source_target_pairs={{0,8},{8,0},{16,24},{24,16},{1,9},{9,1},{17,25},{25,17},{2,10},{10... | collective-permute-start | bytes 110600 | tf_op jit(solution)/shard_map/ppermute | solution.py:480
  213.4 18.0 %collective-permute-start.20 = (bf16[144,128]{1,0:T(8,128)(2,1)S(1)}, bf16[144,128]{1,0:T(8,128)(2,1)S(1)}, u32[]{:S(2)}, u32[]{:S(2)}) collective-permute-start(bf16[144,128]{1,0:T(8,128)(2,1)S(1)} %collective-permute-done.19), channel_id=1, source_target_pairs={{0,8},{8,0},{16,24},{24,16},{1,9},{9,1},{17,25},{25,17},{2,10},{10... | collective-permute-start | bytes 110600 | tf_op jit(solution)/shard_map/ppermute | solution.py:480
  233.2 34.7 %all-to-all-start.7 = ((bf16[8,144,512]{2,1,0:T(8,128)(2,1)}), bf16[8,144,512]{2,1,0:T(8,128)(2,1)S(1)}, u32[]{:S(2)}, u32[]{:S(2)}) async-start(bf16[8,144,512]{2,1,0:T(8,128)(2,1)} %broadcast_in_dim.17), calls=%async_computation.7 | async-start | bytes 2359296 | tf_op jit(solution)/shard_map/all_to_all | solution.py:475
  253.7 24.1 %collective-permute-start.10 = (bf16[576,128]{1,0:T(8,128)(2,1)}, bf16[576,128]{1,0:T(8,128)(2,1)}, u32[]{:S(2)}, u32[]{:S(2)}) collective-permute-start(bf16[576,128]{1,0:T(8,128)(2,1)} %get-tuple-element.105), channel_id=1, source_target_pairs={{0,16},{8,24},{16,0},{24,8},{1,17},{9,25},{17,1},{25,9},{2,18},{10... | collective-permute-start | bytes 442376 | tf_op jit(solution)/shard_map/ppermute | solution.py:480
  255.3 26.0 %collective-permute-start.9 = (bf16[576,128]{1,0:T(8,128)(2,1)}, bf16[576,128]{1,0:T(8,128)(2,1)}, u32[]{:S(2)}, u32[]{:S(2)}) collective-permute-start(bf16[576,128]{1,0:T(8,128)(2,1)} %get-tuple-element.105), channel_id=1, source_target_pairs={{0,8},{8,0},{16,24},{24,16},{1,9},{9,1},{17,25},{25,17},{2,10},{10... | collective-permute-start | bytes 442376 | tf_op jit(solution)/shard_map/ppermute | solution.py:480
  267.9 43.1 %all-to-all-start.12 = ((bf16[8,576,128]{2,1,0:T(8,128)(2,1)}), bf16[8,576,128]{2,1,0:T(8,128)(2,1)S(1)}, u32[]{:S(2)}, u32[]{:S(2)}) async-start(bf16[8,576,128]{2,1,0:T(8,128)(2,1)} %get-tuple-element.98), calls=%async_computation.12 | async-start | bytes 2359296 | tf_op jit(solution)/shard_map/all_to_all | solution.py:475
  271.7 27.5 %collective-permute-start.28 = (bf16[8,144,512]{2,1,0:T(8,128)(2,1)S(1)}, bf16[8,144,512]{2,1,0:T(8,128)(2,1)S(1)}, u32[]{:S(2)}, u32[]{:S(2)}) collective-permute-start(bf16[8,144,512]{2,1,0:T(8,128)(2,1)S(1)} %all-to-all-done.7.act_ref), channel_id=1, source_target_pairs={{0,16},{8,24},{16,0},{24,8},{1,17},{9,25},{17,1},{25,9},{2,18},{10... | collective-permute-start | bytes 3538952 | tf_op jit(solution)/shard_map/ppermute | solution.py:480
  283.2 62.8 %collective-permute-start.27 = (bf16[8,144,512]{2,1,0:T(8,128)(2,1)S(1)}, bf16[8,144,512]{2,1,0:T(8,128)(2,1)}, u32[]{:S(2)}, u32[]{:S(2)}) collective-permute-start(bf16[8,144,512]{2,1,0:T(8,128)(2,1)S(1)} %all-to-all-done.7.act_ref), channel_id=1, source_target_pairs={{0,8},{8,0},{16,24},{24,16},{1,9},{9,1},{17,25},{25,17},{2,10},{10... | collective-permute-start | bytes 3538952 | tf_op jit(solution)/shard_map/ppermute | solution.py:480
  299.3 46.7 %collective-permute-start.29 = (bf16[8,144,512]{2,1,0:T(8,128)(2,1)S(1)}, bf16[8,144,512]{2,1,0:T(8,128)(2,1)}, u32[]{:S(2)}, u32[]{:S(2)}) collective-permute-start(bf16[8,144,512]{2,1,0:T(8,128)(2,1)S(1)} %collective-permute-done.28), channel_id=1, source_target_pairs={{0,8},{8,0},{16,24},{24,16},{1,9},{9,1},{17,25},{25,17},{2,10},{10... | collective-permute-start | bytes 3538952 | tf_op jit(solution)/shard_map/ppermute | solution.py:480
  315.1 14.5 %collective-permute-start.5 = (f32[2,128]{1,0:T(2,128)}, f32[2,128]{1,0:T(2,128)S(1)}, u32[]{:S(2)}, u32[]{:S(2)}) collective-permute-start(f32[2,128]{1,0:T(2,128)} %get-tuple-element.104), channel_id=1, source_target_pairs={{0,24},{8,16},{16,8},{24,0},{1,25},{9,17},{17,9},{25,1},{2,26},{10... | collective-permute-start | bytes 3080 | tf_op jit(solution)/shard_map/ppermute | solution.py:480
  (52 other events, 485.0 us)

commit v2 on v1

v2 whole, which is shorter than its diff:
```python
from functools import partial

import jax
import jax.numpy as jnp
from jax import lax
from jax.experimental import pallas as pl
from jax.experimental.pallas import tpu as pltpu
from jax.sharding import PartitionSpec as P

SIDE = 24
SMALL = 16
GRID = 12
EPS = 1e-06
F32 = jnp.float32
BF16 = jnp.bfloat16
HI = lax.Precision.HIGHEST


def pool_matrix(extent, side_len, grid_len):
    row_index = jnp.arange(grid_len)[:, None]
    col_index = jnp.arange(side_len)[None, :]
    first_col = row_index * extent // grid_len
    end_col = -(-(row_index + 1) * extent // grid_len)
    in_bin = (col_index >= first_col) & (col_index < end_col)
    return jnp.where(in_bin, 1.0, 0.0).astype(F32) / (end_col - first_col).astype(F32)


def shape(dims, dtype=F32):
    return jax.ShapeDtypeStruct(dims, dtype)


def cost(flops, nbytes):
    return pl.CostEstimate(flops=int(flops), bytes_accessed=int(nbytes), transcendentals=0)


def call(kernel, outs, *args, flops=1e6, smem=(), name=None):
    specs = [
        pl.BlockSpec(memory_space=pltpu.SMEM if k in smem else pltpu.VMEM)
        for k in range(len(args))
    ]
    nbytes = sum(a.size * a.dtype.itemsize for a in args) + sum(
        o.size * jnp.dtype(o.dtype).itemsize for o in outs
    )
    return pl.pallas_call(
        kernel,
        out_shape=list(outs),
        in_specs=specs,
        out_specs=[pl.BlockSpec(memory_space=pltpu.VMEM) for _ in outs],
        cost_estimate=cost(flops, nbytes),
        name=name,
    )(*args)


def mm(a, b, ca, cb, precision=None):
    return lax.dot_general(
        a, b, (((ca,), (cb,)), ((), ())), preferred_element_type=F32, precision=precision
    )


def sigmoid(v):
    return 1.0 / (1.0 + jnp.exp(-v))


def silu_grad(v):
    s = sigmoid(v)
    return s * (1.0 + v * (1.0 - s))


def grid_rc(side, lanes):
    i = lax.broadcasted_iota(jnp.int32, (side * side, lanes), 0).astype(F32)
    r = jnp.floor((i + 0.5) * (1.0 / side))
    return r, i - r * side


def tap_ok(r, c, side, dy, dx):
    ok = None
    for v, d in ((r, dy), (c, dx)):
        if d == 0:
            continue
        one = (v >= 0.5) if d < 0 else (v <= side - 1.5)
        ok = one if ok is None else ok & one
    return ok


def tap_sum(y, side, width):
    n = side * side
    r, c = grid_rc(side, width)
    total = None
    for t in range(9):
        dy, dx = t // 3 - 1, t % 3 - 1
        part = y[:, t * width : (t + 1) * width]
        off = dy * side + dx
        if off:
            part = pltpu.roll(part, (-off) % n, 0)
        ok = tap_ok(r, c, side, dy, dx)
        if ok is not None:
            part = jnp.where(ok, part, 0.0)
        total = part if total is None else total + part
    return total


def tap_spread(g, side, width):
    n = side * side
    r, c = grid_rc(side, width)
    parts = []
    for t in range(9):
        dy, dx = t // 3 - 1, t % 3 - 1
        off = dy * side + dx
        part = pltpu.roll(g, off % n, 0) if off else g
        ok = tap_ok(r, c, side, -dy, -dx)
        if ok is not None:
            part = jnp.where(ok, part, 0.0)
        parts.append(part.astype(BF16))
    return jnp.concatenate(parts, axis=1)


def wide(ref):
    return jnp.concatenate([ref[j] for j in range(ref.shape[0])], axis=1)


def split_mm(p, v, ca, cb):
    top = v.astype(BF16)
    low = (v - top.astype(F32)).astype(BF16)
    return mm(p, top, ca, cb) + mm(p, low, ca, cb)


def size_mask(size, width):
    r, c = grid_rc(SIDE, width)
    s = size.astype(F32) - 0.5
    return jnp.where((r < s) & (c < s), 1.0, 0.0).astype(F32)


def put_all(ref, value):
    for j in range(ref.shape[0]):
        ref[j] = value


def pieces_of(v, count):
    out = []
    for _ in range(count):
        top = v.astype(BF16).astype(F32)
        out.append(top)
        v = v - top
    return out


def tail_rows(total):
    return -(-total // 16) * 16


def pack(rows, width):
    height = tail_rows(len(rows))
    index = lax.broadcasted_iota(jnp.int32, (height, width), 0)
    out = jnp.zeros((height, width), F32)
    for k, one in enumerate(rows):
        out = jnp.where(index == k, one, out)
    return out.astype(BF16)


def chop(v, width):
    return [
        p[:, k * width : (k + 1) * width]
        for p in pieces_of(v, 3)
        for k in range(v.shape[1] // width)
    ]


def join(acc, first, length):
    k = length // acc.shape[1]
    rows = [acc[first + i : first + i + 1] for i in range(3 * k)]
    return jnp.concatenate([rows[i] + rows[k + i] + rows[2 * k + i] for i in range(k)], axis=1)


def plain_join(acc, length):
    k = length // acc.shape[1]
    return jnp.concatenate([acc[i : i + 1] for i in range(k)], axis=1)


def block_sum(ref, first, last):
    acc = ref[0, first:last, :].astype(F32)
    for j in range(1, ref.shape[0]):
        acc = acc + ref[j, first:last, :].astype(F32)
    return acc


def wide_rows(ref, first, last):
    return jnp.concatenate([ref[j, first:last, :] for j in range(ref.shape[0])], axis=1)


def two_mm(v, w, cb):
    top, low = pieces_of(jnp.broadcast_to(v, (8, v.shape[1])), 2)
    return (mm(top.astype(BF16), w, 1, cb) + mm(low.astype(BF16), w, 1, cb))[0:1]


def small_mm(v, w, cb):
    return mm(jnp.broadcast_to(v, (8, v.shape[1])), w, 1, cb, HI)[0:1]


def per_side(size, width):
    size = size.astype(F32)
    return 1.0 / (size * size + jnp.zeros((1, width), F32))


def silu(v):
    return v * sigmoid(v)


def flat_rows(v, width):
    return [v[:, k * width : (k + 1) * width] for k in range(v.shape[1] // width)]


def pack32(rows, width):
    height = -(-len(rows) // 8) * 8
    index = lax.broadcasted_iota(jnp.int32, (height, width), 0)
    out = jnp.zeros((height, width), F32)
    for k, one in enumerate(rows):
        out = jnp.where(index == k, one, out)
    return out


def lead_rows(n, width):
    return tail_rows(12 + -(-n // width))


def prep_kernel(place_ref, size_ref, f_ref, p_ref, up1_ref, up2_ref, *rest):
    vec_refs, out_ref = rest[:-1], rest[-1]
    n, width = f_ref.shape
    x = (f_ref[...].astype(F32) + p_ref[...].astype(F32)) * size_mask(size_ref[0], width)
    middle = (jnp.sum(x, axis=1, keepdims=True) * (1.0 / width)).astype(BF16).astype(F32)
    lane = lax.broadcasted_iota(jnp.int32, (n, width), 1)
    line = mm(jnp.ones((8, width), F32), jnp.where(lane == 0, middle, 0.0), 1, 1)[0:1]
    count = -(-n // width)
    if count * width > n:
        line = jnp.concatenate([line, jnp.zeros((1, count * width - n), F32)], axis=1)
    rows = []
    for ref in vec_refs:
        rows += pieces_of(ref[...], 2)
    rows += flat_rows(line, width)
    part = (out_ref.shape[1] - n - tail_rows(len(rows))) // 2
    start = pl.multiple_of(place_ref[0] * part, part)
    up = [r[pl.ds(start, part), :].astype(BF16) for r in (up1_ref, up2_ref)]
    value = jnp.concatenate([(x - middle).astype(BF16), pack(rows, width)] + up, axis=0)
    put_all(out_ref, value)


def lead_of(x_ref, n):
    width = x_ref.shape[2]
    return [x_ref[j, n : n + lead_rows(n, width), :].astype(F32) for j in range(x_ref.shape[0])]


def restore_x(x_ref, lead, n):
    blocks, _, width = x_ref.shape
    count = -(-n // width)
    lines = [
        jnp.concatenate([p[12 + k : 13 + k] for k in range(count)], axis=1)[:, :n] for p in lead
    ]
    lines = jnp.concatenate(lines, axis=0)
    shape2 = (blocks, blocks * width)
    col = lax.broadcasted_iota(jnp.int32, shape2, 1).astype(F32)
    home = lax.broadcasted_iota(jnp.int32, shape2, 0).astype(F32)
    here = jnp.floor((col + 0.5) * (1.0 / width)) == home
    spread = mm(lines, jnp.where(here, 1.0, 0.0).astype(F32), 0, 0)
    return wide_rows(x_ref, 0, n).astype(F32) + spread


def unpack_up_kernel(images, slot_ref, *refs):
    parts, (up1_ref, up2_ref, buf_ref, sems) = refs[:images], refs[images:]
    fetch(slot_ref, parts, buf_ref, sems, whole_ref)
    arrive(parts, buf_ref, sems, whole_ref)
    q = buf_ref.shape[2] // 2
    for s in range(images):
        both = jnp.concatenate([buf_ref[s, j] for j in range(buf_ref.shape[1])], axis=1)
        up1_ref[s * q : (s + 1) * q, :] = both[:q]
        up2_ref[s * q : (s + 1) * q, :] = both[q:]


def unpack_up(slot, parts, se, channels):
    images = len(parts)
    return pl.pallas_call(
        partial(unpack_up_kernel, images),
        out_shape=[shape((se, channels), BF16), shape((se, channels), BF16)],
        in_specs=[pl.BlockSpec(memory_space=pltpu.SMEM)] + any_specs(images),
        out_specs=[pl.BlockSpec(memory_space=pltpu.VMEM)] * 2,
        scratch_shapes=[
            pltpu.VMEM((images,) + parts[0].shape, BF16), pltpu.SemaphoreType.DMA((images,))
        ],
        cost_estimate=cost(1e6, 2e6),
        name="unpack_up",
    )(slot, *parts)


def norm_rows(x, gain, bias):
    scale = 1.0 / x.shape[1]
    center = jnp.sum(x, axis=1, keepdims=True) * scale
    d = x - center
    inv = lax.rsqrt(jnp.sum(d * d, axis=1, keepdims=True) * scale + EPS)
    normed = d * inv
    return normed, inv, normed * gain + bias


def front_kernel(
    size_ref, x_ref, w_ref, cb_ref, pp_ref, down_ref, vec_ref, h_ref, pay_ref, a_ref, b_ref, sq_ref
):
    out = w_ref.shape[2]
    blocks = x_ref.shape[0]
    n = SIDE * SIDE
    packed = lead_of(x_ref, n)
    x = restore_x(x_ref, packed, n)
    a_ref[...] = split_mm(pp_ref[...], x, 1, 0)
    for k in range(6):
        vec_ref[k : k + 1] = jnp.concatenate(
            [p[2 * k : 2 * k + 1] + p[2 * k + 1 : 2 * k + 2] for p in packed], axis=1
        )
    vec_ref[6:8] = jnp.zeros((2, vec_ref.shape[1]), F32)
    _, _, pre = norm_rows(x, vec_ref[0:1], vec_ref[1:2])
    mask = size_mask(size_ref[0], out)
    h = (silu(pre) * jnp.concatenate([mask] * blocks, axis=1)).astype(BF16)
    h_ref[...] = h
    y = mm(h, wide(w_ref), 1, 0)
    conv = (tap_sum(y, SIDE, out) + cb_ref[...]) * mask
    pooled = split_mm(pp_ref[...], conv, 1, 0)
    b_ref[...] = pooled
    sq = jnp.sum(conv, axis=0, keepdims=True) * per_side(size_ref[0], out)
    sq_ref[...] = sq
    tail = pack32(flat_rows(small_mm(sq, down_ref[...], 0), out), out)
    put_all(pay_ref, jnp.concatenate([pooled, tail], axis=0))


def early_slope_kernel(size_ref, x_ref, vec_ref, n_ref, i_ref, d_ref):
    blocks, _, width = x_ref.shape
    x = restore_x(x_ref, lead_of(x_ref, SIDE * SIDE), SIDE * SIDE)
    normed, inv, pre = norm_rows(x, vec_ref[0:1], vec_ref[1:2])
    n_ref[...] = normed
    i_ref[...] = jnp.broadcast_to(inv, i_ref.shape)
    mask = size_mask(size_ref[0], width)
    d_ref[...] = silu_grad(pre) * jnp.concatenate([mask] * blocks, axis=1)


def late_kernel(
    ball_ref, a_ref, up_all_ref, db_ref, vec_ref, up_ref, ub_ref, w_ref, cb_ref, down_ref,
    h_ref, pool_ref, pay_ref, conv_ref, sq_ref, rpre_ref, e_ref, eall_ref,
):
    out = w_ref.shape[2]
    n = GRID * GRID
    rpre = plain_join(block_sum(ball_ref, n, ball_ref.shape[1]), db_ref.shape[1]) + db_ref[...]
    rpre_ref[...] = rpre
    red = silu(rpre)
    e_all = sigmoid(two_mm(red, up_all_ref[...], 0) + vec_ref[4:5])
    eall_ref[...] = e_all
    e_ref[...] = sigmoid(small_mm(red, up_ref[...], 0) + ub_ref[...])
    pooled = a_ref[...] + wide_rows(ball_ref, 0, n) * e_all
    pool_ref[...] = pooled
    _, _, pre = norm_rows(pooled, vec_ref[2:3], vec_ref[3:4])
    h = silu(pre).astype(BF16)
    h_ref[...] = h
    y = mm(h, wide(w_ref), 1, 0)
    conv = tap_sum(y, GRID, out) + cb_ref[...]
    conv_ref[...] = conv
    sq = jnp.sum(conv, axis=0, keepdims=True) * (1.0 / n)
    sq_ref[...] = sq
    tail = pack32(flat_rows(small_mm(sq, down_ref[...], 0), out), out)
    put_all(pay_ref, jnp.concatenate([conv, tail], axis=0))


def late_slope_kernel(pool_ref, vec_ref, n_ref, i_ref, d_ref):
    normed, inv, pre = norm_rows(pool_ref[...], vec_ref[2:3], vec_ref[3:4])
    n_ref[...] = normed
    i_ref[...] = jnp.broadcast_to(inv, i_ref.shape)
    d_ref[...] = silu_grad(pre)


def put_blocks(ref, values, tails):
    step = ref.shape[2]
    for j in range(ref.shape[0]):
        tail = tails if not isinstance(tails, list) else tails[j]
        block = values[:, j * step : (j + 1) * step].astype(BF16)
        ref[j] = jnp.concatenate([block, tail], axis=0)


def readout_kernel(
    call_ref, pool_ref, up_all_ref, db_ref, vec_ref, up_ref, ub_ref, w_ref, b_ref, *rest
):
    gh_refs = rest[:-7]
    t_ref, act_ref, gp_ref, pay_ref, rpre_ref, e_ref, spare_ref = rest[-7:]
    n = GRID * GRID
    width = pay_ref.shape[2]
    rpre = plain_join(block_sum(call_ref, n, call_ref.shape[1]), db_ref.shape[1]) + db_ref[...]
    rpre_ref[...] = rpre
    red = silu(rpre)
    e_all = sigmoid(two_mm(red, up_all_ref[...], 0) + vec_ref[5:6])
    spare_ref[...] = e_all
    e_ref[...] = sigmoid(small_mm(red, up_ref[...], 0) + ub_ref[...])
    conv = wide_rows(call_ref, 0, n)
    tok = (pool_ref[...] + conv * e_all).astype(BF16)
    t_ref[...] = tok
    pre = mm(tok, w_ref[...], 1, 0) + b_ref[...]
    phi = 0.5 * (1.0 + lax.erf(pre * 0.7071067811865476))
    act_ref[...] = (pre * phi).astype(BF16)
    dens = 0.3989422804014327 * jnp.exp(-0.5 * pre * pre)
    gh = gh_refs[0][...].astype(F32)
    for one in gh_refs[1:]:
        gh = gh + one[...].astype(F32)
    gp = (gh * (phi + pre * dens)).astype(BF16)
    gp_ref[...] = gp
    gt = mm(gp, w_ref[...], 1, 1)
    gl = jnp.sum(gt * conv, axis=0, keepdims=True) * e_all * (1.0 - e_all)
    put_blocks(pay_ref, gt, pack(chop(two_mm(gl, up_all_ref[...], 1), width), width))


def act_grad_kernel(order_ref, g_ref, w_ref, out_ref):
    out_ref[0] = mm(g_ref[...], w_ref[...], 1, 1).astype(BF16)


def logits_kernel(blocks_ref, a0_ref, a1_ref, w_ref, b_ref, out_ref, acc_ref):
    j = pl.program_id(0)
    half = pl.num_programs(0) // 2

    @pl.when(j == 0)
    def _():
        acc_ref[...] = jnp.zeros_like(acc_ref)

    @pl.when(j < half)
    def _():
        acc_ref[...] += mm(a0_ref[0], w_ref[...], 1, 0)

    @pl.when(j >= half)
    def _():
        acc_ref[...] += mm(a1_ref[0], w_ref[...], 1, 0)

    @pl.when(j == pl.num_programs(0) - 1)
    def _():
        out_ref[...] = (acc_ref[...] + b_ref[...]).astype(BF16)


def squeeze_back(gr, rpre_ref, down_ref, grp_ref):
    grp = gr * silu_grad(rpre_ref[...])
    grp_ref[...] = grp
    return small_mm(grp, down_ref[...], 1)


def norm_back(gh, d_ref, n_ref, i_ref, gain):
    normed = n_ref[...]
    gpre = gh * d_ref[...]
    scale = 1.0 / gh.shape[1]
    g_gain = jnp.sum(gpre * normed, axis=0, keepdims=True)
    g_bias = jnp.sum(gpre, axis=0, keepdims=True)
    gn = gpre * gain
    m1 = jnp.sum(gn, axis=1, keepdims=True) * scale
    m2 = jnp.sum(gn * normed, axis=1, keepdims=True) * scale
    return (gn - m1 - normed * m2) * i_ref[:, 0:1], g_gain, g_bias


def gain_tails(extra, g_gain, g_bias, width, blocks):
    tails = []
    for j in range(blocks):
        rows = list(extra)
        for v in (g_gain, g_bias):
            rows += pieces_of(v[:, j * width : (j + 1) * width], 3)
        tails.append(pack(rows, width))
    return tails


def late_back_kernel(
    me_ref, gt_ref, conv_ref, e_ref, rpre_ref, down_ref, w_ref, n_ref, i_ref, d_ref, vec_ref,
    ball_ref, eall_ref, up_all_ref, gc_ref, grp_ref, gl_ref, pay_ref,
):
    out = w_ref.shape[2]
    blocks = pay_ref.shape[0]
    n = GRID * GRID
    se = rpre_ref.shape[1]
    g = block_sum(gt_ref, 0, n)
    e = e_ref[...]
    gl_ref[...] = jnp.sum(g * conv_ref[...], axis=0, keepdims=True) * e * (1.0 - e)
    gr = join(block_sum(gt_ref, n, gt_ref.shape[1]), 0, se)
    gs = squeeze_back(gr, rpre_ref, down_ref, grp_ref)
    gc = (g * e + gs * (1.0 / n)).astype(BF16)
    gc_ref[...] = gc
    gh = mm(tap_spread(gc.astype(F32), GRID, out), wide(w_ref), 1, 1)
    part, g_gain, g_bias = norm_back(gh, d_ref, n_ref, i_ref, vec_ref[2:3])
    own = [g * jnp.where(me_ref[0] == j, 1.0, 0.0).astype(F32) for j in range(blocks)]
    part = part + jnp.concatenate(own, axis=1)
    e_all = eall_ref[...]
    pooled = wide_rows(ball_ref, 0, n)
    gl1 = jnp.sum(part * pooled, axis=0, keepdims=True) * e_all * (1.0 - e_all)
    extra = chop(two_mm(gl1, up_all_ref[...], 1), out)
    put_blocks(pay_ref, part, gain_tails(extra, g_gain, g_bias, out, blocks))


def early_back_kernel(
    size_ref, p2_ref, b_ref, e_ref, rpre_ref, down_ref, pp_ref, w_ref, n_ref, i_ref, d_ref, vec_ref,
    gae_ref, gc_ref, grp_ref, gl_ref, gg_ref, pay_ref,
):
    out = w_ref.shape[2]
    blocks = pay_ref.shape[0]
    n2 = GRID * GRID
    se = rpre_ref.shape[1]
    g = block_sum(p2_ref, 0, n2)
    tail = block_sum(p2_ref, n2, p2_ref.shape[1])
    e = e_ref[...]
    gl_ref[...] = jnp.sum(g * b_ref[...], axis=0, keepdims=True) * e * (1.0 - e)
    used = 3 * (se // out)
    gg_ref[0:1] = join(tail, used, out)
    gg_ref[1:2] = join(tail, used + 3, out)
    gs = squeeze_back(join(tail, 0, se), rpre_ref, down_ref, grp_ref) * per_side(size_ref[0], out)
    gae = split_mm(pp_ref[...], g, 0, 0)
    gae_ref[...] = gae
    gc = ((gae * e + gs) * size_mask(size_ref[0], out)).astype(BF16)
    gc_ref[...] = gc
    gh = mm(tap_spread(gc.astype(F32), SIDE, out), wide(w_ref), 1, 1)
    part, g_gain, g_bias = norm_back(gh, d_ref, n_ref, i_ref, vec_ref[0:1])
    put_blocks(pay_ref, part, gain_tails([], g_gain, g_bias, out, blocks))


def final_kernel(size_ref, p1_ref, gae_ref, fg_ref, low_ref):
    n, width = gae_ref.shape
    out = (gae_ref[...] + block_sum(p1_ref, 0, n)) * size_mask(size_ref[0], width)
    fg_ref[...] = out
    tail = block_sum(p1_ref, n, p1_ref.shape[1])
    rows = []
    for k in range(2):
        rows += pieces_of(join(tail, 3 * k, width), 3)
    low_ref[...] = jnp.concatenate([out.astype(BF16), pack(rows, width)], axis=0)


def fetch(slot_ref, refs, dst_ref, sems, pick):
    for s in range(len(refs)):
        for q, ref in enumerate(refs):

            @pl.when(slot_ref[s] == q)
            def _():
                pltpu.make_async_copy(pick(ref), dst_ref.at[s], sems.at[s]).start()


def arrive(refs, dst_ref, sems, pick):
    for s in range(len(refs)):
        pltpu.make_async_copy(pick(refs[0]), dst_ref.at[s], sems.at[s]).wait()


def any_specs(count):
    return [pl.BlockSpec(memory_space=pl.ANY)] * count


def whole_ref(ref):
    return ref


def position_kernel(images, slot_ref, *refs):
    lows, (pos_ref, gg_ref, buf_ref, sems) = refs[:images], refs[images:]
    fetch(slot_ref, lows, buf_ref, sems, whole_ref)
    arrive(lows, buf_ref, sems, whole_ref)
    n = pos_ref.shape[0]
    acc = buf_ref[0].astype(F32)
    for s in range(1, images):
        acc = acc + buf_ref[s].astype(F32)
    pos_ref[...] = acc[:n]
    for k in range(2):
        gg_ref[k : k + 1] = join(acc[n:], 3 * k, acc.shape[1])


def position_sum(slot, lows):
    images = len(lows)
    tall, width = lows[0].shape
    n = SIDE * SIDE
    return pl.pallas_call(
        partial(position_kernel, images),
        out_shape=[shape((n, width)), shape((2, width))],
        in_specs=[pl.BlockSpec(memory_space=pltpu.SMEM)] + any_specs(images),
        out_specs=[pl.BlockSpec(memory_space=pltpu.VMEM)] * 2,
        scratch_shapes=[
            pltpu.VMEM((images, tall, width), BF16), pltpu.SemaphoreType.DMA((images,))
        ],
        cost_estimate=cost(1e6, images * tall * width * 2),
        name="position",
    )(slot, *lows)


def parcel_kernel(g1_ref, g2_ref, *refs):
    vecs, out_ref = refs[:-1], refs[-1]
    width = out_ref.shape[1]
    rows = []
    for ref in vecs[:2]:
        rows += chop(silu(ref[...]), width)
    for ref in vecs[2:8]:
        rows += chop(ref[...], width)
    rows += chop(vecs[8][0:1], width) + chop(vecs[8][1:2], width)
    out_ref[...] = jnp.concatenate([g1_ref[...], g2_ref[...], pack(rows, width)], axis=0)


def small_kernel(images, se, slot_ref, *refs):
    parcels = refs[:images]
    d1_ref, u1_ref, d2_ref, u2_ref, flat_ref, wide_ref, buf_ref, sems = refs[images:]
    first = SIDE * SIDE + GRID * GRID
    count = buf_ref.shape[1]

    def pick(ref):
        return ref.at[pl.ds(first, count), :]

    fetch(slot_ref, parcels, buf_ref, sems, pick)
    arrive(parcels, buf_ref, sems, pick)
    width = buf_ref.shape[2]
    lengths = [se] * 4 + [width] * 6
    tables = []
    at = 0
    tails = [buf_ref[s].astype(F32) for s in range(images)]
    for length in lengths:
        index = lax.broadcasted_iota(jnp.int32, (8, length), 0)
        table = jnp.zeros((8, length), F32)
        for s in range(images):
            table = jnp.where(index == s, join(tails[s], at, length), table)
        tables.append(table)
        at += 3 * (length // width)
    u1_ref[...] = mm(tables[0], tables[4], 0, 0, HI)
    u2_ref[...] = mm(tables[1], tables[5], 0, 0, HI)
    d1_ref[...] = mm(tables[6], tables[2], 0, 0, HI)
    d2_ref[...] = mm(tables[7], tables[3], 0, 0, HI)
    for k, table in enumerate(tables[2:4]):
        flat_ref[k : k + 1] = jnp.sum(table, axis=0, keepdims=True)
    for k, t in enumerate((4, 5, 8, 9)):
        wide_ref[k : k + 1] = jnp.sum(tables[t], axis=0, keepdims=True)


def small_grads(slot, parcels, se):
    images = len(parcels)
    tall, width = parcels[0].shape
    outs = [(width, se), (se, width), (width, se), (se, width), (2, se), (4, width)]
    return pl.pallas_call(
        partial(small_kernel, images, se),
        out_shape=[shape(o) for o in outs],
        in_specs=[pl.BlockSpec(memory_space=pltpu.SMEM)] + any_specs(images),
        out_specs=[pl.BlockSpec(memory_space=pltpu.VMEM)] * 6,
        scratch_shapes=[
            pltpu.VMEM((images, tall - SIDE * SIDE - GRID * GRID, width), BF16),
            pltpu.SemaphoreType.DMA((images,)),
        ],
        cost_estimate=cost(1e6, 1e6),
        name="small_grads",
    )(slot, *parcels)


def spread_all(images, side, g_ref, spread_ref, gb_ref):
    n = side * side
    total = None
    for s in range(images):
        g = g_ref[s].astype(F32)
        one = jnp.sum(g, axis=0, keepdims=True)
        total = one if total is None else total + one
        spread_ref[s * n : (s + 1) * n, :] = tap_spread(g, side, g.shape[1])
    gb_ref[...] = total


def early_weight_kernel(images, slot_ref, *refs):
    hids, parcels = refs[:images], refs[images : 2 * images]
    out_ref, gb_ref, h_ref, g_ref, spread_ref, sems, sems2 = refs[2 * images :]
    n = SIDE * SIDE
    out = g_ref.shape[2]
    step = pl.program_id(0)
    width = out_ref.shape[1]

    def pick(ref):
        return ref.at[pl.ds(0, n), :]

    @pl.when(step == 0)
    def _():
        fetch(slot_ref, parcels, g_ref, sems2, pick)
        fetch(slot_ref, hids, h_ref, sems, whole_ref)
        arrive(parcels, g_ref, sems2, pick)
        spread_all(images, SIDE, g_ref, spread_ref, gb_ref)
        arrive(hids, h_ref, sems, whole_ref)

    lanes = pl.ds(pl.multiple_of(step * width, width), width)
    h = jnp.concatenate([h_ref[s, :, lanes] for s in range(images)], axis=0)
    res = mm(h, spread_ref[...], 0, 0)
    for t in range(9):
        out_ref[t] = res[:, t * out : (t + 1) * out]


def early_weights(slot, hids, parcels, steps):
    images = len(hids)
    n, channels = hids[0].shape
    out = parcels[0].shape[1]
    rows = channels // steps
    return pl.pallas_call(
        partial(early_weight_kernel, images),
        out_shape=[shape((9, channels, out)), shape((1, out))],
        grid_spec=pltpu.PrefetchScalarGridSpec(
            num_scalar_prefetch=1,
            grid=(steps,),
            in_specs=any_specs(2 * images),
            out_specs=[
                pl.BlockSpec((9, rows, out), lambda k, s: (0, k, 0)),
                pl.BlockSpec((1, out), lambda k, s: (0, 0)),
            ],
            scratch_shapes=[
                pltpu.VMEM((images, n, channels), BF16),
                pltpu.VMEM((images, n, out), BF16),
                pltpu.VMEM((images * n, 9 * out), BF16),
                pltpu.SemaphoreType.DMA((images,)),
                pltpu.SemaphoreType.DMA((images,)),
            ],
        ),
        cost_estimate=cost(
            2 * images * n * 9 * out * channels, images * n * channels * 2 + 36 * channels * out
        ),
        name="early_weights",
    )(slot, *hids, *parcels)


def late_weight_kernel(images, channels, cols, slot_ref, *refs):
    cats, parcels = refs[:images], refs[images : 2 * images]
    w_ref, gb_ref, in_ref, ib_ref, c_ref, g_ref, spread_ref, sems, sems2 = refs[2 * images :]
    n = GRID * GRID
    out = g_ref.shape[2]
    step = pl.program_id(0)
    width = w_ref.shape[1]

    def pick_cat(ref):
        return ref.at[:, pl.ds(0, c_ref.shape[2])]

    def pick(ref):
        return ref.at[pl.ds(SIDE * SIDE, n), :]

    @pl.when(step == 0)
    def _():
        fetch(slot_ref, parcels, g_ref, sems2, pick)
        fetch(slot_ref, cats, c_ref, sems, pick_cat)
        arrive(parcels, g_ref, sems2, pick)
        spread_all(images, GRID, g_ref, spread_ref, gb_ref)
        arrive(cats, c_ref, sems, pick_cat)

    gp = jnp.concatenate([c_ref[s, :, 2 * channels :] for s in range(images)], axis=0)

    @pl.when(step == 0)
    def _():
        ib_ref[...] = jnp.sum(gp.astype(F32), axis=0, keepdims=True)

    lanes = pl.ds(pl.multiple_of(step * width, width), width)
    tok = jnp.concatenate([c_ref[s, :, lanes] for s in range(images)], axis=0)
    in_ref[...] = mm(tok, gp, 0, 0)
    lanes = pl.ds(pl.multiple_of(step * width + channels, width), width)
    h = jnp.concatenate([c_ref[s, :, lanes] for s in range(images)], axis=0)
    res = mm(h, spread_ref[...], 0, 0)
    for t in range(9):
        w_ref[t] = res[:, t * out : (t + 1) * out]


def late_weights(slot, cats, parcels, channels, cols, steps):
    images = len(cats)
    n = cats[0].shape[0]
    out = parcels[0].shape[1]
    rows = channels // steps
    return pl.pallas_call(
        partial(late_weight_kernel, images, channels, cols),
        out_shape=[
            shape((9, channels, out)), shape((1, out)), shape((channels, cols)), shape((1, cols))
        ],
        grid_spec=pltpu.PrefetchScalarGridSpec(
            num_scalar_prefetch=1,
            grid=(steps,),
            in_specs=any_specs(2 * images),
            out_specs=[
                pl.BlockSpec((9, rows, out), lambda k, s: (0, k, 0)),
                pl.BlockSpec((1, out), lambda k, s: (0, 0)),
                pl.BlockSpec((rows, cols), lambda k, s: (k, 0)),
                pl.BlockSpec((1, cols), lambda k, s: (0, 0)),
            ],
            scratch_shapes=[
                pltpu.VMEM((images, n, 2 * channels + cols), BF16),
                pltpu.VMEM((images, n, out), BF16),
                pltpu.VMEM((images * n, 9 * out), BF16),
                pltpu.SemaphoreType.DMA((images,)),
                pltpu.SemaphoreType.DMA((images,)),
            ],
        ),
        cost_estimate=cost(2 * images * n * (9 * out + cols) * channels, 12e6),
        name="late_weights",
    )(slot, *cats, *parcels)


def act_weight_kernel(images, offset, slot_ref, blocks_ref, *refs):
    act0, act1, cats = (refs[k * images : (k + 1) * images] for k in range(3))
    out_ref, gb_ref, a_ref, g_ref, sems0, sems1, sems2 = refs[3 * images :]
    j = pl.program_id(0)
    half = pl.num_programs(0) // 2

    def pick(ref):
        return ref.at[:, pl.ds(offset, g_ref.shape[2])]

    @pl.when(j == 0)
    def _():
        fetch(slot_ref, cats, g_ref, sems2, pick)
        fetch(slot_ref, act0, a_ref.at[0], sems0, whole_ref)
        fetch(slot_ref, act1, a_ref.at[1], sems1, whole_ref)
        arrive(cats, g_ref, sems2, pick)
        arrive(act0, a_ref.at[0], sems0, whole_ref)

    @pl.when(j == half)
    def _():
        arrive(act1, a_ref.at[1], sems1, whole_ref)

    g = jnp.concatenate([g_ref[s] for s in range(images)], axis=0)

    @pl.when(j == 0)
    def _():
        gb_ref[...] = jnp.sum(g.astype(F32), axis=0, keepdims=True)

    side = j // half
    k = j % half
    a = jnp.concatenate([a_ref[side, s, k] for s in range(images)], axis=0)
    out_ref[...] = mm(a, g, 0, 0)


def act_weights(slot, blocks, act0, act1, cats, offset, cols):
    images = len(act0)
    half, rows, width = act0[0].shape
    total = 2 * half
    return pl.pallas_call(
        partial(act_weight_kernel, images, offset),
        out_shape=[shape((total * width, cols)), shape((1, cols))],
        grid_spec=pltpu.PrefetchScalarGridSpec(
            num_scalar_prefetch=2,
            grid=(total,),
            in_specs=any_specs(3 * images),
            out_specs=[
                pl.BlockSpec((width, cols), lambda k, s, b: (b[k], 0)),
                pl.BlockSpec((1, cols), lambda k, s, b: (0, 0)),
            ],
            scratch_shapes=[
                pltpu.VMEM((2, images, half, rows, width), BF16),
                pltpu.VMEM((images, rows, cols), BF16),
            ]
            + [pltpu.SemaphoreType.DMA((images,))] * 3,
        ),
        cost_estimate=cost(
            2 * images * rows * total * width * cols, images * total * rows * width * 2 + total * width * cols * 4
        ),
        name="act_weights",
    )(slot, blocks, *act0, *act1, *cats)


def swap(v):
    return lax.all_to_all(v, "mp", 0, 0)


def permute(v, axis, fn):
    n = lax.axis_size(axis)
    return lax.ppermute(v, axis, [(i, fn(i) % n) for i in range(n)])


def dp_gather(v, relay=True):
    n = lax.axis_size("dp")
    slots = [v, permute(v, "dp", lambda i: i ^ 1)]
    for k in range(1, n // 2):
        far = permute(v, "dp", lambda i: i + 2 * k)
        slots.append(far)
        if relay:
            slots.append(permute(far, "dp", lambda i: i ^ 1))
        else:
            slots.append(permute(v, "dp", lambda i: ((i + 2 * k) % n) ^ 1))
    return slots


def after(v, *deps):
    return lax.optimization_barrier((v,) + deps)[0]


def dp_slots():
    n = lax.axis_size("dp")
    me = lax.axis_index("dp")
    s = jnp.arange(n)
    hops = (me // 2 - s // 2) % (n // 2)
    return (2 * hops + ((s ^ me) & 1)).astype(jnp.int32)


def row(v):
    return v.reshape(1, -1)


def per_device(
    features,
    position,
    image_sizes,
    gain_early,
    bias_early,
    conv_early,
    conv_bias_early,
    down_early,
    down_bias_early,
    up_early,
    up_bias_early,
    gain_late,
    bias_late,
    conv_late,
    conv_bias_late,
    down_late,
    down_bias_late,
    up_late,
    up_bias_late,
    readout_in,
    readout_in_bias,
    readout_out,
    readout_out_bias,
    out_grad,
):
    mp = lax.axis_size("mp")
    dp = lax.axis_size("dp")
    width = features.shape[0]
    channels = width * mp
    n = SIDE * SIDE
    n2 = GRID * GRID
    se = down_early.shape[1]
    cols = readout_in.shape[1]
    out_cols = readout_out.shape[1]
    half = mp // 2
    slot = dp_slots()
    me = lax.axis_index("mp")
    place = lax.axis_index("dp").reshape(1).astype(jnp.int32)
    mine = me.reshape(1).astype(jnp.int32)
    step = jnp.arange(half)
    sides = (me % 2) ^ jnp.arange(2)[:, None]
    send_order = (((me // 2 + step) % half)[None] * 2 + sides).reshape(-1).astype(jnp.int32)
    got_order = (((me // 2 - step) % half)[None] * 2 + sides).reshape(-1).astype(jnp.int32)

    feats = jnp.transpose(features.reshape(width, n))
    posn = jnp.transpose(position)
    w_early = jnp.transpose(conv_early, (1, 0, 2))
    w_late = jnp.transpose(conv_late, (1, 0, 2))
    pool = jnp.where(
        image_sizes[0] == SIDE, pool_matrix(SIDE, SIDE, GRID), pool_matrix(SMALL, SIDE, GRID)
    )
    pp = (pool[:, None, :, None] * pool[None, :, None, :]).reshape(n2, n).astype(BF16)
    vecs = (gain_early, bias_early, gain_late, bias_late, up_bias_early, up_bias_late)
    part = se // dp
    up_at = n + lead_rows(n, width)
    tall = up_at + 2 * part
    (pay,) = call(
        prep_kernel, (shape((mp, tall, width), BF16),), place, image_sizes, feats, posn,
        up_early, up_late, *[row(v) for v in vecs], smem=(0, 1), name="prep",
    )
    x_all = swap(pay)

    gact = pl.pallas_call(
        act_grad_kernel,
        out_shape=shape((mp, n2, cols), BF16),
        grid_spec=pltpu.PrefetchScalarGridSpec(
            num_scalar_prefetch=1,
            grid=(mp,),
            in_specs=[
                pl.BlockSpec((n2, out_cols), lambda j, o: (0, 0)),
                pl.BlockSpec((cols, out_cols), lambda j, o: (o[j], 0)),
            ],
            out_specs=pl.BlockSpec((1, n2, cols), lambda j, o: (j, 0, 0)),
        ),
        cost_estimate=cost(2 * n2 * out_cols * cols * mp, cols * mp * out_cols * 2),
        name="act_grad",
    )(send_order, out_grad, readout_out)
    theirs = permute(gact[half:], "mp", lambda i: i ^ 1)
    x_all = after(x_all, gact)
    gact = (gact[:half].astype(F32) + theirs.astype(F32)).astype(BF16)
    gact = [gact[0]] + [permute(gact[k], "mp", lambda i: i + 2 * k) for k in range(1, half)]

    up1_all, up2_all = unpack_up(slot, dp_gather(x_all[:, up_at:]), se, channels)
    tail0 = -(-(se // width) // 8) * 8
    tail1 = tail_rows(3 * (se // width))
    tail2 = tail_rows(3 * (se // width) + 6)
    vec_all, hid, pay, pool_a, pool_b, sq1 = call(
        front_kernel,
        (
            shape((8, channels)), shape((n, channels), BF16), shape((mp, n2 + tail0, width)),
            shape((n2, channels)), shape((n2, width)), shape((1, width)),
        ),
        image_sizes, x_all, w_early, row(conv_bias_early), pp, down_early,
        smem=(0,), flops=2 * n * channels * 9 * width, name="front",
    )
    b_all = swap(pay)
    normed1, inv1, slope1 = call(
        early_slope_kernel,
        (shape((n, channels)), shape((n, 128)), shape((n, channels))),
        image_sizes, x_all, vec_all, smem=(0,), name="early_slope",
    )
    hids = dp_gather(hid)
    b_all = after(b_all, slope1)
    hid2, pooled, pay, conv2, sq2, rpre1, e1, e1_all = call(
        late_kernel,
        (
            shape((n2, channels), BF16), shape((n2, channels)), shape((mp, n2 + tail0, width)),
            shape((n2, width)), shape((1, width)), shape((1, se)), shape((1, width)),
            shape((1, channels)),
        ),
        b_all, pool_a, up1_all, row(down_bias_early), vec_all, up_early, row(up_bias_early),
        w_late, row(conv_bias_late), down_late,
        flops=2 * n2 * channels * 9 * width, name="late",
    )
    c_all = swap(pay)
    normed2, inv2, slope2 = call(
        late_slope_kernel,
        (shape((n2, channels)), shape((n2, 128)), shape((n2, channels))),
        pooled, vec_all, name="late_slope",
    )
    c_all = after(c_all, slope2)
    tok, act, gpre, pay, rpre2, e2, _ = call(
        readout_kernel,
        (
            shape((n2, channels), BF16), shape((n2, cols), BF16), shape((n2, cols), BF16),
            shape((mp, n2 + tail1, width), BF16), shape((1, se)), shape((1, width)),
            shape((1, channels)),
        ),
        c_all, pooled, up2_all, row(down_bias_late), vec_all, up_late, row(up_bias_late),
        readout_in, row(readout_in_bias), *gact,
        flops=4 * n2 * channels * cols, name="readout",
    )
    gtok = swap(pay)
    cats = dp_gather(jnp.concatenate([tok, hid2, gpre, out_grad], axis=1))
    act0 = jnp.stack([act] + [permute(act, "mp", lambda i: i + 2 * k) for k in range(1, half)])
    act1 = permute(act0, "mp", lambda i: i ^ 1)
    tokens_out = pl.pallas_call(
        logits_kernel,
        out_shape=shape((n2, out_cols), BF16),
        grid_spec=pltpu.PrefetchScalarGridSpec(
            num_scalar_prefetch=1,
            grid=(mp,),
            in_specs=[
                pl.BlockSpec((1, n2, cols), lambda j, o: (jnp.minimum(j, half - 1), 0, 0)),
                pl.BlockSpec((1, n2, cols), lambda j, o: (jnp.maximum(j - half, 0), 0, 0)),
                pl.BlockSpec((cols, out_cols), lambda j, o: (o[j], 0)),
                pl.BlockSpec((1, out_cols), lambda j, o: (0, 0)),
            ],
            out_specs=pl.BlockSpec((n2, out_cols), lambda j, o: (0, 0)),
            scratch_shapes=[pltpu.VMEM((n2, out_cols), F32)],
        ),
        cost_estimate=cost(2 * n2 * out_cols * cols * mp, cols * mp * out_cols * 2),
        name="logits",
    )(got_order, act0, act1, readout_out, row(readout_out_bias))

    gconv2, grp2, gl2, pay = call(
        late_back_kernel,
        (
            shape((n2, width), BF16), shape((1, se)), shape((1, width)),
            shape((mp, n2 + tail2, width), BF16),
        ),
        mine, gtok, conv2, e2, rpre2, down_late, w_late, normed2, inv2, slope2, vec_all,
        b_all, e1_all, up1_all,
        smem=(0,), flops=2 * n2 * channels * 9 * width, name="late_back",
    )
    part2 = after(swap(pay), tokens_out)
    gae, gconv1, grp1, gl1, gg2, pay = call(
        early_back_kernel,
        (
            shape((n, width)), shape((n, width), BF16), shape((1, se)), shape((1, width)),
            shape((2, width)), shape((mp, n + 16, width), BF16),
        ),
        image_sizes, part2, pool_b, e1, rpre1, down_early, pp, w_early, normed1, inv1, slope1, vec_all,
        smem=(0,), flops=2 * n * channels * 9 * width, name="early_back",
    )
    part1 = swap(pay)
    (parcel,) = call(
        parcel_kernel, (shape((n + n2 + tail_rows(12 * (se // width) + 18), width), BF16),),
        gconv1, gconv2, rpre1, rpre2, grp1, grp2, gl1, gl2, sq1, sq2, gg2, name="parcel",
    )
    parcels = dp_gather(parcel, relay=False)
    grad_w2, grad_cb2, grad_in_w, grad_in_b = late_weights(slot, cats, parcels, channels, cols, 2)
    grad_w1, grad_cb1 = early_weights(slot, hids, parcels, 2)
    grad_down1, grad_up1, grad_down2, grad_up2, flat, lines = small_grads(slot, parcels, se)
    part1 = after(part1, grad_w1, grad_w2, flat)
    fgrad, low = call(
        final_kernel, (shape((n, width)), shape((n + 16, width), BF16)),
        image_sizes, part1, gae, smem=(0,), name="final",
    )
    pos_grad, gg1 = position_sum(slot, dp_gather(low, relay=False))
    grad_out_w, grad_out_b = act_weights(
        slot, got_order, dp_gather(act0), dp_gather(act1), cats, 2 * channels + cols, out_cols
    )

    return (
        tokens_out,
        jnp.transpose(fgrad).reshape(width, 1, n),
        jnp.transpose(pos_grad),
        gg1[0],
        gg1[1],
        jnp.transpose(grad_w1, (1, 0, 2)),
        grad_cb1[0],
        grad_down1,
        flat[0],
        grad_up1,
        lines[0],
        lines[2],
        lines[3],
        jnp.transpose(grad_w2, (1, 0, 2)),
        grad_cb2[0],
        grad_down2,
        flat[1],
        grad_up2,
        lines[1],
        grad_in_w,
        grad_in_b[0],
        grad_out_w,
        grad_out_b[0],
    )


def solution(mesh):
    by_mp = P("mp")
    block = (by_mp, by_mp, P(None, None, "mp"), by_mp, P("mp", None), P(), P(None, "mp"), by_mp)
    return jax.shard_map(
        per_device,
        mesh=mesh,
        in_specs=(P("mp", "dp", None), P("mp", None), P("dp"))
        + block
        + block
        + (P(None, "mp"), by_mp, P(None, "mp"), by_mp, P("dp", "mp")),
        out_specs=(P("dp", "mp"), P("mp", "dp", None), P("mp", None))
        + block
        + block
        + (P(None, "mp"), by_mp, P(None, "mp"), by_mp),
        check_vma=False,
    )
```

time: 363 us -> 288 us (0.79)
  blocking collectives: 25.9 us -> 0 us
  other arithmetic: 21.2 us -> 2.09 us
  starting transfers between devices: 72.7 us -> 53.9 us
  between operations: 9.6 us -> 1.67 us
  matrix products: 6.83 us -> 0 us
  Pallas kernels: 93.1 us -> 96.8 us
    all_to_all x12 -> x6, waiting for transfers between devices: 84.5 us -> 41.6 us  [swap(): return lax.all_to_all(v, 'mp', 0, 0)]
    ppermute x33 -> x29, waiting for transfers between devices: 29.6 us -> 71.5 us  [permute(): return lax.ppermute(v, axis, [(i, fn(i) % n) for i in range(n)])]
    all_to_all x12 -> x6, starting transfers between devices: 54.1 us -> 27.6 us  [swap(): return lax.all_to_all(v, 'mp', 0, 0)]
    all_to_all x2 -> x0, blocking collectives: 25.9 us -> none  [swap(): return lax.all_to_all(v, 'mp', 0, 0)]
    another operation x12 -> x1, other arithmetic: 17.5 us -> 0.99 us  [per_device(): jnp.stack([act] + [permute(act, 'mp', lambda i: i + 2 * k) for k in range...]
    ppermute x33 -> x29, starting transfers between devices: 18.7 us -> 26.2 us  [permute(): return lax.ppermute(v, axis, [(i, fn(i) % n) for i in range(n)])]
    dot_general x4 -> x0, matrix products: 6.83 us -> none  [mm(): lax.dot_general(a, b, (((ca,), (cb,)), ((), ())), preferred_element_type=...]
    unnamed x69 -> x57, local copies, waits for them, and re-layouts: 7.7 us -> 10.6 us
  transfers between devices with their start and end apart: 45 -> 35, of which waited for: 14 -> 11; matrix products, arithmetic and copies ran while one was open for 8% -> 4% of each run, Pallas kernels for 18% -> 28%
where the time goes in v2:
time: 288 us; the launch traced here: 287 us
  waiting for transfers between devices  113 us (39%)
  Pallas kernels  96.8 us (34%)
  starting transfers between devices  53.9 us (19%)
  local copies, waits for them, and re-layouts  19.4 us (7%)
    ppermute x29, waiting for transfers between devices, permute(): return lax.ppermute(v, axis, [(i, fn(i) % n) for i in range(n)])  71.5 us
    pallas_call x10, Pallas kernels, call(): pl.pallas_call(kernel, out_shape=list(outs), in_specs=specs, out_specs=[p...  43.2 us
    all_to_all x6, waiting for transfers between devices, swap(): return lax.all_to_all(v, 'mp', 0, 0)  41.6 us
    all_to_all x6, starting transfers between devices, swap(): return lax.all_to_all(v, 'mp', 0, 0)  27.6 us
    ppermute x29, starting transfers between devices, permute(): return lax.ppermute(v, axis, [(i, fn(i) % n) for i in range(n)])  26.2 us
    pallas_call x1, Pallas kernels, early_weights(): pl.pallas_call(partial(early_weight_kernel, images), out_shape=[shape((9,...  12.2 us
    unnamed x57, local copies, waits for them, and re-layouts  10.6 us
    pallas_call x1, Pallas kernels, act_weights(): pl.pallas_call(partial(act_weight_kernel, images, offset), out_shape=[sha...  10.2 us
  transfers between devices with their start and end apart: 35, of which 11 were waited for; matrix products, arithmetic and copies ran while one was open for 4% of the time, Pallas kernels for 28%

profile of v2, /device:TPU:0, one launch (start us, length us, event | category | flops | bytes accessed | tf_op | source)
XLA Modules:
  0.0 286.9 jit_solution(10913569255303756370)
XLA Ops:
  3.9 7.3 %all-to-all-start = ((bf16[8,736,128]{2,1,0:T(8,128)(2,1)}), bf16[8,736,128]{2,1,0:T(8,128)(2,1)S(1)}, u32[]{:S(2)}, u32[]{:S(2)}) async-start(bf16[8,736,128]{2,1,0:T(8,128)(2,1)} %prep.1), calls=%async_computation | async-start | bytes 3014656 | tf_op jit(solution)/shard_map/all_to_all | solution.py:841
  13.5 7.7 %act_grad.1 = bf16[8,144,512]{2,1,0:T(8,128)(2,1)} custom-call(s32[8]{0:T(128)} %add.141.order_ref, bf16[144,512]{1,0:T(8,128)(2,1)} %g_ref.1, bf16[4096,512]{1,0:T(8,128)(2,1)} %w_ref.5), custom_call_target="tpu_custom_call" | custom-call | flops 603979776 | bytes 4194304 | tf_op jit(solution)/shard_map/act_grad/pallas_call | solution.py:941
  21.2 25.6 %all-to-all-done.x_ref = bf16[8,736,128]{2,1,0:T(8,128)(2,1)S(1)} async-done(((bf16[8,736,128]{2,1,0:T(8,128)(2,1)}), bf16[8,736,128]{2,1,0:T(8,128)(2,1)S(1)}, u32[]{:S(2)}, u32[]{:S(2)}) %all-to-all-start) | async-done | bytes 1507360 | tf_op jit(solution)/shard_map/all_to_all | solution.py:841
  47.9 6.9 %front.1 = (f32[8,1024]{1,0:T(8,128)}, bf16[576,1024]{1,0:T(8,128)(2,1)}, f32[8,152,128]{2,1,0:T(8,128)}, f32[144,1024]{1,0:T(8,128)}, f32[144,128]{1,0:T(8,128)}, /*index=5*/f32[1,128]{1,0:T(1,128)}) custom-call(s32[1]{0:T(128)S(6)} %copy.50.size_ref, bf16[8,736,128]{2,1,0:T(8,128)(2,1)} %copy-done, bf16[9,1024,128]{2,1,0:T(8,128)(2,1)} %bitcast.61, ...), custom_call_target="tpu_custom_call" | custom-call | flops 1358954496 | bytes 6663172 | tf_op jit(solution)/shard_map/front/pallas_call | solution.py:44
  54.8 3.8 %all-to-all-start.1 = ((f32[8,152,128]{2,1,0:T(8,128)}), f32[8,152,128]{2,1,0:T(8,128)S(1)}, u32[]{:S(2)}, u32[]{:S(2)}) async-start(f32[8,152,128]{2,1,0:T(8,128)} %get-tuple-element.85), calls=%async_computation.1 | async-start | bytes 1245184 | tf_op jit(solution)/shard_map/all_to_all | solution.py:841
  61.2 6.4 %collective-permute-done.1.refs_2_ = bf16[8,128,128]{2,1,0:T(8,128)(2,1)S(1)} collective-permute-done((bf16[8,128,128]{2,1,0:T(8,128)(2,1)S(1)}, bf16[8,128,128]{2,1,0:T(8,128)(2,1)S(1)}, u32[]{:S(2)}, u32[]{:S(2)}) %collective-permute-start.1) | collective-permute-done | bytes 262176 | tf_op jit(solution)/shard_map/ppermute | solution.py:846
  70.0 5.7 %early_slope.1 = (f32[576,1024]{1,0:T(8,128)}, f32[576,128]{1,0:T(8,128)}, f32[576,1024]{1,0:T(8,128)}) custom-call(s32[1]{0:T(128)S(6)} %copy.50.size_ref, bf16[8,736,128]{2,1,0:T(8,128)(2,1)} %copy-done, f32[8,1024]{1,0:T(8,128)} %get-tuple-element.86.vec_ref), custom_call_target="tpu_custom_call" | custom-call | flops 1000000 | bytes 6553604 | tf_op jit(solution)/shard_map/early_slope/pallas_call | solution.py:44
  79.5 4.4 %late.1 = (bf16[144,1024]{1,0:T(8,128)(2,1)}, f32[144,1024]{1,0:T(8,128)}, f32[8,152,128]{2,1,0:T(8,128)}, f32[144,128]{1,0:T(8,128)}, f32[1,128]{1,0:T(1,128)},...) custom-call(f32[8,152,128]{2,1,0:T(8,128)} %copy-done.1, f32[144,1024]{1,0:T(8,128)} %get-tuple-element.89.a_ref, ...), custom_call_target="tpu_custom_call" | custom-call | flops 339738624 | bytes 5980160 | tf_op jit(solution)/shard_map/late/pallas_call | solution.py:44
  83.9 4.6 %all-to-all-start.2 = ((f32[8,152,128]{2,1,0:T(8,128)}), f32[8,152,128]{2,1,0:T(8,128)S(1)}, u32[]{:S(2)}, u32[]{:S(2)}) async-start(f32[8,152,128]{2,1,0:T(8,128)} %get-tuple-element.91), calls=%async_computation.2 | async-start | bytes 1245184 | tf_op jit(solution)/shard_map/all_to_all | solution.py:841
  89.3 3.8 %collective-permute-start.6 = (bf16[144,512]{1,0:T(8,128)(2,1)S(1)}, bf16[144,512]{1,0:T(8,128)(2,1)S(1)}, u32[]{:S(2)}, u32[]{:S(2)}) collective-permute-start(bf16[144,512]{1,0:T(8,128)(2,1)S(1)} %get-tuple-element.145), channel_id=1, source_target_pairs={{0,6},{1,7},{2,0},{3,1},{4,2},{5,3},{6,4},{7,5},{8,14},{9,15},{10,... | collective-permute-start | bytes 442376 | tf_op jit(solution)/shard_map/ppermute | solution.py:846
  96.8 16.0 %all-to-all-done.2.call_ref = f32[8,152,128]{2,1,0:T(8,128)S(1)} async-done(((f32[8,152,128]{2,1,0:T(8,128)}), f32[8,152,128]{2,1,0:T(8,128)S(1)}, u32[]{:S(2)}, u32[]{:S(2)}) %all-to-all-start.2) | async-done | bytes 622624 | tf_op jit(solution)/shard_map/all_to_all | solution.py:841
  112.8 5.3 %collective-permute-done.5.rest_2_ = bf16[144,512]{1,0:T(8,128)(2,1)S(1)} collective-permute-done((bf16[144,512]{1,0:T(8,128)(2,1)S(1)}, bf16[144,512]{1,0:T(8,128)(2,1)S(1)}, u32[]{:S(2)}, u32[]{:S(2)}) %collective-permute-start.5) | collective-permute-done | bytes 147488 | tf_op jit(solution)/shard_map/ppermute | solution.py:846
  118.8 4.4 %readout.1 = (bf16[144,1024]{1,0:T(8,128)(2,1)}, bf16[144,512]{1,0:T(8,128)(2,1)}, bf16[144,512]{1,0:T(8,128)(2,1)}, bf16[8,160,128]{2,1,0:T(8,128)(2,1)}, f32[1...) custom-call(f32[8,152,128]{2,1,0:T(8,128)} %copy-done.4, f32[144,1024]{1,0:T(8,128)} %get-tuple-element.92.pool_ref, ...), custom_call_target="tpu_custom_call" | custom-call | flops 301989888 | bytes 4465664 | tf_op jit(solution)/shard_map/readout/pallas_call | solution.py:44
  136.4 12.6 %collective-permute-done.8 = bf16[144,512]{1,0:T(8,128)(2,1)S(1)} collective-permute-done((bf16[144,512]{1,0:T(8,128)(2,1)}, bf16[144,512]{1,0:T(8,128)(2,1)S(1)}, u32[]{:S(2)}, u32[]{:S(2)}) %collective-permute-start.8) | collective-permute-done | bytes 147488 | tf_op jit(solution)/shard_map/ppermute | solution.py:846
  152.3 5.5 %late_back.1 = (bf16[144,128]{1,0:T(8,128)(2,1)}, f32[1,256]{1,0:T(1,128)}, f32[1,128]{1,0:T(1,128)}, bf16[8,160,128]{2,1,0:T(8,128)(2,1)}) custom-call(s32[1]{0:T(128)} %bitcast.27.me_ref, bf16[8,160,128]{2,1,0:T(8,128)(2,1)} %copy-done.7, f32[144,128]{1,0:T(8,128)} %get-tuple-element.98.conv_ref, f32[1,128]{1,0:T(1,128)} %get-tuple-element.99.e_ref, ...), custom_call_target="tpu_custom_call" | custom-call | flops 339738624 | bytes 5696516 | tf_op jit(solution)/shard_map/late_back/pallas_call | solution.py:44
  166.1 7.3 %logits.1 = bf16[144,512]{1,0:T(8,128)(2,1)} custom-call(s32[8]{0:T(128)} %add.136.blocks_ref, bf16[4,144,512]{2,1,0:T(8,128)(2,1)} %copy-done.5, bf16[4,144,512]{2,1,0:T(8,128)(2,1)} %copy-done.11, bf16[4096,512]{1,0:T(8,128)(2,1)} %w_ref.5, f32[1,512]{1,0:T(1,128)} %bitcast.70), custom_call_target="tpu_custom_call" | custom-call | flops 603979776 | bytes 4194304 | tf_op jit(solution)/shard_map/logits/pallas_call | solution.py:1015
  174.1 7.2 %early_back.1 = (f32[576,128]{1,0:T(8,128)}, bf16[576,128]{1,0:T(8,128)(2,1)}, f32[1,256]{1,0:T(1,128)}, f32[1,128]{1,0:T(1,128)}, f32[2,128]{1,0:T(2,128)}, /*index=5*/bf16[8,592,128]{2,1,0:T(8,128)(2,1)}) custom-call(s32[1]{0:T(128)S(6)} %copy.50.size_ref, bf16[8,160,128]{2,1,0:T(8,128)(2,1)} %copy-done.8, f32[144,128]{1,0:T(8,128)} %get-tuple-element.106.b_ref, ...), custom_call_target="tpu_custom_call" | custom-call | flops 1358954496 | bytes 9762820 | tf_op jit(solution)/shard_map/early_back/pallas_call | solution.py:44
  181.4 5.0 %all-to-all-start.5 = ((bf16[8,592,128]{2,1,0:T(8,128)(2,1)}), bf16[8,592,128]{2,1,0:T(8,128)(2,1)S(1)}, u32[]{:S(2)}, u32[]{:S(2)}) async-start(bf16[8,592,128]{2,1,0:T(8,128)(2,1)} %get-tuple-element.111), calls=%async_computation.5 | async-start | bytes 2424832 | tf_op jit(solution)/shard_map/all_to_all | solution.py:841
  192.5 20.7 %collective-permute-done.16.refs_7_.refs_3_ = bf16[768,128]{1,0:T(8,128)(2,1)S(1)} collective-permute-done((bf16[768,128]{1,0:T(8,128)(2,1)}, bf16[768,128]{1,0:T(8,128)(2,1)S(1)}, u32[]{:S(2)}, u32[]{:S(2)}) %collective-permute-start.16) | collective-permute-done | bytes 196640 | tf_op jit(solution)/shard_map/ppermute | solution.py:846
  225.8 8.0 %collective-permute-done.24.refs_2_ = bf16[4,144,512]{2,1,0:T(8,128)(2,1)} collective-permute-done((bf16[4,144,512]{2,1,0:T(8,128)(2,1)S(1)}, bf16[4,144,512]{2,1,0:T(8,128)(2,1)}, u32[]{:S(2)}, u32[]{:S(2)}) %collective-permute-start.24) | collective-permute-done | bytes 589856 | tf_op jit(solution)/shard_map/ppermute | solution.py:846
  234.3 10.5 %collective-permute-done.27.refs_6_ = bf16[4,144,512]{2,1,0:T(8,128)(2,1)} collective-permute-done((bf16[4,144,512]{2,1,0:T(8,128)(2,1)S(1)}, bf16[4,144,512]{2,1,0:T(8,128)(2,1)}, u32[]{:S(2)}, u32[]{:S(2)}) %collective-permute-start.27) | collective-permute-done | bytes 589856 | tf_op jit(solution)/shard_map/ppermute | solution.py:846
  244.9 12.2 %early_weights.1 = (f32[9,1024,128]{2,1,0:T(8,128)}, f32[1,128]{1,0:T(1,128)}) custom-call(s32[4]{0:T(128)} %fusion.6.slot_ref, bf16[576,1024]{1,0:T(8,128)(2,1)} %get-tuple-element.112.refs_0_, bf16[576,1024]{1,0:T(8,128)(2,1)} %collective-permute-done.11.refs_1_, bf16[576,1024]{1,0:T(8,128)(2,1)} %collective-permute-done.12.refs_2_, ...), custom_call_target="tpu_custom_call" | custom-call | flops 5435817984 | bytes 9437184 | tf_op jit(solution)/shard_map/early_weights/pallas_call | solution.py:682
  258.0 7.8 %late_weights.1 = (f32[9,1024,128]{2,1,0:T(8,128)}, f32[1,128]{1,0:T(1,128)}, f32[1024,512]{1,0:T(8,128)}, f32[1,512]{1,0:T(1,128)}) custom-call(s32[4]{0:T(128)} %fusion.6.slot_ref, bf16[144,3072]{1,0:T(8,128)(2,1)} %constant_dynamic-update-slice_fusion.refs_0_.refs_8_, bf16[144,3072]{1,0:T(8,128)(2,1)} %collective-permute-done.17.refs_1_.refs_9_, ...), custom_call_target="tpu_custom_call" | custom-call | flops 1962934272 | bytes 12000000 | tf_op jit(solution)/shard_map/late_weights/pallas_call | solution.py:751
  271.4 10.2 %act_weights.1 = (f32[4096,512]{1,0:T(8,128)}, f32[1,512]{1,0:T(1,128)}) custom-call(s32[4]{0:T(128)} %fusion.6.slot_ref, s32[8]{0:T(128)} %add.136.blocks_ref, bf16[4,144,512]{2,1,0:T(8,128)(2,1)} %copy-done.5, bf16[4,144,512]{2,1,0:T(8,128)(2,1)} %collective-permute-done.23.refs_1_, bf16[4,144,512]{2,1,0:T(8,128)(2,1)} %collective-permute-done.24.refs_2_, ...), custom_call_target="tpu_custom_call" | custom-call | flops 2415919104 | bytes 13107200 | tf_op jit(solution)/shard_map/act_weights/pallas_call | solution.py:816
  (142 shorter events, 76.4 us)
Async XLA Ops:
  3.9 42.9 %all-to-all-start = ((bf16[8,736,128]{2,1,0:T(8,128)(2,1)}), bf16[8,736,128]{2,1,0:T(8,128)(2,1)S(1)}, u32[]{:S(2)}, u32[]{:S(2)}) async-start(bf16[8,736,128]{2,1,0:T(8,128)(2,1)} %prep.1), calls=%async_computation | async-start | bytes 3014656 | tf_op jit(solution)/shard_map/all_to_all | solution.py:841
  54.8 23.9 %all-to-all-start.1 = ((f32[8,152,128]{2,1,0:T(8,128)}), f32[8,152,128]{2,1,0:T(8,128)S(1)}, u32[]{:S(2)}, u32[]{:S(2)}) async-start(f32[8,152,128]{2,1,0:T(8,128)} %get-tuple-element.85), calls=%async_computation.1 | async-start | bytes 1245184 | tf_op jit(solution)/shard_map/all_to_all | solution.py:841
  67.7 20.8 %collective-permute-start.3 = (bf16[4,144,512]{2,1,0:T(8,128)(2,1)S(1)}, bf16[4,144,512]{2,1,0:T(8,128)(2,1)S(1)}, u32[]{:S(2)}, u32[]{:S(2)}) collective-permute-start(bf16[4,144,512]{2,1,0:T(8,128)(2,1)S(1)} %slice.61), channel_id=1, source_target_pairs={{0,1},{1,0},{2,3},{3,2},{4,5},{5,4},{6,7},{7,6},{8,9},{9,8},{10,11... | collective-permute-start | bytes 1769480 | tf_op jit(solution)/shard_map/ppermute | solution.py:846
  83.9 28.9 %all-to-all-start.2 = ((f32[8,152,128]{2,1,0:T(8,128)}), f32[8,152,128]{2,1,0:T(8,128)S(1)}, u32[]{:S(2)}, u32[]{:S(2)}) async-start(f32[8,152,128]{2,1,0:T(8,128)} %get-tuple-element.91), calls=%async_computation.2 | async-start | bytes 1245184 | tf_op jit(solution)/shard_map/all_to_all | solution.py:841
  89.3 23.5 %collective-permute-start.6 = (bf16[144,512]{1,0:T(8,128)(2,1)S(1)}, bf16[144,512]{1,0:T(8,128)(2,1)S(1)}, u32[]{:S(2)}, u32[]{:S(2)}) collective-permute-start(bf16[144,512]{1,0:T(8,128)(2,1)S(1)} %get-tuple-element.145), channel_id=1, source_target_pairs={{0,6},{1,7},{2,0},{3,1},{4,2},{5,3},{6,4},{7,5},{8,14},{9,15},{10,... | collective-permute-start | bytes 442376 | tf_op jit(solution)/shard_map/ppermute | solution.py:846
  93.1 24.9 %collective-permute-start.5 = (bf16[144,512]{1,0:T(8,128)(2,1)S(1)}, bf16[144,512]{1,0:T(8,128)(2,1)S(1)}, u32[]{:S(2)}, u32[]{:S(2)}) collective-permute-start(bf16[144,512]{1,0:T(8,128)(2,1)S(1)} %get-tuple-element.146), channel_id=1, source_target_pairs={{0,4},{1,5},{2,6},{3,7},{4,0},{5,1},{6,2},{7,3},{8,12},{9,13},{10,... | collective-permute-start | bytes 442376 | tf_op jit(solution)/shard_map/ppermute | solution.py:846
  93.1 24.9 %collective-permute-start.4 = (bf16[144,512]{1,0:T(8,128)(2,1)S(1)}, bf16[144,512]{1,0:T(8,128)(2,1)S(1)}, u32[]{:S(2)}, u32[]{:S(2)}) collective-permute-start(bf16[144,512]{1,0:T(8,128)(2,1)S(1)} %get-tuple-element.147), channel_id=1, source_target_pairs={{0,2},{1,3},{2,4},{3,5},{4,6},{5,7},{6,0},{7,1},{8,10},{9,11},{10,... | collective-permute-start | bytes 442376 | tf_op jit(solution)/shard_map/ppermute | solution.py:846
  123.1 28.4 %all-to-all-start.3 = ((bf16[8,160,128]{2,1,0:T(8,128)(2,1)}), bf16[8,160,128]{2,1,0:T(8,128)(2,1)S(1)}, u32[]{:S(2)}, u32[]{:S(2)}) async-start(bf16[8,160,128]{2,1,0:T(8,128)(2,1)} %get-tuple-element.97), calls=%async_computation.3 | async-start | bytes 655360 | tf_op jit(solution)/shard_map/all_to_all | solution.py:841
  130.3 18.6 %collective-permute-start.8 = (bf16[144,512]{1,0:T(8,128)(2,1)}, bf16[144,512]{1,0:T(8,128)(2,1)S(1)}, u32[]{:S(2)}, u32[]{:S(2)}) collective-permute-start(bf16[144,512]{1,0:T(8,128)(2,1)} %get-tuple-element.96), channel_id=1, source_target_pairs={{0,4},{1,5},{2,6},{3,7},{4,0},{5,1},{6,2},{7,3},{8,12},{9,13},{10,... | collective-permute-start | bytes 442376 | tf_op jit(solution)/shard_map/ppermute | solution.py:846
  130.3 18.6 %collective-permute-start.7 = (bf16[144,512]{1,0:T(8,128)(2,1)}, bf16[144,512]{1,0:T(8,128)(2,1)S(1)}, u32[]{:S(2)}, u32[]{:S(2)}) collective-permute-start(bf16[144,512]{1,0:T(8,128)(2,1)} %get-tuple-element.96), channel_id=1, source_target_pairs={{0,2},{1,3},{2,4},{3,5},{4,6},{5,7},{6,0},{7,1},{8,10},{9,11},{10,... | collective-permute-start | bytes 442376 | tf_op jit(solution)/shard_map/ppermute | solution.py:846
  131.5 57.2 %collective-permute-start.12 = (bf16[576,1024]{1,0:T(8,128)(2,1)}, bf16[576,1024]{1,0:T(8,128)(2,1)}, u32[]{:S(2)}, u32[]{:S(2)}) collective-permute-start(bf16[576,1024]{1,0:T(8,128)(2,1)} %get-tuple-element.112.refs_0_), channel_id=1, source_target_pairs={{0,16},{8,24},{16,0},{24,8},{1,17},{9,25},{17,1},{25,9},{2,18},{10... | collective-permute-start | bytes 3538952 | tf_op jit(solution)/shard_map/ppermute | solution.py:846
  161.9 29.1 %collective-permute-start.11 = (bf16[576,1024]{1,0:T(8,128)(2,1)}, bf16[576,1024]{1,0:T(8,128)(2,1)}, u32[]{:S(2)}, u32[]{:S(2)}) collective-permute-start(bf16[576,1024]{1,0:T(8,128)(2,1)} %get-tuple-element.112.refs_0_), channel_id=1, source_target_pairs={{0,8},{8,0},{16,24},{24,16},{1,9},{9,1},{17,25},{25,17},{2,10},{10... | collective-permute-start | bytes 3538952 | tf_op jit(solution)/shard_map/ppermute | solution.py:846
  181.4 84.4 %all-to-all-start.5 = ((bf16[8,592,128]{2,1,0:T(8,128)(2,1)}), bf16[8,592,128]{2,1,0:T(8,128)(2,1)S(1)}, u32[]{:S(2)}, u32[]{:S(2)}) async-start(bf16[8,592,128]{2,1,0:T(8,128)(2,1)} %get-tuple-element.111), calls=%async_computation.5 | async-start | bytes 2424832 | tf_op jit(solution)/shard_map/all_to_all | solution.py:841
  187.1 35.4 %collective-permute-start.18 = (bf16[144,3072]{1,0:T(8,128)(2,1)}, bf16[144,3072]{1,0:T(8,128)(2,1)}, u32[]{:S(2)}, u32[]{:S(2)}) collective-permute-start(bf16[144,3072]{1,0:T(8,128)(2,1)} %constant_dynamic-update-slice_fusion.refs_0_.refs_8_), channel_id=1, source_target_pairs={{0,16},{8,24},{16,0},{24,8},{1,17},{9,25},{17,1},{25,9},{2,18},{10... | collective-permute-start | bytes 2654216 | tf_op jit(solution)/shard_map/ppermute | solution.py:846
  188.6 36.6 %collective-permute-start.13 = (bf16[576,1024]{1,0:T(8,128)(2,1)}, bf16[576,1024]{1,0:T(8,128)(2,1)}, u32[]{:S(2)}, u32[]{:S(2)}) collective-permute-start(bf16[576,1024]{1,0:T(8,128)(2,1)} %collective-permute-done.12.refs_2_), channel_id=1, source_target_pairs={{0,8},{8,0},{16,24},{24,16},{1,9},{9,1},{17,25},{25,17},{2,10},{10... | collective-permute-start | bytes 3538952 | tf_op jit(solution)/shard_map/ppermute | solution.py:846
  190.4 22.8 %collective-permute-start.16 = (bf16[768,128]{1,0:T(8,128)(2,1)}, bf16[768,128]{1,0:T(8,128)(2,1)S(1)}, u32[]{:S(2)}, u32[]{:S(2)}) collective-permute-start(bf16[768,128]{1,0:T(8,128)(2,1)} %parcel.1.refs_4_.refs_0_), channel_id=1, source_target_pairs={{0,24},{8,16},{16,8},{24,0},{1,25},{9,17},{17,9},{25,1},{2,26},{10... | collective-permute-start | bytes 589832 | tf_op jit(solution)/shard_map/ppermute | solution.py:846
  191.0 42.8 %collective-permute-start.17 = (bf16[144,3072]{1,0:T(8,128)(2,1)}, bf16[144,3072]{1,0:T(8,128)(2,1)}, u32[]{:S(2)}, u32[]{:S(2)}) collective-permute-start(bf16[144,3072]{1,0:T(8,128)(2,1)} %constant_dynamic-update-slice_fusion.refs_0_.refs_8_), channel_id=1, source_target_pairs={{0,8},{8,0},{16,24},{24,16},{1,9},{9,1},{17,25},{25,17},{2,10},{10... | collective-permute-start | bytes 2654216 | tf_op jit(solution)/shard_map/ppermute | solution.py:846
  191.0 26.5 %collective-permute-start.15 = (bf16[768,128]{1,0:T(8,128)(2,1)}, bf16[768,128]{1,0:T(8,128)(2,1)S(1)}, u32[]{:S(2)}, u32[]{:S(2)}) collective-permute-start(bf16[768,128]{1,0:T(8,128)(2,1)} %parcel.1.refs_4_.refs_0_), channel_id=1, source_target_pairs={{0,16},{8,24},{16,0},{24,8},{1,17},{9,25},{17,1},{25,9},{2,18},{10... | collective-permute-start | bytes 589832 | tf_op jit(solution)/shard_map/ppermute | solution.py:846
  219.0 25.8 %collective-permute-start.27 = (bf16[4,144,512]{2,1,0:T(8,128)(2,1)S(1)}, bf16[4,144,512]{2,1,0:T(8,128)(2,1)}, u32[]{:S(2)}, u32[]{:S(2)}) collective-permute-start(bf16[4,144,512]{2,1,0:T(8,128)(2,1)S(1)} %copy-done.12), channel_id=1, source_target_pairs={{0,16},{8,24},{16,0},{24,8},{1,17},{9,25},{17,1},{25,9},{2,18},{10... | collective-permute-start | bytes 1769480 | tf_op jit(solution)/shard_map/ppermute | solution.py:846
  222.5 34.6 %collective-permute-start.19 = (bf16[144,3072]{1,0:T(8,128)(2,1)}, bf16[144,3072]{1,0:T(8,128)(2,1)S(1)}, u32[]{:S(2)}, u32[]{:S(2)}) collective-permute-start(bf16[144,3072]{1,0:T(8,128)(2,1)} %collective-permute-done.18.refs_2_.refs_10_), channel_id=1, source_target_pairs={{0,8},{8,0},{16,24},{24,16},{1,9},{9,1},{17,25},{25,17},{2,10},{10... | collective-permute-start | bytes 2654216 | tf_op jit(solution)/shard_map/ppermute | solution.py:846
  225.3 45.5 %collective-permute-start.23 = (bf16[4,144,512]{2,1,0:T(8,128)(2,1)S(1)}, bf16[4,144,512]{2,1,0:T(8,128)(2,1)}, u32[]{:S(2)}, u32[]{:S(2)}) collective-permute-start(bf16[4,144,512]{2,1,0:T(8,128)(2,1)S(1)} %copy-done.6), channel_id=1, source_target_pairs={{0,8},{8,0},{16,24},{24,16},{1,9},{9,1},{17,25},{25,17},{2,10},{10... | collective-permute-start | bytes 1769480 | tf_op jit(solution)/shard_map/ppermute | solution.py:846
  233.8 37.6 %collective-permute-start.26 = (bf16[4,144,512]{2,1,0:T(8,128)(2,1)S(1)}, bf16[4,144,512]{2,1,0:T(8,128)(2,1)}, u32[]{:S(2)}, u32[]{:S(2)}) collective-permute-start(bf16[4,144,512]{2,1,0:T(8,128)(2,1)S(1)} %copy-done.12), channel_id=1, source_target_pairs={{0,8},{8,0},{16,24},{24,16},{1,9},{9,1},{17,25},{25,17},{2,10},{10... | collective-permute-start | bytes 1769480 | tf_op jit(solution)/shard_map/ppermute | solution.py:846
  233.8 37.6 %collective-permute-start.25 = (bf16[4,144,512]{2,1,0:T(8,128)(2,1)}, bf16[4,144,512]{2,1,0:T(8,128)(2,1)}, u32[]{:S(2)}, u32[]{:S(2)}) collective-permute-start(bf16[4,144,512]{2,1,0:T(8,128)(2,1)} %collective-permute-done.24.refs_2_), channel_id=1, source_target_pairs={{0,8},{8,0},{16,24},{24,16},{1,9},{9,1},{17,25},{25,17},{2,10},{10... | collective-permute-start | bytes 1769480 | tf_op jit(solution)/shard_map/ppermute | solution.py:846
  244.9 26.5 %collective-permute-start.28 = (bf16[4,144,512]{2,1,0:T(8,128)(2,1)}, bf16[4,144,512]{2,1,0:T(8,128)(2,1)}, u32[]{:S(2)}, u32[]{:S(2)}) collective-permute-start(bf16[4,144,512]{2,1,0:T(8,128)(2,1)} %collective-permute-done.27.refs_6_), channel_id=1, source_target_pairs={{0,8},{8,0},{16,24},{24,16},{1,9},{9,1},{17,25},{25,17},{2,10},{10... | collective-permute-start | bytes 1769480 | tf_op jit(solution)/shard_map/ppermute | solution.py:846
  (38 other events, 305.7 us)

commit v3 on v2

--- a/solution.py
+++ b/solution.py
@@ -954,8 +954,8 @@
         name="act_grad",
     )(send_order, out_grad, readout_out)
     theirs = permute(gact[half:], "mp", lambda i: i ^ 1)
+    gact = (gact[:half].astype(F32) + theirs.astype(F32)).astype(BF16)
     x_all = after(x_all, gact)
-    gact = (gact[:half].astype(F32) + theirs.astype(F32)).astype(BF16)
     gact = [gact[0]] + [permute(gact[k], "mp", lambda i: i + 2 * k) for k in range(1, half)]
 
     up1_all, up2_all = unpack_up(slot, dp_gather(x_all[:, up_at:]), se, channels)
@@ -978,7 +978,7 @@
         image_sizes, x_all, vec_all, smem=(0,), name="early_slope",
     )
     hids = dp_gather(hid)
-    b_all = after(b_all, slope1)
+    b_all = after(b_all, slope1, *gact[1:])
     hid2, pooled, pay, conv2, sq2, rpre1, e1, e1_all = call(
         late_kernel,
         (
@@ -1009,9 +1009,38 @@
         flops=4 * n2 * channels * cols, name="readout",
     )
     gtok = swap(pay)
-    cats = dp_gather(jnp.concatenate([tok, hid2, gpre, out_grad], axis=1))
-    act0 = jnp.stack([act] + [permute(act, "mp", lambda i: i + 2 * k) for k in range(1, half)])
+    cat = jnp.concatenate([tok, hid2, gpre, out_grad], axis=1)
+    cats = dp_gather(cat)
+    gtok = after(gtok, cat, *hids[1:3])
+    gconv2, grp2, gl2, pay = call(
+        late_back_kernel,
+        (
+            shape((n2, width), BF16), shape((1, se)), shape((1, width)),
+            shape((mp, n2 + tail2, width), BF16),
+        ),
+        mine, gtok, conv2, e2, rpre2, down_late, w_late, normed2, inv2, slope2, vec_all,
+        b_all, e1_all, up1_all,
+        smem=(0,), flops=2 * n2 * channels * 9 * width, name="late_back",
+    )
+    acts = [permute(act, "mp", lambda i: i + 2 * k) for k in range(1, half)]
+    act0 = jnp.stack([act] + [after(one, grp2) for one in acts])
     act1 = permute(act0, "mp", lambda i: i ^ 1)
+    part2 = after(swap(pay), *hids[3:], *cats[1:3])
+    gae, gconv1, grp1, gl1, gg2, pay = call(
+        early_back_kernel,
+        (
+            shape((n, width)), shape((n, width), BF16), shape((1, se)), shape((1, width)),
+            shape((2, width)), shape((mp, n + 16, width), BF16),
+        ),
+        image_sizes, part2, pool_b, e1, rpre1, down_early, pp, w_early, normed1, inv1, slope1, vec_all,
+        smem=(0,), flops=2 * n * channels * 9 * width, name="early_back",
+    )
+    part1 = swap(pay)
+    (parcel,) = call(
+        parcel_kernel, (shape((n + n2 + tail_rows(12 * (se // width) + 18), width), BF16),),
+        gconv1, gconv2, rpre1, rpre2, grp1, grp2, gl1, gl2, sq1, sq2, gg2, name="parcel",
+    )
+    parcels = dp_gather(parcel, relay=False)
     tokens_out = pl.pallas_call(
         logits_kernel,
         out_shape=shape((n2, out_cols), BF16),
@@ -1029,38 +1058,12 @@
         ),
         cost_estimate=cost(2 * n2 * out_cols * cols * mp, cols * mp * out_cols * 2),
         name="logits",
-    )(got_order, act0, act1, readout_out, row(readout_out_bias))
-
-    gconv2, grp2, gl2, pay = call(
-        late_back_kernel,
-        (
-            shape((n2, width), BF16), shape((1, se)), shape((1, width)),
-            shape((mp, n2 + tail2, width), BF16),
-        ),
-        mine, gtok, conv2, e2, rpre2, down_late, w_late, normed2, inv2, slope2, vec_all,
-        b_all, e1_all, up1_all,
-        smem=(0,), flops=2 * n2 * channels * 9 * width, name="late_back",
-    )
-    part2 = after(swap(pay), tokens_out)
-    gae, gconv1, grp1, gl1, gg2, pay = call(
-        early_back_kernel,
-        (
-            shape((n, width)), shape((n, width), BF16), shape((1, se)), shape((1, width)),
-            shape((2, width)), shape((mp, n + 16, width), BF16),
-        ),
-        image_sizes, part2, pool_b, e1, rpre1, down_early, pp, w_early, normed1, inv1, slope1, vec_all,
-        smem=(0,), flops=2 * n * channels * 9 * width, name="early_back",
-    )
-    part1 = swap(pay)
-    (parcel,) = call(
-        parcel_kernel, (shape((n + n2 + tail_rows(12 * (se // width) + 18), width), BF16),),
-        gconv1, gconv2, rpre1, rpre2, grp1, grp2, gl1, gl2, sq1, sq2, gg2, name="parcel",
-    )
-    parcels = dp_gather(parcel, relay=False)
+    )(got_order, act0, after(act1, parcels[1]), readout_out, row(readout_out_bias))
+
     grad_w2, grad_cb2, grad_in_w, grad_in_b = late_weights(slot, cats, parcels, channels, cols, 2)
     grad_w1, grad_cb1 = early_weights(slot, hids, parcels, 2)
     grad_down1, grad_up1, grad_down2, grad_up2, flat, lines = small_grads(slot, parcels, se)
-    part1 = after(part1, grad_w1, grad_w2, flat)
+    part1 = after(part1, grad_w1, grad_w2, flat, tokens_out)
     fgrad, low = call(
         final_kernel, (shape((n, width)), shape((n + 16, width), BF16)),
         image_sizes, part1, gae, smem=(0,), name="final",

time: 288 us -> 257 us (0.89)
  waiting for transfers between devices: 113 us -> 76.8 us
  starting transfers between devices: 53.9 us -> 58.4 us
    ppermute x29, waiting for transfers between devices: 71.5 us -> 47.4 us  [permute(): return lax.ppermute(v, axis, [(i, fn(i) % n) for i in range(n)])]
    all_to_all x6, waiting for transfers between devices: 41.6 us -> 29.4 us  [swap(): return lax.all_to_all(v, 'mp', 0, 0)]
    all_to_all x6, starting transfers between devices: 27.6 us -> 31.3 us  [swap(): return lax.all_to_all(v, 'mp', 0, 0)]
    unnamed x57 -> x65, local copies, waits for them, and re-layouts: 10.6 us -> 9.46 us
  transfers between devices with their start and end apart: 35 -> 35, of which waited for: 11 -> 9; matrix products, arithmetic and copies ran while one was open for 4% -> 5% of each run, Pallas kernels for 28% -> 33%
where the time goes in v3:
time: 257 us; the launch traced here: 255 us
  Pallas kernels  97 us (38%)
  waiting for transfers between devices  76.8 us (30%)
  starting transfers between devices  58.4 us (23%)
  local copies, waits for them, and re-layouts  18.4 us (7%)
  other arithmetic  3.16 us (1%)
    ppermute x29, waiting for transfers between devices, permute(): return lax.ppermute(v, axis, [(i, fn(i) % n) for i in range(n)])  47.4 us
    pallas_call x10, Pallas kernels, call(): pl.pallas_call(kernel, out_shape=list(outs), in_specs=specs, out_specs=[p...  43.2 us
    all_to_all x6, starting transfers between devices, swap(): return lax.all_to_all(v, 'mp', 0, 0)  31.3 us
    all_to_all x6, waiting for transfers between devices, swap(): return lax.all_to_all(v, 'mp', 0, 0)  29.4 us
    ppermute x29, starting transfers between devices, permute(): return lax.ppermute(v, axis, [(i, fn(i) % n) for i in range(n)])  27 us
    pallas_call x1, Pallas kernels, early_weights(): pl.pallas_call(partial(early_weight_kernel, images), out_shape=[shape((9,...  12.2 us
    pallas_call x1, Pallas kernels, act_weights(): pl.pallas_call(partial(act_weight_kernel, images, offset), out_shape=[sha...  10.2 us
    unnamed x65, local copies, waits for them, and re-layouts  9.46 us
  transfers between devices with their start and end apart: 35, of which 9 were waited for; matrix products, arithmetic and copies ran while one was open for 5% of the time, Pallas kernels for 33%

profile of v3, /device:TPU:0, one launch (start us, length us, event | category | flops | bytes accessed | tf_op | source)
XLA Modules:
  0.0 255.5 jit_solution(2759141388913473579)
XLA Ops:
  3.9 7.3 %all-to-all-start = ((bf16[8,736,128]{2,1,0:T(8,128)(2,1)}), bf16[8,736,128]{2,1,0:T(8,128)(2,1)S(1)}, u32[]{:S(2)}, u32[]{:S(2)}) async-start(bf16[8,736,128]{2,1,0:T(8,128)(2,1)} %prep.1), calls=%async_computation | async-start | bytes 3014656 | tf_op jit(solution)/shard_map/all_to_all | solution.py:841
  11.9 7.7 %act_grad.1 = bf16[8,144,512]{2,1,0:T(8,128)(2,1)} custom-call(s32[8]{0:T(128)} %add.141.order_ref, bf16[144,512]{1,0:T(8,128)(2,1)} %g_ref.1, bf16[4096,512]{1,0:T(8,128)(2,1)} %w_ref.5), custom_call_target="tpu_custom_call" | custom-call | flops 603979776 | bytes 4194304 | tf_op jit(solution)/shard_map/act_grad/pallas_call | solution.py:941
  26.7 16.7 %collective-permute-done = bf16[4,144,512]{2,1,0:T(8,128)(2,1)} collective-permute-done((bf16[4,144,512]{2,1,0:T(8,128)(2,1)S(1)}, bf16[4,144,512]{2,1,0:T(8,128)(2,1)}, u32[]{:S(2)}, u32[]{:S(2)}) %collective-permute-start) | collective-permute-done | bytes 589856 | tf_op jit(solution)/shard_map/ppermute | solution.py:846
  47.9 6.9 %front.1 = (f32[8,1024]{1,0:T(8,128)}, bf16[576,1024]{1,0:T(8,128)(2,1)}, f32[8,152,128]{2,1,0:T(8,128)}, f32[144,1024]{1,0:T(8,128)}, f32[144,128]{1,0:T(8,128)}, /*index=5*/f32[1,128]{1,0:T(1,128)}) custom-call(s32[1]{0:T(128)S(6)} %copy.50.size_ref, bf16[8,736,128]{2,1,0:T(8,128)(2,1)} %copy-done, bf16[9,1024,128]{2,1,0:T(8,128)(2,1)} %bitcast.61, ...), custom_call_target="tpu_custom_call" | custom-call | flops 1358954496 | bytes 6663172 | tf_op jit(solution)/shard_map/front/pallas_call | solution.py:44
  54.8 4.9 %all-to-all-start.1 = ((f32[8,152,128]{2,1,0:T(8,128)}), f32[8,152,128]{2,1,0:T(8,128)S(1)}, u32[]{:S(2)}, u32[]{:S(2)}) async-start(f32[8,152,128]{2,1,0:T(8,128)} %get-tuple-element.90), calls=%async_computation.1 | async-start | bytes 1245184 | tf_op jit(solution)/shard_map/all_to_all | solution.py:841
  62.3 6.4 %collective-permute-done.5.refs_2_ = bf16[8,128,128]{2,1,0:T(8,128)(2,1)S(1)} collective-permute-done((bf16[8,128,128]{2,1,0:T(8,128)(2,1)S(1)}, bf16[8,128,128]{2,1,0:T(8,128)(2,1)S(1)}, u32[]{:S(2)}, u32[]{:S(2)}) %collective-permute-start.5) | collective-permute-done | bytes 262176 | tf_op jit(solution)/shard_map/ppermute | solution.py:846
  76.1 5.7 %early_slope.1 = (f32[576,1024]{1,0:T(8,128)}, f32[576,128]{1,0:T(8,128)}, f32[576,1024]{1,0:T(8,128)}) custom-call(s32[1]{0:T(128)S(6)} %copy.50.size_ref, bf16[8,736,128]{2,1,0:T(8,128)(2,1)} %copy-done, f32[8,1024]{1,0:T(8,128)} %get-tuple-element.91.vec_ref), custom_call_target="tpu_custom_call" | custom-call | flops 1000000 | bytes 6553604 | tf_op jit(solution)/shard_map/early_slope/pallas_call | solution.py:44
  90.0 4.4 %late.1 = (bf16[144,1024]{1,0:T(8,128)(2,1)}, f32[144,1024]{1,0:T(8,128)}, f32[8,152,128]{2,1,0:T(8,128)}, f32[144,128]{1,0:T(8,128)}, f32[1,128]{1,0:T(1,128)},...) custom-call(f32[8,152,128]{2,1,0:T(8,128)} %copy-done.1, f32[144,1024]{1,0:T(8,128)} %get-tuple-element.94.a_ref, ...), custom_call_target="tpu_custom_call" | custom-call | flops 339738624 | bytes 5980160 | tf_op jit(solution)/shard_map/late/pallas_call | solution.py:44
  94.4 3.6 %all-to-all-start.2 = ((f32[8,152,128]{2,1,0:T(8,128)}), f32[8,152,128]{2,1,0:T(8,128)S(1)}, u32[]{:S(2)}, u32[]{:S(2)}) async-start(f32[8,152,128]{2,1,0:T(8,128)} %get-tuple-element.96), calls=%async_computation.2 | async-start | bytes 1245184 | tf_op jit(solution)/shard_map/all_to_all | solution.py:841
  101.9 12.1 %all-to-all-done.2.call_ref = f32[8,152,128]{2,1,0:T(8,128)S(1)} async-done(((f32[8,152,128]{2,1,0:T(8,128)}), f32[8,152,128]{2,1,0:T(8,128)S(1)}, u32[]{:S(2)}, u32[]{:S(2)}) %all-to-all-start.2) | async-done | bytes 622624 | tf_op jit(solution)/shard_map/all_to_all | solution.py:841
  114.9 4.4 %readout.1 = (bf16[144,1024]{1,0:T(8,128)(2,1)}, bf16[144,512]{1,0:T(8,128)(2,1)}, bf16[144,512]{1,0:T(8,128)(2,1)}, bf16[8,160,128]{2,1,0:T(8,128)(2,1)}, f32[1...) custom-call(f32[8,152,128]{2,1,0:T(8,128)} %copy-done.4, f32[144,1024]{1,0:T(8,128)} %get-tuple-element.97.pool_ref, ...), custom_call_target="tpu_custom_call" | custom-call | flops 301989888 | bytes 4465664 | tf_op jit(solution)/shard_map/readout/pallas_call | solution.py:44
  119.3 3.8 %all-to-all-start.3 = ((bf16[8,160,128]{2,1,0:T(8,128)(2,1)}), bf16[8,160,128]{2,1,0:T(8,128)(2,1)S(1)}, u32[]{:S(2)}, u32[]{:S(2)}) async-start(bf16[8,160,128]{2,1,0:T(8,128)(2,1)} %get-tuple-element.102), calls=%async_computation.3 | async-start | bytes 655360 | tf_op jit(solution)/shard_map/all_to_all | solution.py:841
  125.7 7.7 %all-to-all-done.3.gt_ref = bf16[8,160,128]{2,1,0:T(8,128)(2,1)S(1)} async-done(((bf16[8,160,128]{2,1,0:T(8,128)(2,1)}), bf16[8,160,128]{2,1,0:T(8,128)(2,1)S(1)}, u32[]{:S(2)}, u32[]{:S(2)}) %all-to-all-start.3) | async-done | bytes 327712 | tf_op jit(solution)/shard_map/all_to_all | solution.py:841
  134.1 5.4 %late_back.1 = (bf16[144,128]{1,0:T(8,128)(2,1)}, f32[1,256]{1,0:T(1,128)}, f32[1,128]{1,0:T(1,128)}, bf16[8,160,128]{2,1,0:T(8,128)(2,1)}) custom-call(s32[1]{0:T(128)} %bitcast.23.me_ref, bf16[8,160,128]{2,1,0:T(8,128)(2,1)} %copy-done.7, f32[144,128]{1,0:T(8,128)} %get-tuple-element.108.conv_ref, f32[1,128]{1,0:T(1,128)} %get-tuple-element.109.e_ref, ...), custom_call_target="tpu_custom_call" | custom-call | flops 339738624 | bytes 5696516 | tf_op jit(solution)/shard_map/late_back/pallas_call | solution.py:44
  139.5 3.6 %all-to-all-start.4 = ((bf16[8,160,128]{2,1,0:T(8,128)(2,1)}), bf16[8,160,128]{2,1,0:T(8,128)(2,1)S(1)}, u32[]{:S(2)}, u32[]{:S(2)}) async-start(bf16[8,160,128]{2,1,0:T(8,128)(2,1)} %get-tuple-element.118), calls=%async_computation.4 | async-start | bytes 655360 | tf_op jit(solution)/shard_map/all_to_all | solution.py:841
  143.2 3.8 %collective-permute-start.11 = (bf16[144,512]{1,0:T(8,128)(2,1)S(1)}, bf16[144,512]{1,0:T(8,128)(2,1)S(1)}, u32[]{:S(2)}, u32[]{:S(2)}) collective-permute-start(bf16[144,512]{1,0:T(8,128)(2,1)S(1)} %copy-done.21), channel_id=1, source_target_pairs={{0,6},{1,7},{2,0},{3,1},{4,2},{5,3},{6,4},{7,5},{8,14},{9,15},{10,... | collective-permute-start | bytes 442376 | tf_op jit(solution)/shard_map/ppermute | solution.py:846
  148.2 7.4 %all-to-all-done.4.p2_ref = bf16[8,160,128]{2,1,0:T(8,128)(2,1)S(1)} async-done(((bf16[8,160,128]{2,1,0:T(8,128)(2,1)}), bf16[8,160,128]{2,1,0:T(8,128)(2,1)S(1)}, u32[]{:S(2)}, u32[]{:S(2)}) %all-to-all-start.4) | async-done | bytes 327712 | tf_op jit(solution)/shard_map/all_to_all | solution.py:841
  156.3 7.2 %early_back.1 = (f32[576,128]{1,0:T(8,128)}, bf16[576,128]{1,0:T(8,128)(2,1)}, f32[1,256]{1,0:T(1,128)}, f32[1,128]{1,0:T(1,128)}, f32[2,128]{1,0:T(2,128)}, /*index=5*/bf16[8,592,128]{2,1,0:T(8,128)(2,1)}) custom-call(s32[1]{0:T(128)S(6)} %copy.50.size_ref, bf16[8,160,128]{2,1,0:T(8,128)(2,1)} %copy-done.6, f32[144,128]{1,0:T(8,128)} %get-tuple-element.120.b_ref, ...), custom_call_target="tpu_custom_call" | custom-call | flops 1358954496 | bytes 9762820 | tf_op jit(solution)/shard_map/early_back/pallas_call | solution.py:44
  163.5 8.2 %all-to-all-start.5 = ((bf16[8,592,128]{2,1,0:T(8,128)(2,1)}), bf16[8,592,128]{2,1,0:T(8,128)(2,1)S(1)}, u32[]{:S(2)}, u32[]{:S(2)}) async-start(bf16[8,592,128]{2,1,0:T(8,128)(2,1)} %get-tuple-element.134), calls=%async_computation.5 | async-start | bytes 2424832 | tf_op jit(solution)/shard_map/all_to_all | solution.py:841
  179.3 19.4 %collective-permute-done.12.a1_ref.refs_4_ = bf16[4,144,512]{2,1,0:T(8,128)(2,1)S(1)} collective-permute-done((bf16[4,144,512]{2,1,0:T(8,128)(2,1)S(1)}, bf16[4,144,512]{2,1,0:T(8,128)(2,1)S(1)}, u32[]{:S(2)}, u32[]{:S(2)}) %collective-permute-start.12) | collective-permute-done | bytes 589856 | tf_op jit(solution)/shard_map/ppermute | solution.py:846
  204.9 7.5 %logits.1 = bf16[144,512]{1,0:T(8,128)(2,1)} custom-call(s32[8]{0:T(128)} %add.136.blocks_ref, bf16[4,144,512]{2,1,0:T(8,128)(2,1)} %copy-done.5, bf16[4,144,512]{2,1,0:T(8,128)(2,1)} %copy-done.10, bf16[4096,512]{1,0:T(8,128)(2,1)} %w_ref.5, f32[1,512]{1,0:T(1,128)} %bitcast.70), custom_call_target="tpu_custom_call" | custom-call | flops 603979776 | bytes 4194304 | tf_op jit(solution)/shard_map/logits/pallas_call | solution.py:1044
  213.9 12.2 %early_weights.1 = (f32[9,1024,128]{2,1,0:T(8,128)}, f32[1,128]{1,0:T(1,128)}) custom-call(s32[4]{0:T(128)} %fusion.6.slot_ref, bf16[576,1024]{1,0:T(8,128)(2,1)} %get-tuple-element.106.refs_0_, bf16[576,1024]{1,0:T(8,128)(2,1)} %collective-permute-done.8.refs_1_, bf16[576,1024]{1,0:T(8,128)(2,1)} %collective-permute-done.9.refs_2_, ...), custom_call_target="tpu_custom_call" | custom-call | flops 5435817984 | bytes 9437184 | tf_op jit(solution)/shard_map/early_weights/pallas_call | solution.py:682
  226.1 7.8 %late_weights.1 = (f32[9,1024,128]{2,1,0:T(8,128)}, f32[1,128]{1,0:T(1,128)}, f32[1024,512]{1,0:T(8,128)}, f32[1,512]{1,0:T(1,128)}) custom-call(s32[4]{0:T(128)} %fusion.6.slot_ref, bf16[144,3072]{1,0:T(8,128)(2,1)} %copy-done.26, bf16[144,3072]{1,0:T(8,128)(2,1)} %collective-permute-done.14.refs_1_.refs_9_, bf16[144,3072]{1,0:T(8,128)(2,1)} %copy-done.29, ...), custom_call_target="tpu_custom_call" | custom-call | flops 1962934272 | bytes 12000000 | tf_op jit(solution)/shard_map/late_weights/pallas_call | solution.py:751
  240.0 10.2 %act_weights.1 = (f32[4096,512]{1,0:T(8,128)}, f32[1,512]{1,0:T(1,128)}) custom-call(s32[4]{0:T(128)} %fusion.6.slot_ref, s32[8]{0:T(128)} %add.136.blocks_ref, bf16[4,144,512]{2,1,0:T(8,128)(2,1)} %copy-done.5, bf16[4,144,512]{2,1,0:T(8,128)(2,1)} %collective-permute-done.23.refs_1_, bf16[4,144,512]{2,1,0:T(8,128)(2,1)} %collective-permute-done.24.refs_2_, ...), custom_call_target="tpu_custom_call" | custom-call | flops 2415919104 | bytes 13107200 | tf_op jit(solution)/shard_map/act_weights/pallas_call | solution.py:816
  (150 shorter events, 69.7 us)
Async XLA Ops:
  3.9 42.9 %all-to-all-start = ((bf16[8,736,128]{2,1,0:T(8,128)(2,1)}), bf16[8,736,128]{2,1,0:T(8,128)(2,1)S(1)}, u32[]{:S(2)}, u32[]{:S(2)}) async-start(bf16[8,736,128]{2,1,0:T(8,128)(2,1)} %prep.1), calls=%async_computation | async-start | bytes 3014656 | tf_op jit(solution)/shard_map/all_to_all | solution.py:841
  20.8 22.5 %collective-permute-start = (bf16[4,144,512]{2,1,0:T(8,128)(2,1)S(1)}, bf16[4,144,512]{2,1,0:T(8,128)(2,1)}, u32[]{:S(2)}, u32[]{:S(2)}) collective-permute-start(bf16[4,144,512]{2,1,0:T(8,128)(2,1)S(1)} %slice.61), channel_id=1, source_target_pairs={{0,1},{1,0},{2,3},{3,2},{4,5},{5,4},{6,7},{7,6},{8,9},{9,8},{10,11... | collective-permute-start | bytes 1769480 | tf_op jit(solution)/shard_map/ppermute | solution.py:846
  54.8 34.3 %all-to-all-start.1 = ((f32[8,152,128]{2,1,0:T(8,128)}), f32[8,152,128]{2,1,0:T(8,128)S(1)}, u32[]{:S(2)}, u32[]{:S(2)}) async-start(f32[8,152,128]{2,1,0:T(8,128)} %get-tuple-element.90), calls=%async_computation.1 | async-start | bytes 1245184 | tf_op jit(solution)/shard_map/all_to_all | solution.py:841
  73.0 16.1 %collective-permute-start.1 = (bf16[144,512]{1,0:T(8,128)(2,1)S(1)}, bf16[144,512]{1,0:T(8,128)(2,1)S(1)}, u32[]{:S(2)}, u32[]{:S(2)}) collective-permute-start(bf16[144,512]{1,0:T(8,128)(2,1)S(1)} %get-tuple-element.158), channel_id=1, source_target_pairs={{0,2},{1,3},{2,4},{3,5},{4,6},{5,7},{6,0},{7,1},{8,10},{9,11},{10,... | collective-permute-start | bytes 442376 | tf_op jit(solution)/shard_map/ppermute | solution.py:846
  74.1 27.8 %collective-permute-start.9 = (bf16[576,1024]{1,0:T(8,128)(2,1)}, bf16[576,1024]{1,0:T(8,128)(2,1)}, u32[]{:S(2)}, u32[]{:S(2)}) collective-permute-start(bf16[576,1024]{1,0:T(8,128)(2,1)} %get-tuple-element.106.refs_0_), channel_id=1, source_target_pairs={{0,16},{8,24},{16,0},{24,8},{1,17},{9,25},{17,1},{25,9},{2,18},{10... | collective-permute-start | bytes 3538952 | tf_op jit(solution)/shard_map/ppermute | solution.py:846
  94.4 19.7 %all-to-all-start.2 = ((f32[8,152,128]{2,1,0:T(8,128)}), f32[8,152,128]{2,1,0:T(8,128)S(1)}, u32[]{:S(2)}, u32[]{:S(2)}) async-start(f32[8,152,128]{2,1,0:T(8,128)} %get-tuple-element.96), calls=%async_computation.2 | async-start | bytes 1245184 | tf_op jit(solution)/shard_map/all_to_all | solution.py:841
  97.9 27.8 %collective-permute-start.8 = (bf16[576,1024]{1,0:T(8,128)(2,1)}, bf16[576,1024]{1,0:T(8,128)(2,1)}, u32[]{:S(2)}, u32[]{:S(2)}) collective-permute-start(bf16[576,1024]{1,0:T(8,128)(2,1)} %get-tuple-element.106.refs_0_), channel_id=1, source_target_pairs={{0,8},{8,0},{16,24},{24,16},{1,9},{9,1},{17,25},{25,17},{2,10},{10... | collective-permute-start | bytes 3538952 | tf_op jit(solution)/shard_map/ppermute | solution.py:846
  101.9 45.1 %collective-permute-start.13 = (bf16[576,1024]{1,0:T(8,128)(2,1)}, bf16[576,1024]{1,0:T(8,128)(2,1)}, u32[]{:S(2)}, u32[]{:S(2)}) collective-permute-start(bf16[576,1024]{1,0:T(8,128)(2,1)} %collective-permute-done.9.refs_2_), channel_id=1, source_target_pairs={{0,8},{8,0},{16,24},{24,16},{1,9},{9,1},{17,25},{25,17},{2,10},{10... | collective-permute-start | bytes 3538952 | tf_op jit(solution)/shard_map/ppermute | solution.py:846
  124.1 24.0 %collective-permute-start.15 = (bf16[144,3072]{1,0:T(8,128)(2,1)S(1)}, bf16[144,3072]{1,0:T(8,128)(2,1)S(1)}, u32[]{:S(2)}, u32[]{:S(2)}) collective-permute-start(bf16[144,3072]{1,0:T(8,128)(2,1)S(1)} %constant_dynamic-update-slice_fusion.refs_0_.refs_8_), channel_id=1, source_target_pairs={{0,16},{8,24},{16,0},{24,8},{1,17},{9,25},{17,1},{25,9},{2,18},{10... | collective-permute-start | bytes 2654216 | tf_op jit(solution)/shard_map/ppermute | solution.py:846
  125.7 22.4 %collective-permute-start.14 = (bf16[144,3072]{1,0:T(8,128)(2,1)S(1)}, bf16[144,3072]{1,0:T(8,128)(2,1)}, u32[]{:S(2)}, u32[]{:S(2)}) collective-permute-start(bf16[144,3072]{1,0:T(8,128)(2,1)S(1)} %constant_dynamic-update-slice_fusion.refs_0_.refs_8_), channel_id=1, source_target_pairs={{0,8},{8,0},{16,24},{24,16},{1,9},{9,1},{17,25},{25,17},{2,10},{10... | collective-permute-start | bytes 2654216 | tf_op jit(solution)/shard_map/ppermute | solution.py:846
  143.2 28.5 %collective-permute-start.11 = (bf16[144,512]{1,0:T(8,128)(2,1)S(1)}, bf16[144,512]{1,0:T(8,128)(2,1)S(1)}, u32[]{:S(2)}, u32[]{:S(2)}) collective-permute-start(bf16[144,512]{1,0:T(8,128)(2,1)S(1)} %copy-done.21), channel_id=1, source_target_pairs={{0,6},{1,7},{2,0},{3,1},{4,2},{5,3},{6,4},{7,5},{8,14},{9,15},{10,... | collective-permute-start | bytes 442376 | tf_op jit(solution)/shard_map/ppermute | solution.py:846
  147.0 24.7 %collective-permute-start.10 = (bf16[144,512]{1,0:T(8,128)(2,1)S(1)}, bf16[144,512]{1,0:T(8,128)(2,1)S(1)}, u32[]{:S(2)}, u32[]{:S(2)}) collective-permute-start(bf16[144,512]{1,0:T(8,128)(2,1)S(1)} %copy-done.21), channel_id=1, source_target_pairs={{0,4},{1,5},{2,6},{3,7},{4,0},{5,1},{6,2},{7,3},{8,12},{9,13},{10,... | collective-permute-start | bytes 442376 | tf_op jit(solution)/shard_map/ppermute | solution.py:846
  147.0 24.7 %collective-permute-start.7 = (bf16[144,512]{1,0:T(8,128)(2,1)S(1)}, bf16[144,512]{1,0:T(8,128)(2,1)S(1)}, u32[]{:S(2)}, u32[]{:S(2)}) collective-permute-start(bf16[144,512]{1,0:T(8,128)(2,1)S(1)} %copy-done.21), channel_id=1, source_target_pairs={{0,2},{1,3},{2,4},{3,5},{4,6},{5,7},{6,0},{7,1},{8,10},{9,11},{10,... | collective-permute-start | bytes 442376 | tf_op jit(solution)/shard_map/ppermute | solution.py:846
  163.5 70.4 %all-to-all-start.5 = ((bf16[8,592,128]{2,1,0:T(8,128)(2,1)}), bf16[8,592,128]{2,1,0:T(8,128)(2,1)S(1)}, u32[]{:S(2)}, u32[]{:S(2)}) async-start(bf16[8,592,128]{2,1,0:T(8,128)(2,1)} %get-tuple-element.134), calls=%async_computation.5 | async-start | bytes 2424832 | tf_op jit(solution)/shard_map/all_to_all | solution.py:841
  171.8 26.9 %collective-permute-start.12 = (bf16[4,144,512]{2,1,0:T(8,128)(2,1)S(1)}, bf16[4,144,512]{2,1,0:T(8,128)(2,1)S(1)}, u32[]{:S(2)}, u32[]{:S(2)}) collective-permute-start(bf16[4,144,512]{2,1,0:T(8,128)(2,1)S(1)} %pad_maximum_fusion.a0_ref.refs_0_), channel_id=1, source_target_pairs={{0,1},{1,0},{2,3},{3,2},{4,5},{5,4},{6,7},{7,6},{8,9},{9,8},{10,11... | collective-permute-start | bytes 1769480 | tf_op jit(solution)/shard_map/ppermute | solution.py:846
  173.9 26.9 %collective-permute-start.24 = (bf16[4,144,512]{2,1,0:T(8,128)(2,1)S(1)}, bf16[4,144,512]{2,1,0:T(8,128)(2,1)}, u32[]{:S(2)}, u32[]{:S(2)}) collective-permute-start(bf16[4,144,512]{2,1,0:T(8,128)(2,1)S(1)} %pad_maximum_fusion.a0_ref.refs_0_), channel_id=1, source_target_pairs={{0,16},{8,24},{16,0},{24,8},{1,17},{9,25},{17,1},{25,9},{2,18},{10... | collective-permute-start | bytes 1769480 | tf_op jit(solution)/shard_map/ppermute | solution.py:846
  177.2 23.6 %collective-permute-start.16 = (bf16[768,128]{1,0:T(8,128)(2,1)}, bf16[768,128]{1,0:T(8,128)(2,1)S(1)}, u32[]{:S(2)}, u32[]{:S(2)}) collective-permute-start(bf16[768,128]{1,0:T(8,128)(2,1)} %parcel.1.refs_4_.refs_0_), channel_id=1, source_target_pairs={{0,8},{8,0},{16,24},{24,16},{1,9},{9,1},{17,25},{25,17},{2,10},{10... | collective-permute-start | bytes 589832 | tf_op jit(solution)/shard_map/ppermute | solution.py:846
  177.2 24.1 %collective-permute-start.18 = (bf16[768,128]{1,0:T(8,128)(2,1)}, bf16[768,128]{1,0:T(8,128)(2,1)S(1)}, u32[]{:S(2)}, u32[]{:S(2)}) collective-permute-start(bf16[768,128]{1,0:T(8,128)(2,1)} %parcel.1.refs_4_.refs_0_), channel_id=1, source_target_pairs={{0,24},{8,16},{16,8},{24,0},{1,25},{9,17},{17,9},{25,1},{2,26},{10... | collective-permute-start | bytes 589832 | tf_op jit(solution)/shard_map/ppermute | solution.py:846
  177.8 23.6 %collective-permute-start.17 = (bf16[768,128]{1,0:T(8,128)(2,1)}, bf16[768,128]{1,0:T(8,128)(2,1)S(1)}, u32[]{:S(2)}, u32[]{:S(2)}) collective-permute-start(bf16[768,128]{1,0:T(8,128)(2,1)} %parcel.1.refs_4_.refs_0_), channel_id=1, source_target_pairs={{0,16},{8,24},{16,0},{24,8},{1,17},{9,25},{17,1},{25,9},{2,18},{10... | collective-permute-start | bytes 589832 | tf_op jit(solution)/shard_map/ppermute | solution.py:846
  200.8 36.7 %collective-permute-start.23 = (bf16[4,144,512]{2,1,0:T(8,128)(2,1)S(1)}, bf16[4,144,512]{2,1,0:T(8,128)(2,1)}, u32[]{:S(2)}, u32[]{:S(2)}) collective-permute-start(bf16[4,144,512]{2,1,0:T(8,128)(2,1)S(1)} %pad_maximum_fusion.a0_ref.refs_0_), channel_id=1, source_target_pairs={{0,8},{8,0},{16,24},{24,16},{1,9},{9,1},{17,25},{25,17},{2,10},{10... | collective-permute-start | bytes 1769480 | tf_op jit(solution)/shard_map/ppermute | solution.py:846
  200.8 25.3 %collective-permute-start.19 = (bf16[144,3072]{1,0:T(8,128)(2,1)}, bf16[144,3072]{1,0:T(8,128)(2,1)}, u32[]{:S(2)}, u32[]{:S(2)}) collective-permute-start(bf16[144,3072]{1,0:T(8,128)(2,1)} %copy-done.29), channel_id=1, source_target_pairs={{0,8},{8,0},{16,24},{24,16},{1,9},{9,1},{17,25},{25,17},{2,10},{10... | collective-permute-start | bytes 2654216 | tf_op jit(solution)/shard_map/ppermute | solution.py:846
  201.3 37.8 %collective-permute-start.26 = (bf16[4,144,512]{2,1,0:T(8,128)(2,1)S(1)}, bf16[4,144,512]{2,1,0:T(8,128)(2,1)}, u32[]{:S(2)}, u32[]{:S(2)}) collective-permute-start(bf16[4,144,512]{2,1,0:T(8,128)(2,1)S(1)} %collective-permute-done.12.a1_ref.refs_4_), channel_id=1, source_target_pairs={{0,8},{8,0},{16,24},{24,16},{1,9},{9,1},{17,25},{25,17},{2,10},{10... | collective-permute-start | bytes 1769480 | tf_op jit(solution)/shard_map/ppermute | solution.py:846
  201.4 37.6 %collective-permute-start.25 = (bf16[4,144,512]{2,1,0:T(8,128)(2,1)}, bf16[4,144,512]{2,1,0:T(8,128)(2,1)}, u32[]{:S(2)}, u32[]{:S(2)}) collective-permute-start(bf16[4,144,512]{2,1,0:T(8,128)(2,1)} %collective-permute-done.24.refs_2_), channel_id=1, source_target_pairs={{0,8},{8,0},{16,24},{24,16},{1,9},{9,1},{17,25},{25,17},{2,10},{10... | collective-permute-start | bytes 1769480 | tf_op jit(solution)/shard_map/ppermute | solution.py:846
  213.5 25.7 %collective-permute-start.28 = (bf16[4,144,512]{2,1,0:T(8,128)(2,1)}, bf16[4,144,512]{2,1,0:T(8,128)(2,1)S(1)}, u32[]{:S(2)}, u32[]{:S(2)}) collective-permute-start(bf16[4,144,512]{2,1,0:T(8,128)(2,1)} %collective-permute-done.27.refs_6_), channel_id=1, source_target_pairs={{0,8},{8,0},{16,24},{24,16},{1,9},{9,1},{17,25},{25,17},{2,10},{10... | collective-permute-start | bytes 1769480 | tf_op jit(solution)/shard_map/ppermute | solution.py:846
  (42 other events, 439.7 us)

commit v4 on v3

--- a/solution.py
+++ b/solution.py
@@ -1035,12 +1035,15 @@
         image_sizes, part2, pool_b, e1, rpre1, down_early, pp, w_early, normed1, inv1, slope1, vec_all,
         smem=(0,), flops=2 * n * channels * 9 * width, name="early_back",
     )
-    part1 = swap(pay)
+    part1 = swap(after(pay, *acts))
     (parcel,) = call(
         parcel_kernel, (shape((n + n2 + tail_rows(12 * (se // width) + 18), width), BF16),),
         gconv1, gconv2, rpre1, rpre2, grp1, grp2, gl1, gl2, sq1, sq2, gg2, name="parcel",
     )
     parcels = dp_gather(parcel, relay=False)
+    grad_w2, grad_cb2, grad_in_w, grad_in_b = late_weights(slot, cats, parcels, channels, cols, 2)
+    grad_w1, grad_cb1 = early_weights(slot, hids, parcels, 2)
+    act1 = after(act1, grad_cb1)
     tokens_out = pl.pallas_call(
         logits_kernel,
         out_shape=shape((n2, out_cols), BF16),
@@ -1058,10 +1061,8 @@
         ),
         cost_estimate=cost(2 * n2 * out_cols * cols * mp, cols * mp * out_cols * 2),
         name="logits",
-    )(got_order, act0, after(act1, parcels[1]), readout_out, row(readout_out_bias))
-
-    grad_w2, grad_cb2, grad_in_w, grad_in_b = late_weights(slot, cats, parcels, channels, cols, 2)
-    grad_w1, grad_cb1 = early_weights(slot, hids, parcels, 2)
+    )(got_order, act0, act1, readout_out, row(readout_out_bias))
+
     grad_down1, grad_up1, grad_down2, grad_up2, flat, lines = small_grads(slot, parcels, se)
     part1 = after(part1, grad_w1, grad_w2, flat, tokens_out)
     fgrad, low = call(

time: 257 us -> 245 us (0.953)
  waiting for transfers between devices: 76.8 us -> 68 us
  starting transfers between devices: 58.4 us -> 55.4 us
    ppermute x29, waiting for transfers between devices: 47.4 us -> 38.6 us  [permute(): return lax.ppermute(v, axis, [(i, fn(i) % n) for i in range(n)])]
  transfers between devices with their start and end apart: 35 -> 35, of which waited for: 9 -> 13; matrix products, arithmetic and copies ran while one was open for 5% -> 5% of each run, Pallas kernels for 33% -> 35%
where the time goes in v4:
time: 245 us; the launch traced here: 244 us
  Pallas kernels  97 us (40%)
  waiting for transfers between devices  68 us (28%)
  starting transfers between devices  55.4 us (23%)
  local copies, waits for them, and re-layouts  18.7 us (8%)
  other arithmetic  3.16 us (1%)
    pallas_call x10, Pallas kernels, call(): pl.pallas_call(kernel, out_shape=list(outs), in_specs=specs, out_specs=[p...  43.2 us
    ppermute x29, waiting for transfers between devices, permute(): return lax.ppermute(v, axis, [(i, fn(i) % n) for i in range(n)])  38.6 us
    all_to_all x6, waiting for transfers between devices, swap(): return lax.all_to_all(v, 'mp', 0, 0)  29.4 us
    all_to_all x6, starting transfers between devices, swap(): return lax.all_to_all(v, 'mp', 0, 0)  28.8 us
    ppermute x29, starting transfers between devices, permute(): return lax.ppermute(v, axis, [(i, fn(i) % n) for i in range(n)])  26.6 us
    pallas_call x1, Pallas kernels, early_weights(): pl.pallas_call(partial(early_weight_kernel, images), out_shape=[shape((9,...  12.2 us
    pallas_call x1, Pallas kernels, act_weights(): pl.pallas_call(partial(act_weight_kernel, images, offset), out_shape=[sha...  10.2 us
    unnamed x65, local copies, waits for them, and re-layouts  9.72 us
  transfers between devices with their start and end apart: 35, of which 13 were waited for; matrix products, arithmetic and copies ran while one was open for 5% of the time, Pallas kernels for 35%

profile of v4, /device:TPU:0, one launch (start us, length us, event | category | flops | bytes accessed | tf_op | source)
XLA Modules:
  0.0 244.0 jit_solution(16999919232043290414)
XLA Ops:
  3.9 7.3 %all-to-all-start = ((bf16[8,736,128]{2,1,0:T(8,128)(2,1)}), bf16[8,736,128]{2,1,0:T(8,128)(2,1)S(1)}, u32[]{:S(2)}, u32[]{:S(2)}) async-start(bf16[8,736,128]{2,1,0:T(8,128)(2,1)} %prep.1), calls=%async_computation | async-start | bytes 3014656 | tf_op jit(solution)/shard_map/all_to_all | solution.py:841
  11.9 7.7 %act_grad.1 = bf16[8,144,512]{2,1,0:T(8,128)(2,1)} custom-call(s32[8]{0:T(128)} %add.141.order_ref, bf16[144,512]{1,0:T(8,128)(2,1)} %g_ref.1, bf16[4096,512]{1,0:T(8,128)(2,1)} %w_ref.5), custom_call_target="tpu_custom_call" | custom-call | flops 603979776 | bytes 4194304 | tf_op jit(solution)/shard_map/act_grad/pallas_call | solution.py:941
  26.7 16.7 %collective-permute-done = bf16[4,144,512]{2,1,0:T(8,128)(2,1)} collective-permute-done((bf16[4,144,512]{2,1,0:T(8,128)(2,1)S(1)}, bf16[4,144,512]{2,1,0:T(8,128)(2,1)}, u32[]{:S(2)}, u32[]{:S(2)}) %collective-permute-start) | collective-permute-done | bytes 589856 | tf_op jit(solution)/shard_map/ppermute | solution.py:846
  47.9 6.9 %front.1 = (f32[8,1024]{1,0:T(8,128)}, bf16[576,1024]{1,0:T(8,128)(2,1)}, f32[8,152,128]{2,1,0:T(8,128)}, f32[144,1024]{1,0:T(8,128)}, f32[144,128]{1,0:T(8,128)}, /*index=5*/f32[1,128]{1,0:T(1,128)}) custom-call(s32[1]{0:T(128)S(6)} %copy.50.size_ref, bf16[8,736,128]{2,1,0:T(8,128)(2,1)} %copy-done, bf16[9,1024,128]{2,1,0:T(8,128)(2,1)} %bitcast.61, ...), custom_call_target="tpu_custom_call" | custom-call | flops 1358954496 | bytes 6663172 | tf_op jit(solution)/shard_map/front/pallas_call | solution.py:44
  54.8 4.9 %all-to-all-start.1 = ((f32[8,152,128]{2,1,0:T(8,128)}), f32[8,152,128]{2,1,0:T(8,128)S(1)}, u32[]{:S(2)}, u32[]{:S(2)}) async-start(f32[8,152,128]{2,1,0:T(8,128)} %get-tuple-element.91), calls=%async_computation.1 | async-start | bytes 1245184 | tf_op jit(solution)/shard_map/all_to_all | solution.py:841
  62.3 6.4 %collective-permute-done.5.refs_2_ = bf16[8,128,128]{2,1,0:T(8,128)(2,1)S(1)} collective-permute-done((bf16[8,128,128]{2,1,0:T(8,128)(2,1)S(1)}, bf16[8,128,128]{2,1,0:T(8,128)(2,1)S(1)}, u32[]{:S(2)}, u32[]{:S(2)}) %collective-permute-start.5) | collective-permute-done | bytes 262176 | tf_op jit(solution)/shard_map/ppermute | solution.py:846
  76.1 5.7 %early_slope.1 = (f32[576,1024]{1,0:T(8,128)}, f32[576,128]{1,0:T(8,128)}, f32[576,1024]{1,0:T(8,128)}) custom-call(s32[1]{0:T(128)S(6)} %copy.50.size_ref, bf16[8,736,128]{2,1,0:T(8,128)(2,1)} %copy-done, f32[8,1024]{1,0:T(8,128)} %get-tuple-element.92.vec_ref), custom_call_target="tpu_custom_call" | custom-call | flops 1000000 | bytes 6553604 | tf_op jit(solution)/shard_map/early_slope/pallas_call | solution.py:44
  90.0 4.4 %late.1 = (bf16[144,1024]{1,0:T(8,128)(2,1)}, f32[144,1024]{1,0:T(8,128)}, f32[8,152,128]{2,1,0:T(8,128)}, f32[144,128]{1,0:T(8,128)}, f32[1,128]{1,0:T(1,128)},...) custom-call(f32[8,152,128]{2,1,0:T(8,128)} %copy-done.1, f32[144,1024]{1,0:T(8,128)} %get-tuple-element.95.a_ref, ...), custom_call_target="tpu_custom_call" | custom-call | flops 339738624 | bytes 5980160 | tf_op jit(solution)/shard_map/late/pallas_call | solution.py:44
  94.3 3.6 %all-to-all-start.2 = ((f32[8,152,128]{2,1,0:T(8,128)}), f32[8,152,128]{2,1,0:T(8,128)S(1)}, u32[]{:S(2)}, u32[]{:S(2)}) async-start(f32[8,152,128]{2,1,0:T(8,128)} %get-tuple-element.97), calls=%async_computation.2 | async-start | bytes 1245184 | tf_op jit(solution)/shard_map/all_to_all | solution.py:841
  101.9 12.1 %all-to-all-done.2.call_ref = f32[8,152,128]{2,1,0:T(8,128)S(1)} async-done(((f32[8,152,128]{2,1,0:T(8,128)}), f32[8,152,128]{2,1,0:T(8,128)S(1)}, u32[]{:S(2)}, u32[]{:S(2)}) %all-to-all-start.2) | async-done | bytes 622624 | tf_op jit(solution)/shard_map/all_to_all | solution.py:841
  114.9 4.4 %readout.1 = (bf16[144,1024]{1,0:T(8,128)(2,1)}, bf16[144,512]{1,0:T(8,128)(2,1)}, bf16[144,512]{1,0:T(8,128)(2,1)}, bf16[8,160,128]{2,1,0:T(8,128)(2,1)}, f32[1...) custom-call(f32[8,152,128]{2,1,0:T(8,128)} %copy-done.4, f32[144,1024]{1,0:T(8,128)} %get-tuple-element.98.pool_ref, ...), custom_call_target="tpu_custom_call" | custom-call | flops 301989888 | bytes 4465664 | tf_op jit(solution)/shard_map/readout/pallas_call | solution.py:44
  119.3 3.8 %all-to-all-start.3 = ((bf16[8,160,128]{2,1,0:T(8,128)(2,1)}), bf16[8,160,128]{2,1,0:T(8,128)(2,1)S(1)}, u32[]{:S(2)}, u32[]{:S(2)}) async-start(bf16[8,160,128]{2,1,0:T(8,128)(2,1)} %get-tuple-element.103), calls=%async_computation.3 | async-start | bytes 655360 | tf_op jit(solution)/shard_map/all_to_all | solution.py:841
  125.7 7.7 %all-to-all-done.3.gt_ref = bf16[8,160,128]{2,1,0:T(8,128)(2,1)S(1)} async-done(((bf16[8,160,128]{2,1,0:T(8,128)(2,1)}), bf16[8,160,128]{2,1,0:T(8,128)(2,1)S(1)}, u32[]{:S(2)}, u32[]{:S(2)}) %all-to-all-start.3) | async-done | bytes 327712 | tf_op jit(solution)/shard_map/all_to_all | solution.py:841
  134.2 5.4 %late_back.1 = (bf16[144,128]{1,0:T(8,128)(2,1)}, f32[1,256]{1,0:T(1,128)}, f32[1,128]{1,0:T(1,128)}, bf16[8,160,128]{2,1,0:T(8,128)(2,1)}) custom-call(s32[1]{0:T(128)} %bitcast.23.me_ref, bf16[8,160,128]{2,1,0:T(8,128)(2,1)} %copy-done.7, f32[144,128]{1,0:T(8,128)} %get-tuple-element.109.conv_ref, f32[1,128]{1,0:T(1,128)} %get-tuple-element.110.e_ref, ...), custom_call_target="tpu_custom_call" | custom-call | flops 339738624 | bytes 5696516 | tf_op jit(solution)/shard_map/late_back/pallas_call | solution.py:44
  139.6 3.6 %all-to-all-start.4 = ((bf16[8,160,128]{2,1,0:T(8,128)(2,1)}), bf16[8,160,128]{2,1,0:T(8,128)(2,1)S(1)}, u32[]{:S(2)}, u32[]{:S(2)}) async-start(bf16[8,160,128]{2,1,0:T(8,128)(2,1)} %get-tuple-element.119), calls=%async_computation.4 | async-start | bytes 655360 | tf_op jit(solution)/shard_map/all_to_all | solution.py:841
  143.2 3.8 %collective-permute-start.11 = (bf16[144,512]{1,0:T(8,128)(2,1)S(1)}, bf16[144,512]{1,0:T(8,128)(2,1)S(1)}, u32[]{:S(2)}, u32[]{:S(2)}) collective-permute-start(bf16[144,512]{1,0:T(8,128)(2,1)S(1)} %copy-done.21), channel_id=1, source_target_pairs={{0,6},{1,7},{2,0},{3,1},{4,2},{5,3},{6,4},{7,5},{8,14},{9,15},{10,... | collective-permute-start | bytes 442376 | tf_op jit(solution)/shard_map/ppermute | solution.py:846
  148.2 7.4 %all-to-all-done.4.p2_ref = bf16[8,160,128]{2,1,0:T(8,128)(2,1)S(1)} async-done(((bf16[8,160,128]{2,1,0:T(8,128)(2,1)}), bf16[8,160,128]{2,1,0:T(8,128)(2,1)S(1)}, u32[]{:S(2)}, u32[]{:S(2)}) %all-to-all-start.4) | async-done | bytes 327712 | tf_op jit(solution)/shard_map/all_to_all | solution.py:841
  156.3 7.2 %early_back.1 = (f32[576,128]{1,0:T(8,128)}, bf16[576,128]{1,0:T(8,128)(2,1)}, f32[1,256]{1,0:T(1,128)}, f32[1,128]{1,0:T(1,128)}, f32[2,128]{1,0:T(2,128)}, /*index=5*/bf16[8,592,128]{2,1,0:T(8,128)(2,1)}) custom-call(s32[1]{0:T(128)S(6)} %copy.50.size_ref, bf16[8,160,128]{2,1,0:T(8,128)(2,1)} %copy-done.6, f32[144,128]{1,0:T(8,128)} %get-tuple-element.121.b_ref, ...), custom_call_target="tpu_custom_call" | custom-call | flops 1358954496 | bytes 9762820 | tf_op jit(solution)/shard_map/early_back/pallas_call | solution.py:44
  166.0 5.7 %all-to-all-start.5 = ((bf16[8,592,128]{2,1,0:T(8,128)(2,1)}), bf16[8,592,128]{2,1,0:T(8,128)(2,1)S(1)}, u32[]{:S(2)}, u32[]{:S(2)}) async-start(bf16[8,592,128]{2,1,0:T(8,128)(2,1)} %get-tuple-element.137), calls=%async_computation.5 | async-start | bytes 2424832 | tf_op jit(solution)/shard_map/all_to_all | solution.py:841
  180.9 4.3 %collective-permute-done.17.refs_6_.refs_2_ = bf16[768,128]{1,0:T(8,128)(2,1)S(1)} collective-permute-done((bf16[768,128]{1,0:T(8,128)(2,1)}, bf16[768,128]{1,0:T(8,128)(2,1)S(1)}, u32[]{:S(2)}, u32[]{:S(2)}) %collective-permute-start.17) | collective-permute-done | bytes 196640 | tf_op jit(solution)/shard_map/ppermute | solution.py:846
  186.6 12.2 %early_weights.1 = (f32[9,1024,128]{2,1,0:T(8,128)}, f32[1,128]{1,0:T(1,128)}) custom-call(s32[4]{0:T(128)} %fusion.6.slot_ref, bf16[576,1024]{1,0:T(8,128)(2,1)} %get-tuple-element.107.refs_0_, bf16[576,1024]{1,0:T(8,128)(2,1)} %collective-permute-done.8.refs_1_, bf16[576,1024]{1,0:T(8,128)(2,1)} %collective-permute-done.9.refs_2_, ...), custom_call_target="tpu_custom_call" | custom-call | flops 5435817984 | bytes 9437184 | tf_op jit(solution)/shard_map/early_weights/pallas_call | solution.py:682
  205.0 7.5 %logits.1 = bf16[144,512]{1,0:T(8,128)(2,1)} custom-call(s32[8]{0:T(128)} %add.136.blocks_ref, bf16[4,144,512]{2,1,0:T(8,128)(2,1)} %copy-done.5, bf16[4,144,512]{2,1,0:T(8,128)(2,1)} %copy-done.10, bf16[4096,512]{1,0:T(8,128)(2,1)} %w_ref.5, f32[1,512]{1,0:T(1,128)} %bitcast.70), custom_call_target="tpu_custom_call" | custom-call | flops 603979776 | bytes 4194304 | tf_op jit(solution)/shard_map/logits/pallas_call | solution.py:1047
  215.3 7.8 %late_weights.1 = (f32[9,1024,128]{2,1,0:T(8,128)}, f32[1,128]{1,0:T(1,128)}, f32[1024,512]{1,0:T(8,128)}, f32[1,512]{1,0:T(1,128)}) custom-call(s32[4]{0:T(128)} %fusion.6.slot_ref, bf16[144,3072]{1,0:T(8,128)(2,1)} %copy-done.26, bf16[144,3072]{1,0:T(8,128)(2,1)} %collective-permute-done.14.refs_1_.refs_9_, bf16[144,3072]{1,0:T(8,128)(2,1)} %copy-done.29, ...), custom_call_target="tpu_custom_call" | custom-call | flops 1962934272 | bytes 12000000 | tf_op jit(solution)/shard_map/late_weights/pallas_call | solution.py:751
  228.5 10.2 %act_weights.1 = (f32[4096,512]{1,0:T(8,128)}, f32[1,512]{1,0:T(1,128)}) custom-call(s32[4]{0:T(128)} %fusion.6.slot_ref, s32[8]{0:T(128)} %add.136.blocks_ref, bf16[4,144,512]{2,1,0:T(8,128)(2,1)} %copy-done.5, bf16[4,144,512]{2,1,0:T(8,128)(2,1)} %collective-permute-done.23.refs_1_, bf16[4,144,512]{2,1,0:T(8,128)(2,1)} %collective-permute-done.24.refs_2_, ...), custom_call_target="tpu_custom_call" | custom-call | flops 2415919104 | bytes 13107200 | tf_op jit(solution)/shard_map/act_weights/pallas_call | solution.py:816
  (150 shorter events, 75.7 us)
Async XLA Ops:
  3.9 42.9 %all-to-all-start = ((bf16[8,736,128]{2,1,0:T(8,128)(2,1)}), bf16[8,736,128]{2,1,0:T(8,128)(2,1)S(1)}, u32[]{:S(2)}, u32[]{:S(2)}) async-start(bf16[8,736,128]{2,1,0:T(8,128)(2,1)} %prep.1), calls=%async_computation | async-start | bytes 3014656 | tf_op jit(solution)/shard_map/all_to_all | solution.py:841
  20.8 22.5 %collective-permute-start = (bf16[4,144,512]{2,1,0:T(8,128)(2,1)S(1)}, bf16[4,144,512]{2,1,0:T(8,128)(2,1)}, u32[]{:S(2)}, u32[]{:S(2)}) collective-permute-start(bf16[4,144,512]{2,1,0:T(8,128)(2,1)S(1)} %slice.61), channel_id=1, source_target_pairs={{0,1},{1,0},{2,3},{3,2},{4,5},{5,4},{6,7},{7,6},{8,9},{9,8},{10,11... | collective-permute-start | bytes 1769480 | tf_op jit(solution)/shard_map/ppermute | solution.py:846
  54.8 34.3 %all-to-all-start.1 = ((f32[8,152,128]{2,1,0:T(8,128)}), f32[8,152,128]{2,1,0:T(8,128)S(1)}, u32[]{:S(2)}, u32[]{:S(2)}) async-start(f32[8,152,128]{2,1,0:T(8,128)} %get-tuple-element.91), calls=%async_computation.1 | async-start | bytes 1245184 | tf_op jit(solution)/shard_map/all_to_all | solution.py:841
  69.4 16.1 %collective-permute-start.3 = (bf16[144,512]{1,0:T(8,128)(2,1)S(1)}, bf16[144,512]{1,0:T(8,128)(2,1)S(1)}, u32[]{:S(2)}, u32[]{:S(2)}) collective-permute-start(bf16[144,512]{1,0:T(8,128)(2,1)S(1)} %get-tuple-element.158), channel_id=1, source_target_pairs={{0,6},{1,7},{2,0},{3,1},{4,2},{5,3},{6,4},{7,5},{8,14},{9,15},{10,... | collective-permute-start | bytes 442376 | tf_op jit(solution)/shard_map/ppermute | solution.py:846
  73.0 16.1 %collective-permute-start.2 = (bf16[144,512]{1,0:T(8,128)(2,1)S(1)}, bf16[144,512]{1,0:T(8,128)(2,1)S(1)}, u32[]{:S(2)}, u32[]{:S(2)}) collective-permute-start(bf16[144,512]{1,0:T(8,128)(2,1)S(1)} %get-tuple-element.159), channel_id=1, source_target_pairs={{0,4},{1,5},{2,6},{3,7},{4,0},{5,1},{6,2},{7,3},{8,12},{9,13},{10,... | collective-permute-start | bytes 442376 | tf_op jit(solution)/shard_map/ppermute | solution.py:846
  73.0 16.1 %collective-permute-start.1 = (bf16[144,512]{1,0:T(8,128)(2,1)S(1)}, bf16[144,512]{1,0:T(8,128)(2,1)S(1)}, u32[]{:S(2)}, u32[]{:S(2)}) collective-permute-start(bf16[144,512]{1,0:T(8,128)(2,1)S(1)} %get-tuple-element.160), channel_id=1, source_target_pairs={{0,2},{1,3},{2,4},{3,5},{4,6},{5,7},{6,0},{7,1},{8,10},{9,11},{10,... | collective-permute-start | bytes 442376 | tf_op jit(solution)/shard_map/ppermute | solution.py:846
  74.1 27.8 %collective-permute-start.9 = (bf16[576,1024]{1,0:T(8,128)(2,1)}, bf16[576,1024]{1,0:T(8,128)(2,1)}, u32[]{:S(2)}, u32[]{:S(2)}) collective-permute-start(bf16[576,1024]{1,0:T(8,128)(2,1)} %get-tuple-element.107.refs_0_), channel_id=1, source_target_pairs={{0,16},{8,24},{16,0},{24,8},{1,17},{9,25},{17,1},{25,9},{2,18},{10... | collective-permute-start | bytes 3538952 | tf_op jit(solution)/shard_map/ppermute | solution.py:846
  94.3 19.7 %all-to-all-start.2 = ((f32[8,152,128]{2,1,0:T(8,128)}), f32[8,152,128]{2,1,0:T(8,128)S(1)}, u32[]{:S(2)}, u32[]{:S(2)}) async-start(f32[8,152,128]{2,1,0:T(8,128)} %get-tuple-element.97), calls=%async_computation.2 | async-start | bytes 1245184 | tf_op jit(solution)/shard_map/all_to_all | solution.py:841
  97.9 27.8 %collective-permute-start.8 = (bf16[576,1024]{1,0:T(8,128)(2,1)}, bf16[576,1024]{1,0:T(8,128)(2,1)}, u32[]{:S(2)}, u32[]{:S(2)}) collective-permute-start(bf16[576,1024]{1,0:T(8,128)(2,1)} %get-tuple-element.107.refs_0_), channel_id=1, source_target_pairs={{0,8},{8,0},{16,24},{24,16},{1,9},{9,1},{17,25},{25,17},{2,10},{10... | collective-permute-start | bytes 3538952 | tf_op jit(solution)/shard_map/ppermute | solution.py:846
  101.9 45.1 %collective-permute-start.13 = (bf16[576,1024]{1,0:T(8,128)(2,1)}, bf16[576,1024]{1,0:T(8,128)(2,1)}, u32[]{:S(2)}, u32[]{:S(2)}) collective-permute-start(bf16[576,1024]{1,0:T(8,128)(2,1)} %collective-permute-done.9.refs_2_), channel_id=1, source_target_pairs={{0,8},{8,0},{16,24},{24,16},{1,9},{9,1},{17,25},{25,17},{2,10},{10... | collective-permute-start | bytes 3538952 | tf_op jit(solution)/shard_map/ppermute | solution.py:846
  124.1 24.0 %collective-permute-start.15 = (bf16[144,3072]{1,0:T(8,128)(2,1)S(1)}, bf16[144,3072]{1,0:T(8,128)(2,1)S(1)}, u32[]{:S(2)}, u32[]{:S(2)}) collective-permute-start(bf16[144,3072]{1,0:T(8,128)(2,1)S(1)} %constant_dynamic-update-slice_fusion.refs_0_.refs_8_), channel_id=1, source_target_pairs={{0,16},{8,24},{16,0},{24,8},{1,17},{9,25},{17,1},{25,9},{2,18},{10... | collective-permute-start | bytes 2654216 | tf_op jit(solution)/shard_map/ppermute | solution.py:846
  125.7 22.5 %collective-permute-start.14 = (bf16[144,3072]{1,0:T(8,128)(2,1)S(1)}, bf16[144,3072]{1,0:T(8,128)(2,1)}, u32[]{:S(2)}, u32[]{:S(2)}) collective-permute-start(bf16[144,3072]{1,0:T(8,128)(2,1)S(1)} %constant_dynamic-update-slice_fusion.refs_0_.refs_8_), channel_id=1, source_target_pairs={{0,8},{8,0},{16,24},{24,16},{1,9},{9,1},{17,25},{25,17},{2,10},{10... | collective-permute-start | bytes 2654216 | tf_op jit(solution)/shard_map/ppermute | solution.py:846
  139.6 16.0 %all-to-all-start.4 = ((bf16[8,160,128]{2,1,0:T(8,128)(2,1)}), bf16[8,160,128]{2,1,0:T(8,128)(2,1)S(1)}, u32[]{:S(2)}, u32[]{:S(2)}) async-start(bf16[8,160,128]{2,1,0:T(8,128)(2,1)} %get-tuple-element.119), calls=%async_computation.4 | async-start | bytes 655360 | tf_op jit(solution)/shard_map/all_to_all | solution.py:841
  143.2 20.3 %collective-permute-start.11 = (bf16[144,512]{1,0:T(8,128)(2,1)S(1)}, bf16[144,512]{1,0:T(8,128)(2,1)S(1)}, u32[]{:S(2)}, u32[]{:S(2)}) collective-permute-start(bf16[144,512]{1,0:T(8,128)(2,1)S(1)} %copy-done.21), channel_id=1, source_target_pairs={{0,6},{1,7},{2,0},{3,1},{4,2},{5,3},{6,4},{7,5},{8,14},{9,15},{10,... | collective-permute-start | bytes 442376 | tf_op jit(solution)/shard_map/ppermute | solution.py:846
  147.0 19.0 %collective-permute-start.10 = (bf16[144,512]{1,0:T(8,128)(2,1)S(1)}, bf16[144,512]{1,0:T(8,128)(2,1)S(1)}, u32[]{:S(2)}, u32[]{:S(2)}) collective-permute-start(bf16[144,512]{1,0:T(8,128)(2,1)S(1)} %copy-done.21), channel_id=1, source_target_pairs={{0,4},{1,5},{2,6},{3,7},{4,0},{5,1},{6,2},{7,3},{8,12},{9,13},{10,... | collective-permute-start | bytes 442376 | tf_op jit(solution)/shard_map/ppermute | solution.py:846
  147.0 19.0 %collective-permute-start.7 = (bf16[144,512]{1,0:T(8,128)(2,1)S(1)}, bf16[144,512]{1,0:T(8,128)(2,1)S(1)}, u32[]{:S(2)}, u32[]{:S(2)}) collective-permute-start(bf16[144,512]{1,0:T(8,128)(2,1)S(1)} %copy-done.21), channel_id=1, source_target_pairs={{0,2},{1,3},{2,4},{3,5},{4,6},{5,7},{6,0},{7,1},{8,10},{9,11},{10,... | collective-permute-start | bytes 442376 | tf_op jit(solution)/shard_map/ppermute | solution.py:846
  166.0 57.0 %all-to-all-start.5 = ((bf16[8,592,128]{2,1,0:T(8,128)(2,1)}), bf16[8,592,128]{2,1,0:T(8,128)(2,1)S(1)}, u32[]{:S(2)}, u32[]{:S(2)}) async-start(bf16[8,592,128]{2,1,0:T(8,128)(2,1)} %get-tuple-element.137), calls=%async_computation.5 | async-start | bytes 2424832 | tf_op jit(solution)/shard_map/all_to_all | solution.py:841
  175.5 23.6 %collective-permute-start.12 = (bf16[4,144,512]{2,1,0:T(8,128)(2,1)S(1)}, bf16[4,144,512]{2,1,0:T(8,128)(2,1)S(1)}, u32[]{:S(2)}, u32[]{:S(2)}) collective-permute-start(bf16[4,144,512]{2,1,0:T(8,128)(2,1)S(1)} %pad_maximum_fusion.a0_ref.refs_0_), channel_id=1, source_target_pairs={{0,1},{1,0},{2,3},{3,2},{4,5},{5,4},{6,7},{7,6},{8,9},{9,8},{10,11... | collective-permute-start | bytes 1769480 | tf_op jit(solution)/shard_map/ppermute | solution.py:846
  177.6 24.1 %collective-permute-start.24 = (bf16[4,144,512]{2,1,0:T(8,128)(2,1)S(1)}, bf16[4,144,512]{2,1,0:T(8,128)(2,1)}, u32[]{:S(2)}, u32[]{:S(2)}) collective-permute-start(bf16[4,144,512]{2,1,0:T(8,128)(2,1)S(1)} %pad_maximum_fusion.a0_ref.refs_0_), channel_id=1, source_target_pairs={{0,16},{8,24},{16,0},{24,8},{1,17},{9,25},{17,1},{25,9},{2,18},{10... | collective-permute-start | bytes 1769480 | tf_op jit(solution)/shard_map/ppermute | solution.py:846
  199.1 15.0 %collective-permute-start.27 = (bf16[4,144,512]{2,1,0:T(8,128)(2,1)S(1)}, bf16[4,144,512]{2,1,0:T(8,128)(2,1)S(1)}, u32[]{:S(2)}, u32[]{:S(2)}) collective-permute-start(bf16[4,144,512]{2,1,0:T(8,128)(2,1)S(1)} %collective-permute-done.12.a1_ref.refs_4_), channel_id=1, source_target_pairs={{0,16},{8,24},{16,0},{24,8},{1,17},{9,25},{17,1},{25,9},{2,18},{10... | collective-permute-start | bytes 1769480 | tf_op jit(solution)/shard_map/ppermute | solution.py:846
  200.6 14.7 %collective-permute-start.19 = (bf16[144,3072]{1,0:T(8,128)(2,1)}, bf16[144,3072]{1,0:T(8,128)(2,1)}, u32[]{:S(2)}, u32[]{:S(2)}) collective-permute-start(bf16[144,3072]{1,0:T(8,128)(2,1)} %copy-done.29), channel_id=1, source_target_pairs={{0,8},{8,0},{16,24},{24,16},{1,9},{9,1},{17,25},{25,17},{2,10},{10... | collective-permute-start | bytes 2654216 | tf_op jit(solution)/shard_map/ppermute | solution.py:846
  201.2 27.0 %collective-permute-start.23 = (bf16[4,144,512]{2,1,0:T(8,128)(2,1)S(1)}, bf16[4,144,512]{2,1,0:T(8,128)(2,1)}, u32[]{:S(2)}, u32[]{:S(2)}) collective-permute-start(bf16[4,144,512]{2,1,0:T(8,128)(2,1)S(1)} %pad_maximum_fusion.a0_ref.refs_0_), channel_id=1, source_target_pairs={{0,8},{8,0},{16,24},{24,16},{1,9},{9,1},{17,25},{25,17},{2,10},{10... | collective-permute-start | bytes 1769480 | tf_op jit(solution)/shard_map/ppermute | solution.py:846
  201.7 26.8 %collective-permute-start.25 = (bf16[4,144,512]{2,1,0:T(8,128)(2,1)}, bf16[4,144,512]{2,1,0:T(8,128)(2,1)}, u32[]{:S(2)}, u32[]{:S(2)}) collective-permute-start(bf16[4,144,512]{2,1,0:T(8,128)(2,1)} %collective-permute-done.24.refs_2_), channel_id=1, source_target_pairs={{0,8},{8,0},{16,24},{24,16},{1,9},{9,1},{17,25},{25,17},{2,10},{10... | collective-permute-start | bytes 1769480 | tf_op jit(solution)/shard_map/ppermute | solution.py:846
  201.8 26.8 %collective-permute-start.26 = (bf16[4,144,512]{2,1,0:T(8,128)(2,1)S(1)}, bf16[4,144,512]{2,1,0:T(8,128)(2,1)}, u32[]{:S(2)}, u32[]{:S(2)}) collective-permute-start(bf16[4,144,512]{2,1,0:T(8,128)(2,1)S(1)} %collective-permute-done.12.a1_ref.refs_4_), channel_id=1, source_target_pairs={{0,8},{8,0},{16,24},{24,16},{1,9},{9,1},{17,25},{25,17},{2,10},{10... | collective-permute-start | bytes 1769480 | tf_op jit(solution)/shard_map/ppermute | solution.py:846
  (42 other events, 426.3 us)
